TPU v7x, 32 devices: a whole 2x2x4 slice. The times are simulated.
32 devices in a mesh: groups: 2 (over y), particle: 8 (over z, x), tensor: 2 (over core).
Axes of the slice: x: 2, y: 2, z: 4, core: 2. Of those that a mesh axis runs over, the one named last changes fastest.
Arguments:
- prefix_cache: bfloat16 [2, 2048, 1024], P(None, 'groups', 'tensor'), parts along dimension 1, may hold values from -5 to 5
- tail_cache: bfloat16 [2, 128, 128, 1024], P(None, ('groups', 'particle'), None, 'tensor'), parts along dimension 1, may hold values from -5 to 5
- ancestors: int32 [128], P('groups'), parts along dimension 0, may hold values from 0 to 63, as said below
- queries: bfloat16 [4, 128, 8192], P(None, ('groups', 'particle'), 'tensor'), parts along dimension 1, may hold values from -8 to 8
- fresh_kv: bfloat16 [2, 4, 128, 1024], P(None, None, ('groups', 'particle'), 'tensor'), parts along dimension 2, may hold values from -5 to 5
- prompt_ids: int32 [2048], P('groups'), parts along dimension 0, may hold values from 0 to 128255
- sampled_ids: int32 [4, 128], P(None, ('groups', 'particle')), parts along dimension 1, may hold values from 0 to 128255
- twist_table: float32 [128256], replicated, may hold values from -5 to 5
- readout: float32 [8192], P('tensor'), may hold values from -0.3 to 0.3
Outputs:
- attended: bfloat16 [4, 128, 8192], P(None, ('groups', 'particle'), 'tensor'), parts along dimension 1
- twists: float32 [4, 128], P(None, ('groups', 'particle')), parts along dimension 1
There are 2 independent parts, one for each index of `groups`. A program takes and returns all parts, laid end to end along the dimension named above; an argument that names none is the same for every part. Nothing has to cross between parts.
Inputs may be any that keep to these rules, and one draw needn't show every extreme that they name: Particle i's ancestor lies on a device at most 2 indices from its own: |ancestors[i] // 8 - i // 8| <= 2, with equality for some particle.
All inputs are finite; a program needn't handle non-finite values.
Results may differ from a plain program's by a relative error of at most 0.0027.
Values may be sent and summed in bfloat16 or wider, within the bound.
No kernel may reach another device: no remote copies, remote signals or barrier semaphores. Data moves between devices by JAX's collectives and lax.ppermute only.
A program may use at most 64 MiB of HBM per device.

v0:
```python
from functools import reduce
import math

import jax
import jax.numpy as jnp
from jax import lax
from jax.sharding import PartitionSpec as P

HEADS = 64
KV_HEADS = 8
HEAD = 128
REACH = 2


NEG_FILL = -1e30


def shifted(value, axis, by):
    length = lax.axis_size(axis)
    pairs = [(i, i + by) for i in range(length) if 0 <= i + by < length]
    return lax.ppermute(value, axis, pairs)


def finish_block(scores, values, pattern):
    block_max = jnp.max(scores, axis=-1)
    expo_terms = jnp.exp(scores - block_max[..., None])
    block_sum = jnp.sum(expo_terms, axis=-1)
    weights = expo_terms.astype(jnp.bfloat16)
    block_out = jnp.einsum(pattern, weights, values, preferred_element_type=jnp.float32)
    return (block_out, block_max, block_sum)


def combine_blocks(blocks):
    overall = reduce(jnp.maximum, [member[1] for member in blocks])
    numerator = sum((jnp.exp(member[1] - overall)[..., None] * member[0] for member in blocks))
    denominator = sum((jnp.exp(member[1] - overall) * member[2] for member in blocks))
    return numerator / denominator[..., None]


def tail_block(query_heads, tails, score_scale):
    tail_heads = tails.reshape(
        2, tails.shape[1], tails.shape[2], query_heads.shape[2], query_heads.shape[4]
    )
    scores = (
        jnp.einsum(
            "tpkgh,pnkh->tpkgn", query_heads, tail_heads[0], preferred_element_type=jnp.float32
        )
        * score_scale
    )
    return finish_block(scores, tail_heads[1], "tpkgn,pnkh->tpkgh")


def on_device(
    prefix_cache,
    tail_cache,
    ancestors,
    queries,
    fresh_kv,
    prompt_ids,
    sampled_ids,
    twist_table,
    readout,
):
    step_count = queries.shape[0]
    per_device = queries.shape[1]
    local_groups = prefix_cache.shape[2] // HEAD
    group_size = HEADS // KV_HEADS
    score_scale = 1.0 / math.sqrt(HEAD)
    own_index = lax.axis_index("particle")
    my_parents = lax.dynamic_slice_in_dim(ancestors, own_index * per_device, per_device)
    parent_device = my_parents // per_device
    own_slot = my_parents % per_device
    query_heads = queries.reshape(step_count, per_device, local_groups, group_size, HEAD)
    prefix_heads = prefix_cache.reshape(2, prefix_cache.shape[1], local_groups, HEAD)
    prefix_scores = (
        jnp.einsum(
            "tpkgh,nkh->tpkgn", query_heads, prefix_heads[0], preferred_element_type=jnp.float32
        )
        * score_scale
    )
    prefix_part = finish_block(prefix_scores, prefix_heads[1], "tpkgn,nkh->tpkgh")
    fresh_heads = fresh_kv.reshape(2, step_count, per_device, local_groups, HEAD)
    fresh_scores = (
        jnp.einsum(
            "tpkgh,spkh->tpkgs", query_heads, fresh_heads[0], preferred_element_type=jnp.float32
        )
        * score_scale
    )
    step_index = jnp.arange(step_count)
    later_mask = step_index[None, :] > step_index[:, None]
    fresh_scores = jnp.where(later_mask[:, None, None, None, :], NEG_FILL, fresh_scores)
    fresh_part = finish_block(fresh_scores, fresh_heads[1], "tpkgs,spkh->tpkgh")

    def pick_from(source, offset, current):
        chosen = jnp.take(source, own_slot, axis=1)
        is_parent = (parent_device == own_index + offset)[None, :, None, None]
        return jnp.where(is_parent, chosen, current)

    inherited = pick_from(tail_cache, 0, jnp.zeros_like(tail_cache))
    for offset in list(range(-REACH, 0)) + list(range(1, REACH + 1)):
        arrived = shifted(tail_cache, "particle", -offset)
        inherited = pick_from(arrived, offset, inherited)
    inherit_part = tail_block(query_heads, inherited, score_scale)
    context = combine_blocks([prefix_part, inherit_part, fresh_part])
    context = context.reshape(step_count, per_device, local_groups * group_size * HEAD)
    attended = context.astype(jnp.bfloat16)
    partial_value = jnp.einsum("tpc,c->tp", context, readout, precision=lax.Precision.HIGHEST)
    twist_attn = lax.psum(partial_value, "tensor")
    repeats = jnp.sum(
        (sampled_ids[:, :, None] == prompt_ids[None, None, :]).astype(jnp.int32), axis=-1
    )
    twists = jnp.take(twist_table, sampled_ids) - 2.0 * repeats.astype(jnp.float32) + twist_attn
    return (attended, twists)


def solution(mesh):
    return jax.shard_map(
        on_device,
        mesh=mesh,
        in_specs=(
            P(None, "groups", "tensor"),
            P(None, ("groups", "particle"), None, "tensor"),
            P("groups"),
            P(None, ("groups", "particle"), "tensor"),
            P(None, None, ("groups", "particle"), "tensor"),
            P("groups"),
            P(None, ("groups", "particle")),
            P(),
            P("tensor"),
        ),
        out_specs=(P(None, ("groups", "particle"), "tensor"), P(None, ("groups", "particle"))),
        check_vma=False,
    )
```

profile of v0, /device:TPU:9, one launch (start us, length us, event | category | flops | bytes accessed | tf_op | source)
XLA Modules:
  0.0 129.3 jit_solution(8170295366046834399)
XLA Ops:
  0.6 2.1 %collective-permute-start = (bf16[2,8,128,512]{3,2,1,0:T(8,128)(2,1)}, bf16[2,8,128,512]{3,2,1,0:T(8,128)(2,1)}, u32[]{:S(2)}, u32[]{:S(2)}) collective-permute-start(bf16[2,8,128,512]{3,2,1,0:T(8,128)(2,1)} %param.12), channel_id=1, source_target_pairs={{4,0},{6,2},{8,4},{10,6},{12,8},{14,10},{5,1},{7,3},{9,5},{11,7},{... | collective-permute-start | bytes 6291464 | tf_op jit(solution)/shard_map/ppermute | solution.py:21
  2.7 2.4 %collective-permute-start.1 = (bf16[2,8,128,512]{3,2,1,0:T(8,128)(2,1)}, bf16[2,8,128,512]{3,2,1,0:T(8,128)(2,1)}, u32[]{:S(2)}, u32[]{:S(2)}) collective-permute-start(bf16[2,8,128,512]{3,2,1,0:T(8,128)(2,1)} %param.12), channel_id=1, source_target_pairs={{2,0},{4,2},{6,4},{8,6},{10,8},{12,10},{14,12},{3,1},{5,3},{7,5},{... | collective-permute-start | bytes 6291464 | tf_op jit(solution)/shard_map/ppermute | solution.py:21
  5.1 2.9 %collective-permute-start.2 = (bf16[2,8,128,512]{3,2,1,0:T(8,128)(2,1)}, bf16[2,8,128,512]{3,2,1,0:T(8,128)(2,1)}, u32[]{:S(2)}, u32[]{:S(2)}) collective-permute-start(bf16[2,8,128,512]{3,2,1,0:T(8,128)(2,1)} %param.12), channel_id=1, source_target_pairs={{0,2},{2,4},{4,6},{6,8},{8,10},{10,12},{12,14},{1,3},{3,5},{5,7},{... | collective-permute-start | bytes 6291464 | tf_op jit(solution)/shard_map/ppermute | solution.py:21
  8.0 3.4 %collective-permute-start.3 = (bf16[2,8,128,512]{3,2,1,0:T(8,128)(2,1)}, bf16[2,8,128,512]{3,2,1,0:T(8,128)(2,1)}, u32[]{:S(2)}, u32[]{:S(2)}) collective-permute-start(bf16[2,8,128,512]{3,2,1,0:T(8,128)(2,1)} %param.12), channel_id=1, source_target_pairs={{0,4},{2,6},{4,8},{6,10},{8,12},{10,14},{1,5},{3,7},{5,9},{7,11},{... | collective-permute-start | bytes 6291464 | tf_op jit(solution)/shard_map/ppermute | solution.py:21
  12.2 2.3 %gather_fusion.5 = bf16[8,2,128,512]{3,2,1,0:T(8,128)(2,1)S(1)} fusion(bf16[2,8,128,512]{3,2,1,0:T(8,128)(2,1)} %param.12, s32[1024]{0:T(1024)S(1)} %pad_clamp_fusion.1), kind=kCustom, calls=%fused_computation.4.clone | custom fusion | bytes 4194336 | tf_op jit(solution)/shard_map/jit(_take)/gather | solution.py:95
  14.4 3.1 %fusion.42 = (bf16[1,1024,512]{2,1,0:T(8,128)(2,1)}, bf16[1,1024,512]{2,1,0:T(8,128)(2,1)}) fusion(bf16[2,1024,512]{2,1,0:T(8,128)(2,1)} %param.11), kind=kLoop, calls=%fused_computation.78 | loop fusion | bytes 4194304 | tf_op jit(solution)/shard_map/slice | solution.py:81
  17.5 2.3 %copy.136 = bf16[1,1024,512]{1,2,0:T(8,128)(2,1)} copy(bf16[1,1024,512]{2,1,0:T(8,128)(2,1)} %get-tuple-element.15) | data formatting | bytes 2097152
  19.8 2.3 %copy.137 = bf16[1,1024,512]{1,2,0:T(8,128)(2,1)} copy(bf16[1,1024,512]{2,1,0:T(8,128)(2,1)} %get-tuple-element.14) | data formatting | bytes 2097152
  23.3 1.3 fusion.43
  25.4 2.0 %bitcast_reduce_fusion = (f32[4,8,4,8]{3,1,0,2:T(8,128)S(1)}, f32[4,1024,4,8,8]{1,4,3,2,0:T(8,128)S(1)}) fusion(bf16[1024,4,128,1,1]{0,2,4,3,1:T(8,128)(2,1)} %bitcast.94, bf16[4,8,4,8,128]{4,1,3,2,0:T(8,128)(2,1)S(1)} %bitcast.101), kind=kOutput, calls=%fused_computation.7 | convolution fusion | flops 270531584 | bytes 5509120 | tf_op jit(solution)/shard_map/tpkgh,nkh->tpkgn/dot_general | solution.py:76
  28.4 1.0 copy-done.1
  29.4 20.1 %collective-permute-done = bf16[2,8,128,512]{3,2,1,0:T(8,128)(2,1)} collective-permute-done((bf16[2,8,128,512]{3,2,1,0:T(8,128)(2,1)}, bf16[2,8,128,512]{3,2,1,0:T(8,128)(2,1)}, u32[]{:S(2)}, u32[]{:S(2)}) %collective-permute-start) | collective-permute-done | bytes 2097184 | tf_op jit(solution)/shard_map/ppermute | solution.py:21
  49.5 3.6 %gather_fusion.1 = bf16[8,2,128,512]{3,2,1,0:T(8,128)(2,1)} fusion(bf16[2,8,128,512]{3,2,1,0:T(8,128)(2,1)} %collective-permute-done, s32[1024]{0:T(1024)S(1)} %pad_clamp_fusion.1), kind=kCustom, calls=%fused_computation.clone | custom fusion | bytes 4194336 | tf_op jit(solution)/shard_map/jit(_take)/gather | solution.py:95
  53.1 43.3 %collective-permute-done.1 = bf16[2,8,128,512]{3,2,1,0:T(8,128)(2,1)} collective-permute-done((bf16[2,8,128,512]{3,2,1,0:T(8,128)(2,1)}, bf16[2,8,128,512]{3,2,1,0:T(8,128)(2,1)}, u32[]{:S(2)}, u32[]{:S(2)}) %collective-permute-start.1) | collective-permute-done | bytes 2097184 | tf_op jit(solution)/shard_map/ppermute | solution.py:21
  96.4 3.6 %gather_fusion.2 = bf16[8,2,128,512]{3,2,1,0:T(8,128)(2,1)} fusion(bf16[2,8,128,512]{3,2,1,0:T(8,128)(2,1)} %collective-permute-done.1, s32[1024]{0:T(1024)S(1)} %pad_clamp_fusion.1), kind=kCustom, calls=%fused_computation.1.clone | custom fusion | bytes 4194336 | tf_op jit(solution)/shard_map/jit(_take)/gather | solution.py:95
  100.0 3.6 %gather_fusion.3 = bf16[8,2,128,512]{3,2,1,0:T(8,128)(2,1)} fusion(bf16[2,8,128,512]{3,2,1,0:T(8,128)(2,1)} %collective-permute-done.2, s32[1024]{0:T(1024)S(1)} %pad_clamp_fusion.1), kind=kCustom, calls=%fused_computation.2.clone | custom fusion | bytes 4194336 | tf_op jit(solution)/shard_map/jit(_take)/gather | solution.py:95
  103.6 3.6 %gather_fusion.4 = bf16[8,2,128,512]{3,2,1,0:T(8,128)(2,1)} fusion(bf16[2,8,128,512]{3,2,1,0:T(8,128)(2,1)} %collective-permute-done.3, s32[1024]{0:T(1024)S(1)} %pad_clamp_fusion.1), kind=kCustom, calls=%fused_computation.3.clone | custom fusion | bytes 4194336 | tf_op jit(solution)/shard_map/jit(_take)/gather | solution.py:95
  107.2 4.0 %fusion.8 = bf16[2,8,128,512]{3,2,0,1:T(8,128)(2,1)S(1)} fusion(bf16[8,2,128,512]{3,2,1,0:T(8,128)(2,1)S(1)} %gather_fusion.5, bf16[8,2,128,512]{3,2,1,0:T(8,128)(2,1)} %gather_fusion.4, bf16[8,2,128,512]{3,2,1,0:T(8,128)(2,1)} %gather_fusion.3, bf16[8,2,128,512]{3,2,1,0:T(8,128)(2,1)} %gather_fusion.2, bf16[8,2,128,512]{3,2,1,0:T(8,128)(2,1)} %gather_fusion.1, ...), kind=kLoop, calls=%fused_computation.16 | loop fusion | flops 10485760 | bytes 12582960 | tf_op jit(solution)/shard_map/jit(_where)/select_n | solution.py:97
  111.4 1.3 %copy.98 = bf16[1,8,128,512]{2,3,1,0:T(8,128)(2,1)} copy(bf16[1,8,128,512]{3,2,0,1:T(8,128)(2,1)S(1)} %get-tuple-element.13) | data formatting | bytes 2097152 | tf_op jit(solution)/shard_map/slice | solution.py:46
  112.7 1.7 %fusion.44 = (f32[4,8,4,8]{3,0,2,1:T(4,128)S(1)}, f32[4,8,4,8,128]{4,3,0,2,1:T(8,128)S(1)}) fusion(bf16[8,128,4,128,1]{1,3,4,2,0:T(8,128)(2,1)} %bitcast.96, bf16[4,8,4,8,128]{4,1,3,2,0:T(8,128)(2,1)} %bitcast.99), kind=kOutput, calls=%fused_computation.80 | convolution fusion | flops 33815552 | bytes 1839104 | tf_op jit(solution)/shard_map/tpkgh,pnkh->tpkgn/dot_general | solution.py:45
  114.5 1.3 %copy.108 = bf16[1,8,128,512]{2,3,1,0:T(8,128)(2,1)} copy(bf16[1,8,128,512]{3,2,0,1:T(8,128)(2,1)S(1)} %get-tuple-element.12) | data formatting | bytes 2097152 | tf_op jit(solution)/shard_map/slice | solution.py:50
  116.4 3.3 %fusion.20 = f32[4,8,4,8,128]{4,3,1,0,2:T(8,128)S(1)} fusion(bf16[1024,4,128,1,1]{0,2,4,3,1:T(8,128)(2,1)S(1)} %bitcast.93, f32[4,1024,4,8,8]{1,4,3,2,0:T(8,128)} %copy-done.1, f32[4,8,4,8]{3,1,0,2:T(8,128)S(1)} %get-tuple-element.30, f32[4,8,4,8]{3,1,0,2:T(8,128)S(1)} %get-tuple-element.5), kind=kOutput, calls=%fused_computation.29 | convolution fusion | flops 271712256 | bytes 5775360 | tf_op jit(solution)/shard_map/tpkgn,nkh->tpkgh/dot_general | solution.py:29
  121.6 3.5 %fusion.45 = f32[1,4,8]{2,0,1:T(1,128)S(1)} fusion(f32[4,8,4096]{2,1,0:T(8,128)S(1)} %reshape.100, f32[4096,1,1]{0,1,2:T(1,128)S(1)} %bitcast.97), kind=kOutput, calls=%fused_computation.81 | convolution fusion | flops 1572864 | bytes 540800 | tf_op jit(solution)/shard_map/tpc,c->tp/dot_general | solution.py:107
  125.1 3.6 %psum.7 = f32[4,8]{1,0:T(4,128)S(1)} all-reduce(f32[4,8]{1,0:T(4,128)S(1)} %bitcast.98), channel_id=1, replica_groups=mesh['groups'=2,'particle'=8,'tensor'=2] {'tensor'}, use_global_device_ids=true, to_apply=%region_7.9 | all-reduce | flops 32 | bytes 256 | tf_op jit(solution)/shard_map/psum | solution.py:108
  (43 shorter events, 6.8 us)
Async XLA Ops:
  0.6 21.6 %copy-start = (f32[128256]{0:T(1024)S(1)}, f32[128256]{0:T(1024)}, u32[]{:S(2)}) copy-start(f32[128256]{0:T(1024)} %param.18) | copy-start | bytes 1539076
  0.6 48.9 %collective-permute-start = (bf16[2,8,128,512]{3,2,1,0:T(8,128)(2,1)}, bf16[2,8,128,512]{3,2,1,0:T(8,128)(2,1)}, u32[]{:S(2)}, u32[]{:S(2)}) collective-permute-start(bf16[2,8,128,512]{3,2,1,0:T(8,128)(2,1)} %param.12), channel_id=1, source_target_pairs={{4,0},{6,2},{8,4},{10,6},{12,8},{14,10},{5,1},{7,3},{9,5},{11,7},{... | collective-permute-start | bytes 6291464 | tf_op jit(solution)/shard_map/ppermute | solution.py:21
  2.7 93.7 %collective-permute-start.1 = (bf16[2,8,128,512]{3,2,1,0:T(8,128)(2,1)}, bf16[2,8,128,512]{3,2,1,0:T(8,128)(2,1)}, u32[]{:S(2)}, u32[]{:S(2)}) collective-permute-start(bf16[2,8,128,512]{3,2,1,0:T(8,128)(2,1)} %param.12), channel_id=1, source_target_pairs={{2,0},{4,2},{6,4},{8,6},{10,8},{12,10},{14,12},{3,1},{5,3},{7,5},{... | collective-permute-start | bytes 6291464 | tf_op jit(solution)/shard_map/ppermute | solution.py:21
  5.1 94.9 %collective-permute-start.2 = (bf16[2,8,128,512]{3,2,1,0:T(8,128)(2,1)}, bf16[2,8,128,512]{3,2,1,0:T(8,128)(2,1)}, u32[]{:S(2)}, u32[]{:S(2)}) collective-permute-start(bf16[2,8,128,512]{3,2,1,0:T(8,128)(2,1)} %param.12), channel_id=1, source_target_pairs={{0,2},{2,4},{4,6},{6,8},{8,10},{10,12},{12,14},{1,3},{3,5},{5,7},{... | collective-permute-start | bytes 6291464 | tf_op jit(solution)/shard_map/ppermute | solution.py:21
  8.0 95.6 %collective-permute-start.3 = (bf16[2,8,128,512]{3,2,1,0:T(8,128)(2,1)}, bf16[2,8,128,512]{3,2,1,0:T(8,128)(2,1)}, u32[]{:S(2)}, u32[]{:S(2)}) collective-permute-start(bf16[2,8,128,512]{3,2,1,0:T(8,128)(2,1)} %param.12), channel_id=1, source_target_pairs={{0,4},{2,6},{4,8},{6,10},{8,12},{10,14},{1,5},{3,7},{5,9},{7,11},{... | collective-permute-start | bytes 6291464 | tf_op jit(solution)/shard_map/ppermute | solution.py:21
  17.5 4.6 %copy-start.6 = (s32[4,8]{1,0:T(4,128)S(1)}, s32[4,8]{1,0:T(4,128)}, u32[]{:S(2)}) copy-start(s32[4,8]{1,0:T(4,128)} %param.17) | copy-start | bytes 388
  19.8 3.2 %copy-start.8 = (s32[1024]{0:T(1024)S(1)}, s32[1024]{0:T(1024)}, u32[]{:S(2)}) copy-start(s32[1024]{0:T(1024)} %param.16) | copy-start | bytes 12292
  19.8 3.5 %copy-start.5 = (bf16[2,4,8,512]{3,2,1,0:T(8,128)(2,1)S(1)}, bf16[2,4,8,512]{3,2,1,0:T(8,128)(2,1)}, u32[]{:S(2)}) copy-start(bf16[2,4,8,512]{3,2,1,0:T(8,128)(2,1)} %param.15) | copy-start | bytes 196612
  19.8 3.5 %copy-start.9 = (bf16[4,8,4096]{2,1,0:T(8,128)(2,1)S(1)}, bf16[4,8,4096]{2,1,0:T(8,128)(2,1)}, u32[]{:S(2)}) copy-start(bf16[4,8,4096]{2,1,0:T(8,128)(2,1)} %param.14) | copy-start | bytes 786436
  27.4 1.9 %copy-start.1 = (f32[4,1024,4,8,8]{1,4,3,2,0:T(8,128)}, f32[4,1024,4,8,8]{1,4,3,2,0:T(8,128)S(1)}, u32[]{:S(2)}) copy-start(f32[4,1024,4,8,8]{1,4,3,2,0:T(8,128)S(1)} %get-tuple-element.31) | copy-start | bytes 12582916
  114.4 1.9 %copy-start.2 = (bf16[1,1024,512]{1,2,0:T(8,128)(2,1)S(1)}, bf16[1,1024,512]{1,2,0:T(8,128)(2,1)}, u32[]{:S(2)}) copy-start(bf16[1,1024,512]{1,2,0:T(8,128)(2,1)} %copy.137) | copy-start | bytes 3145732
  116.3 3.3 %copy-start.4 = (bf16[4,8,4,8,4]{3,4,0,2,1:T(4,128)(2,1)S(1)}, bf16[4,8,4,8,4]{3,4,0,2,1:T(4,128)(2,1)}, u32[]{:S(2)}) copy-start(bf16[4,8,4,8,4]{3,4,0,2,1:T(4,128)(2,1)} %get-tuple-element.18) | copy-start | bytes 24580
  116.4 3.6 %copy-start.3 = (bf16[1,8,128,512]{2,3,1,0:T(8,128)(2,1)S(1)}, bf16[1,8,128,512]{2,3,1,0:T(8,128)(2,1)}, u32[]{:S(2)}) copy-start(bf16[1,8,128,512]{2,3,1,0:T(8,128)(2,1)} %copy.108) | copy-start | bytes 3145732
  120.7 0.9 copy-start.7
where the time goes:
time: 131 us; the launch traced here: 129 us
  waiting for transfers between devices  63.4 us (48%)
  local copies, waits for them, and re-layouts  29.3 us (22%)
  matrix products  12.8 us (10%)
  starting transfers between devices  10.7 us (8%)
  other arithmetic  8.6 us (7%)
  blocking collectives  3.65 us (3%)
    ppermute x4, waiting for transfers between devices, shifted(): return lax.ppermute(value, axis, pairs)  63.4 us
    gather x5, local copies, waits for them, and re-layouts, pick_from(): chosen = jnp.take(source, own_slot, axis=1)  16.7 us
    ppermute x4, starting transfers between devices, shifted(): return lax.ppermute(value, axis, pairs)  10.7 us
    unnamed x22, local copies, waits for them, and re-layouts  5.66 us
    dot_general x3, matrix products, finish_block(): jnp.einsum(pattern, weights, values, preferred_element_type=jnp.float32)  4.26 us
    select_n x1, other arithmetic, pick_from(): return jnp.where(is_parent, chosen, current)  4 us
    psum x1, blocking collectives, on_device(): twist_attn = lax.psum(partial_value, 'tensor')  3.65 us
    dot_general x1, matrix products, on_device(): jnp.einsum('tpc,c->tp', context, readout, precision=lax.Precision.HIGHEST)  3.54 us
  transfers between devices with their start and end apart: 4, of which 2 were waited for; matrix products, arithmetic and copies ran while one was open for 21% of the time, Pallas kernels for 0%

commit v1 on v0

v1 whole, which is shorter than its diff:
```python
import functools
import math

import jax
import jax.numpy as jnp
from jax import lax
from jax.experimental import pallas as pl
from jax.experimental.pallas import tpu as pltpu
from jax.sharding import PartitionSpec as P

HEADS = 64
KV_HEADS = 8
HEAD = 128
REACH = 2
GROUP = HEADS // KV_HEADS
EXPONENT_SCALE = math.log2(math.e) / math.sqrt(HEAD)

NEG_FILL = -1e30
LOG_STEPS = 32.0
LOG_FRACTION = 65534.0
TOP_CODE = 32000.0
TINY = 1e-30

F32 = jnp.float32
BF16 = jnp.bfloat16
VMEM = pltpu.MemorySpace.VMEM
SMEM = pltpu.MemorySpace.SMEM


def exchanges(length):
    found = []
    for reach in range(REACH, 0, -1):
        for parity in (0, 1):
            pairs = []
            for i in range(length - reach):
                if (i // reach) % 2 == parity:
                    pairs += [(i, i + reach), (i + reach, i)]
            found.append((reach, parity, pairs))
    return found


def partner_of(index, reach, parity):
    return jnp.where((index // reach) % 2 == parity, index + reach, index - reach)


def slots_on(ancestors_ref, owner, holder, length, count):
    safe = jnp.clip(owner, 0, length - 1)
    exists = safe == owner
    rows = lax.broadcasted_iota(jnp.int32, (count, 1), 0)
    slots = jnp.full((count, 1), -1, jnp.int32)
    for p in range(count):
        slot = ancestors_ref[safe * count + p] - holder * count
        here = exists & (slot >= 0) & (slot < count)
        slots = jnp.where(rows == p, jnp.where(here, slot, -1), slots)
    return slots


def head_rows(query_ref, base):
    steps = query_ref.shape[0]
    pieces = [
        query_ref[t, :, base + g * HEAD : base + (g + 1) * HEAD].astype(F32)
        for t in range(steps)
        for g in range(GROUP)
    ]
    return jnp.concatenate(pieces, axis=0).astype(BF16)


def scores_of(rows, keys):
    return lax.dot_general(rows, keys, (((1,), (1,)), ((), ())), preferred_element_type=F32)


def softmax_terms(scores):
    top = jnp.max(scores, axis=-1, keepdims=True)
    expo = jnp.exp2((scores - top) * EXPONENT_SCALE)
    return top, expo, jnp.sum(expo, axis=-1, keepdims=True)


def tail_block(rows, keys, values, slots):
    count, length = keys.shape[0], keys.shape[1]
    scores = scores_of(rows, keys.reshape(count * length, HEAD))
    scores = scores.reshape(-1, count, count * length)
    picked = scores[:, :, :length]
    for j in range(1, count):
        picked = jnp.where((slots == j)[None], scores[:, :, j * length : (j + 1) * length], picked)
    top, expo, total = softmax_terms(picked)
    spread = jnp.concatenate(
        [jnp.where((slots == j)[None], expo, 0.0) for j in range(count)], axis=-1
    )
    spread = spread.reshape(-1, count * length).astype(BF16)
    out = jnp.dot(spread, values.reshape(count * length, HEAD), preferred_element_type=F32)
    return out.reshape(-1, count, HEAD), top, total


def pack_columns(columns, first, steps, count):
    lanes = lax.broadcasted_iota(jnp.int32, (count, 128), 1)
    packed = []
    for t in range(steps):
        held = jnp.zeros((count, 128), columns.dtype)
        for g in range(GROUP):
            held = jnp.where(lanes == first + g, columns[t * GROUP + g], held)
        packed.append(held)
    return packed


def local_kernel(length, ancestors_ref, query_ref, prefix_ref, tail_ref, fresh_ref, out_ref, log_ref):
    steps, count = query_ref.shape[0], query_ref.shape[1]
    heads = prefix_ref.shape[2] // HEAD
    me = lax.axis_index("particle")
    slots = slots_on(ancestors_ref, me, me, length, count)
    own = (slots >= 0)[None]
    logs = [jnp.zeros((count, 128), F32) for _ in range(steps)]
    for k in range(heads):
        cols = slice(k * HEAD, (k + 1) * HEAD)
        rows = head_rows(query_ref, k * GROUP * HEAD)
        many = rows.shape[0]
        top1, expo1, total1 = softmax_terms(scores_of(rows, prefix_ref[0, :, cols]))
        out1 = jnp.dot(expo1.astype(BF16), prefix_ref[1, :, cols], preferred_element_type=F32)
        fresh_keys = jnp.concatenate([fresh_ref[0, s, :, cols].astype(F32) for s in range(steps)], axis=0)
        fresh_values = jnp.concatenate([fresh_ref[1, s, :, cols].astype(F32) for s in range(steps)], axis=0)
        scores2 = scores_of(rows, fresh_keys.astype(BF16))
        row = lax.broadcasted_iota(jnp.int32, scores2.shape, 0)
        col = lax.broadcasted_iota(jnp.int32, scores2.shape, 1)
        seen = (row % count == col % count) & (col // count <= row // (GROUP * count))
        top2, expo2, total2 = softmax_terms(jnp.where(seen, scores2, NEG_FILL))
        out2 = jnp.dot(expo2.astype(BF16), fresh_values.astype(BF16), preferred_element_type=F32)
        out3, top3, total3 = tail_block(rows, tail_ref[0, :, :, cols], tail_ref[1, :, :, cols], slots)
        shape = (many // count, count, 1)
        top1, total1 = top1.reshape(shape), total1.reshape(shape)
        top2, total2 = top2.reshape(shape), total2.reshape(shape)
        out1 = out1.reshape(many // count, count, HEAD)
        out2 = out2.reshape(many // count, count, HEAD)
        top3 = jnp.where(own, top3, NEG_FILL)
        top = jnp.maximum(jnp.maximum(top1, top2), top3)
        share1 = jnp.exp2((top1 - top) * EXPONENT_SCALE)
        share2 = jnp.exp2((top2 - top) * EXPONENT_SCALE)
        share3 = jnp.where(own, jnp.exp2((top3 - top) * EXPONENT_SCALE), 0.0)
        total = share1 * total1 + share2 * total2 + share3 * total3
        context = (share1 * out1 + share2 * out2 + share3 * out3) / total
        for t in range(steps):
            for g in range(GROUP):
                at = (k * GROUP + g) * HEAD
                out_ref[t, :, at : at + HEAD] = context[t * GROUP + g]
        level = top * EXPONENT_SCALE + jnp.log2(total)
        logs = [a + b for a, b in zip(logs, pack_columns(level, k * GROUP, steps, count))]
    for t in range(steps):
        log_ref[t] = logs[t]


def serve_kernel(length, reach, parity, ancestors_ref, query_ref, tail_ref, out_ref):
    steps, count = query_ref.shape[0], query_ref.shape[1]
    heads = tail_ref.shape[3] // HEAD
    lanes = heads * GROUP
    me = lax.axis_index("particle")
    slots = slots_on(ancestors_ref, partner_of(me, reach, parity), me, length, count)
    notes = [jnp.zeros((count, 128), F32) for _ in range(steps)]
    for k in range(heads):
        cols = slice(k * HEAD, (k + 1) * HEAD)
        rows = head_rows(query_ref, k * GROUP * HEAD)
        out, top, total = tail_block(rows, tail_ref[0, :, :, cols], tail_ref[1, :, :, cols], slots)
        mean = out / total
        largest = jnp.maximum(jnp.max(jnp.abs(mean), axis=-1, keepdims=True), TINY)
        power = jnp.ceil(jnp.log2(largest * (1.0 / TOP_CODE)))
        code = jnp.round(mean * jnp.exp2(-power)).astype(jnp.int32)
        for t in range(steps):
            for g in range(GROUP):
                at = (k * GROUP + g) * HEAD
                out_ref[t, :, at : at + HEAD] = code[t * GROUP + g].astype(jnp.int16)
        level = (top * EXPONENT_SCALE + jnp.log2(total)) * LOG_STEPS
        whole = jnp.round(level)
        part = jnp.round((level - whole) * LOG_FRACTION)
        for base, column in ((0, whole), (lanes, part), (2 * lanes, power)):
            packed = pack_columns(column, base + k * GROUP, steps, count)
            notes = [a + b for a, b in zip(notes, packed)]
    at = lanes * HEAD
    for t in range(steps):
        out_ref[t, :, at : at + 128] = notes[t].astype(jnp.int32).astype(jnp.int16)


def combine_kernel(length, plans, ancestors_ref, local_ref, log_ref, readout_ref, *refs):
    remote_refs, (out_ref, twist_ref) = refs[: len(plans)], refs[len(plans) :]
    steps, count = local_ref.shape[0], local_ref.shape[1]
    lanes = local_ref.shape[2] // HEAD
    me = lax.axis_index("particle")
    from_plan = [
        slots_on(ancestors_ref, me, partner_of(me, reach, parity), length, count) >= 0
        for reach, parity in plans
    ]
    away = functools.reduce(jnp.logical_or, from_plan)

    def chosen(t, at):
        value = remote_refs[0][t, :, at : at + HEAD].astype(jnp.int32)
        for ref, mine in zip(remote_refs[1:], from_plan[1:]):
            value = jnp.where(mine, ref[t, :, at : at + HEAD].astype(jnp.int32), value)
        return value.astype(F32)

    row = lax.broadcasted_iota(jnp.int32, (count, 128), 0)
    lane = lax.broadcasted_iota(jnp.int32, (count, 128), 1)
    for t in range(steps):
        notes = chosen(t, lanes * HEAD)
        whole, part, power = (notes[:, i * lanes : (i + 1) * lanes] for i in range(3))
        remote_level = (whole + part * (1.0 / LOG_FRACTION)) * (1.0 / LOG_STEPS)
        remote_level = jnp.where(away, remote_level, NEG_FILL)
        local_level = log_ref[t, :, :lanes]
        level = jnp.maximum(local_level, remote_level)
        local_share = jnp.exp2(local_level - level)
        remote_share = jnp.where(away, jnp.exp2(remote_level - level), 0.0)
        total = local_share + remote_share
        local_share = local_share / total
        remote_share = remote_share / total * jnp.exp2(power)
        gathered = jnp.zeros((count, HEAD), F32)
        for h in range(lanes):
            at = h * HEAD
            context = local_share[:, h : h + 1] * local_ref[t, :, at : at + HEAD]
            context = context + remote_share[:, h : h + 1] * chosen(t, at)
            out_ref[t, :, at : at + HEAD] = context.astype(BF16)
            gathered = gathered + context * readout_ref[:, at : at + HEAD]
        column = jnp.sum(gathered, axis=-1, keepdims=True)
        line = jnp.sum(jnp.where(row == lane, column, 0.0), axis=0, keepdims=True)
        twist_ref[t : t + 1, :] = line[:, :count]


def call(kernel, outs, name, operands, flops, limit=24 << 20):
    moved = sum(math.prod(o.shape) * o.dtype.itemsize for o in operands)
    moved += sum(math.prod(o.shape) * o.dtype.itemsize for o in outs)
    specs = [pl.BlockSpec(memory_space=SMEM)] + [pl.BlockSpec(memory_space=VMEM)] * (len(operands) - 1)
    return pl.pallas_call(
        kernel,
        out_shape=tuple(outs),
        in_specs=specs,
        out_specs=tuple(pl.BlockSpec(memory_space=VMEM) for _ in outs),
        compiler_params=pltpu.CompilerParams(vmem_limit_bytes=limit),
        cost_estimate=pl.CostEstimate(flops=flops, bytes_accessed=moved, transcendentals=0),
        name=name,
    )(*operands)


def on_device(
    length,
    prefix_cache,
    tail_cache,
    ancestors,
    queries,
    fresh_kv,
    prompt_ids,
    sampled_ids,
    twist_table,
    readout,
):
    steps, count, width = queries.shape
    lanes = width // HEAD
    plans = exchanges(length)
    asked = [lax.ppermute(queries, "particle", pairs) for _, _, pairs in plans]
    work = 4 * steps * count * width * HEAD
    tail_work = 4 * steps * count * width * count * tail_cache.shape[2]
    local_work = 4 * steps * count * width * (prefix_cache.shape[1] + count * tail_cache.shape[2]) + work
    local, logs = call(
        functools.partial(local_kernel, length),
        [
            jax.ShapeDtypeStruct(queries.shape, F32),
            jax.ShapeDtypeStruct((steps, count, 128), F32),
        ],
        "local",
        [ancestors, queries, prefix_cache, tail_cache, fresh_kv],
        local_work,
    )
    answers = []
    for (reach, parity, pairs), question in zip(plans, asked):
        (answer,) = call(
            functools.partial(serve_kernel, length, reach, parity),
            [jax.ShapeDtypeStruct((steps, count, width + 128), jnp.int16)],
            "serve",
            [ancestors, question, tail_cache],
            tail_work,
        )
        answers.append(lax.ppermute(answer, "particle", pairs))
    attended, partial_value = call(
        functools.partial(combine_kernel, length, [plan[:2] for plan in plans]),
        [
            jax.ShapeDtypeStruct(queries.shape, BF16),
            jax.ShapeDtypeStruct((steps, count), F32),
        ],
        "combine",
        [ancestors, local, logs, readout.reshape(1, width)] + answers,
        16 * steps * count * width,
    )
    other = lax.axis_size("tensor")
    swap = [(i, (i + 1) % other) for i in range(other)]
    twist_attn = partial_value + lax.ppermute(partial_value, "tensor", swap)
    repeats = jnp.sum(
        (sampled_ids[:, :, None] == prompt_ids[None, None, :]).astype(jnp.int32), axis=-1
    )
    twists = jnp.take(twist_table, sampled_ids) - 2.0 * repeats.astype(F32) + twist_attn
    return (attended, twists)


def solution(mesh):
    return jax.shard_map(
        functools.partial(on_device, mesh.shape["particle"]),
        mesh=mesh,
        in_specs=(
            P(None, "groups", "tensor"),
            P(None, ("groups", "particle"), None, "tensor"),
            P("groups"),
            P(None, ("groups", "particle"), "tensor"),
            P(None, None, ("groups", "particle"), "tensor"),
            P("groups"),
            P(None, ("groups", "particle")),
            P(),
            P("tensor"),
        ),
        out_specs=(P(None, ("groups", "particle"), "tensor"), P(None, ("groups", "particle"))),
        check_vma=False,
    )
```

time: 131 us -> 45.8 us (0.35); the launches traced: 129 us -> 45.5 us
  waiting for transfers between devices: 63.4 us -> 3.24 us
  local copies, waits for them, and re-layouts: 29.3 us -> 3.17 us
  Pallas kernels: 0 us -> 18.7 us
  matrix products: 12.8 us -> 0 us
  starting transfers between devices: 10.7 us -> 18.1 us
  other arithmetic: 8.6 us -> 1.5 us
  blocking collectives: 3.65 us -> 0 us
    ppermute x4 -> x9, waiting for transfers between devices: 63.4 us -> 3.24 us  [the longest x4 3.2 us: on_device(): asked = [lax.ppermute(queries, 'particle', pairs) for _, _, pairs in plans]]
    pallas_call x0 -> x6, Pallas kernels: none -> 18.7 us  [call(): pl.pallas_call(kernel, out_shape=tuple(outs), in_specs=specs, out_specs=t...]
    gather x7 -> x2, local copies, waits for them, and re-layouts: 17.5 us -> 0.78 us  [on_device(): jnp.take(twist_table, sampled_ids) - 2.0 * repeats.astype(F32) + twist_attn]
    dot_general x7 -> x0, matrix products: 12.8 us -> none  [the longest x3 4.26 us: finish_block(): jnp.einsum(pattern, weights, values, preferred_element_type=jnp.float32)]
    ppermute x4 -> x9, starting transfers between devices: 10.7 us -> 18.1 us  [the longest x4 7.86 us: on_device(): asked = [lax.ppermute(queries, 'particle', pairs) for _, _, pairs in plans]]
    slice x4 -> x0, local copies, waits for them, and re-layouts: 5.87 us -> none  [the longest x1 3.09 us: on_device(): prefix_heads[1]]
    psum x1 -> x0, blocking collectives: 3.65 us -> none  [on_device(): twist_attn = lax.psum(partial_value, 'tensor')]
    unnamed x22, local copies, waits for them, and re-layouts: 5.66 us -> 2.31 us
  transfers between devices with their start and end apart: 4 -> 9, of which waited for: 2 -> 1; matrix products, arithmetic and copies ran while one was open for 21% -> 4% of each run, Pallas kernels for 0% -> 36%
where the time goes in v1:
time: 45.8 us; the launch traced here: 45.5 us
  Pallas kernels  18.7 us (41%)
  starting transfers between devices  18.1 us (40%)
  waiting for transfers between devices  3.24 us (7%)
  local copies, waits for them, and re-layouts  3.17 us (7%)
  other arithmetic  1.5 us (3%)
  between operations  0.89 us (2%)
    pallas_call x6, Pallas kernels, call(): pl.pallas_call(kernel, out_shape=tuple(outs), in_specs=specs, out_specs=t...  18.7 us
    ppermute x4, starting transfers between devices, on_device(): asked = [lax.ppermute(queries, 'particle', pairs) for _, _, pairs in plans]  7.86 us
    ppermute x4, starting transfers between devices, on_device(): answers.append(lax.ppermute(answer, 'particle', pairs))  7.16 us
    ppermute x4, waiting for transfers between devices, on_device(): asked = [lax.ppermute(queries, 'particle', pairs) for _, _, pairs in plans]  3.2 us
    ppermute x1, starting transfers between devices, on_device(): twist_attn = partial_value + lax.ppermute(partial_value, 'tensor', swap)  3.03 us
    unnamed x22, local copies, waits for them, and re-layouts  2.31 us
  transfers between devices with their start and end apart: 9, of which 1 were waited for; matrix products, arithmetic and copies ran while one was open for 4% of the time, Pallas kernels for 36%

profile of v1, /device:TPU:9, one launch (start us, length us, event | category | flops | bytes accessed | tf_op | source)
XLA Modules:
  0.0 45.5 jit_solution(2892934770996909197)
XLA Ops:
  0.6 1.3 %collective-permute-start.4 = (bf16[4,8,4096]{2,1,0:T(8,128)(2,1)}, bf16[4,8,4096]{2,1,0:T(8,128)(2,1)S(1)}, u32[]{:S(2)}, u32[]{:S(2)}) collective-permute-start(bf16[4,8,4096]{2,1,0:T(8,128)(2,1)} %query_ref.1), channel_id=1, source_target_pairs={{0,2},{2,0},{4,6},{6,4},{8,10},{10,8},{12,14},{14,12},{1,3},{3,1},... | collective-permute-start | bytes 786440 | tf_op jit(solution)/shard_map/ppermute | solution.py:252
  1.9 3.2 %collective-permute-start.2 = (bf16[4,8,4096]{2,1,0:T(8,128)(2,1)}, bf16[4,8,4096]{2,1,0:T(8,128)(2,1)S(1)}, u32[]{:S(2)}, u32[]{:S(2)}) collective-permute-start(bf16[4,8,4096]{2,1,0:T(8,128)(2,1)} %query_ref.1), channel_id=1, source_target_pairs={{4,8},{8,4},{6,10},{10,6},{5,9},{9,5},{7,11},{11,7},{20,24},{24,20... | collective-permute-start | bytes 786440 | tf_op jit(solution)/shard_map/ppermute | solution.py:252
  5.1 0.1 collective-permute-start
  5.2 3.3 %collective-permute-start.6 = (bf16[4,8,4096]{2,1,0:T(8,128)(2,1)}, bf16[4,8,4096]{2,1,0:T(8,128)(2,1)S(1)}, u32[]{:S(2)}, u32[]{:S(2)}) collective-permute-start(bf16[4,8,4096]{2,1,0:T(8,128)(2,1)} %query_ref.1), channel_id=1, source_target_pairs={{2,4},{4,2},{6,8},{8,6},{10,12},{12,10},{3,5},{5,3},{7,9},{9,7},{1... | collective-permute-start | bytes 786440 | tf_op jit(solution)/shard_map/ppermute | solution.py:252
  8.5 0.7 %compare_select_fusion = s32[4,8]{1,0:T(4,128)S(1)} fusion(s32[4,8]{1,0:T(4,128)} %param.15), kind=kLoop, calls=%fused_computation.2 | loop fusion | flops 96 | bytes 256 | tf_op jit(solution)/shard_map/jit(_take)/jit(_where)/select_n | solution.py:292
  9.2 1.6 %copy-done.1 = bf16[2,8,128,512]{3,2,1,0:T(8,128)(2,1)S(1)} copy-done((bf16[2,8,128,512]{3,2,1,0:T(8,128)(2,1)S(1)}, bf16[2,8,128,512]{3,2,1,0:T(8,128)(2,1)}, u32[]{:S(2)}) %copy-start.1) | copy-done | bytes 2097176
  10.8 0.7 %copy-done.6 = s32[64]{0:T(128)S(1)} copy-done((s32[64]{0:T(128)S(1)}, s32[64]{0:T(128)}, u32[]{:S(2)}) %copy-start.6) | copy-done | bytes 280
  11.5 2.8 %serve.6 = s16[4,8,4224]{2,1,0:T(8,128)(2,1)S(1)} custom-call(s32[64]{0:T(128)S(1)} %copy-done.6, bf16[4,8,4096]{2,1,0:T(8,128)(2,1)S(1)} %collective-permute-done.4.query_ref, bf16[2,8,128,512]{3,2,1,0:T(8,128)(2,1)S(1)} %copy-done.1), custom_call_target="tpu_custom_call" | custom-call | flops 536870912 | bytes 2629888 | tf_op jit(solution)/shard_map/serve/pallas_call | solution.py:226
  14.3 0.2 collective-permute-start.5
  14.4 3.2 %collective-permute-done.6.query_ref = bf16[4,8,4096]{2,1,0:T(8,128)(2,1)S(1)} collective-permute-done((bf16[4,8,4096]{2,1,0:T(8,128)(2,1)}, bf16[4,8,4096]{2,1,0:T(8,128)(2,1)S(1)}, u32[]{:S(2)}, u32[]{:S(2)}) %collective-permute-start.6) | collective-permute-done | bytes 262176 | tf_op jit(solution)/shard_map/ppermute | solution.py:252
  17.6 2.8 %serve.7 = s16[4,8,4224]{2,1,0:T(8,128)(2,1)S(1)} custom-call(s32[64]{0:T(128)S(1)} %copy-done.6, bf16[4,8,4096]{2,1,0:T(8,128)(2,1)S(1)} %collective-permute-done.6.query_ref, bf16[2,8,128,512]{3,2,1,0:T(8,128)(2,1)S(1)} %copy-done.1), custom_call_target="tpu_custom_call" | custom-call | flops 536870912 | bytes 2629888 | tf_op jit(solution)/shard_map/serve/pallas_call | solution.py:226
  20.5 3.4 %collective-permute-start.7 = (s16[4,8,4224]{2,1,0:T(8,128)(2,1)S(1)}, s16[4,8,4224]{2,1,0:T(8,128)(2,1)S(1)}, u32[]{:S(2)}, u32[]{:S(2)}) collective-permute-start(s16[4,8,4224]{2,1,0:T(8,128)(2,1)S(1)} %serve.7), channel_id=1, source_target_pairs={{2,4},{4,2},{6,8},{8,6},{10,12},{12,10},{3,5},{5,3},{7,9},{9,7},{1... | collective-permute-start | bytes 811016 | tf_op jit(solution)/shard_map/ppermute | solution.py:275
  23.9 2.8 %serve.4 = s16[4,8,4224]{2,1,0:T(8,128)(2,1)S(1)} custom-call(s32[64]{0:T(128)S(1)} %copy-done.6, bf16[4,8,4096]{2,1,0:T(8,128)(2,1)S(1)} %collective-permute-done.query_ref, bf16[2,8,128,512]{3,2,1,0:T(8,128)(2,1)S(1)} %copy-done.1), custom_call_target="tpu_custom_call" | custom-call | flops 536870912 | bytes 2629888 | tf_op jit(solution)/shard_map/serve/pallas_call | solution.py:226
  26.7 0.1 collective-permute-start.1
  26.7 2.8 %serve.5 = s16[4,8,4224]{2,1,0:T(8,128)(2,1)S(1)} custom-call(s32[64]{0:T(128)S(1)} %copy-done.6, bf16[4,8,4096]{2,1,0:T(8,128)(2,1)S(1)} %collective-permute-done.2.query_ref, bf16[2,8,128,512]{3,2,1,0:T(8,128)(2,1)S(1)} %copy-done.1), custom_call_target="tpu_custom_call" | custom-call | flops 536870912 | bytes 2629888 | tf_op jit(solution)/shard_map/serve/pallas_call | solution.py:226
  29.6 3.5 %collective-permute-start.3 = (s16[4,8,4224]{2,1,0:T(8,128)(2,1)S(1)}, s16[4,8,4224]{2,1,0:T(8,128)(2,1)S(1)}, u32[]{:S(2)}, u32[]{:S(2)}) collective-permute-start(s16[4,8,4224]{2,1,0:T(8,128)(2,1)S(1)} %serve.5), channel_id=1, source_target_pairs={{4,8},{8,4},{6,10},{10,6},{5,9},{9,5},{7,11},{11,7},{20,24},{24,20... | collective-permute-start | bytes 811016 | tf_op jit(solution)/shard_map/ppermute | solution.py:275
  33.2 5.4 %local.1 = (f32[4,8,4096]{2,1,0:T(8,128)S(1)}, f32[4,8,128]{2,1,0:T(8,128)S(1)}) custom-call(s32[64]{0:T(128)S(1)} %copy-done.6, bf16[4,8,4096]{2,1,0:T(8,128)(2,1)S(1)} %copy-done.4, bf16[2,1024,512]{2,1,0:T(8,128)(2,1)S(1)} %copy-done.3, bf16[2,8,128,512]{3,2,1,0:T(8,128)(2,1)S(1)} %copy-done.2, bf16[2,4,8,512]{3,2,1,0:T(8,128)(2,1)S(1)} %copy-done.5), custom_call_target="tpu_custom_call" | custom-call | flops 1140850688 | bytes 5062912 | tf_op jit(solution)/shard_map/local/pallas_call | solution.py:226
  38.6 0.1 reshape.17
  38.7 0.2 convert_reduce_fusion
  39.0 2.1 %combine.1 = (bf16[4,8,4096]{2,1,0:T(8,128)(2,1)}, f32[4,8]{1,0:T(4,128)S(1)}) custom-call(s32[64]{0:T(128)S(1)} %copy-done.7, f32[4,8,4096]{2,1,0:T(8,128)S(1)} %get-tuple-element.6.local_ref, f32[4,8,128]{2,1,0:T(8,128)S(1)} %get-tuple-element.7.log_ref, f32[1,4096]{1,0:T(1,128)S(1)} %bitcast.1, s16[4,8,4224]{2,1,0:T(8,128)(2,1)S(1)} %collective-permute-done.1.refs_0_, ...), custom_call_target="tpu_custom_call" | custom-call | flops 2097152 | bytes 1900928 | tf_op jit(solution)/shard_map/combine/pallas_call | solution.py:226
  41.1 3.0 %collective-permute-start.8 = (f32[4,8]{1,0:T(4,128)S(1)}, f32[4,8]{1,0:T(4,128)S(1)}, u32[]{:S(2)}, u32[]{:S(2)}) collective-permute-start(f32[4,8]{1,0:T(4,128)S(1)} %get-tuple-element.9), channel_id=1, source_target_pairs={{0,1},{1,0},{2,3},{3,2},{4,5},{5,4},{6,7},{7,6},{8,9},{9,8},{10,11... | collective-permute-start | bytes 392 | tf_op jit(solution)/shard_map/ppermute | solution.py:288
  44.1 0.7 %gather_fusion = f32[32]{0:T(128)S(1)} fusion(f32[128256]{0:T(1024)S(1)} %copy-done, s32[1024]{0:T(1024)S(1)} %pad_clamp_fusion), kind=kCustom, calls=%fused_computation | custom fusion | bytes 384 | tf_op jit(solution)/shard_map/jit(_take)/gather | solution.py:292
  44.8 0.1 reshape.16
  45.0 0.6 %add_add_fusion = f32[4,8]{1,0:T(4,128)} fusion(f32[4,8]{1,0:T(4,128)S(1)} %get-tuple-element.9, f32[4,8]{1,0:T(4,128)S(1)} %collective-permute-done.8, s32[4,8]{1,0:T(4,128)S(1)} %convert_reduce_fusion, f32[4,8]{1,0:T(4,128)S(1)} %reshape.16, s32[4,8]{1,0:T(4,128)S(1)} %copy-done.9), kind=kLoop, calls=%fused_computation.4 | loop fusion | flops 384 | bytes 768 | tf_op jit(solution)/shard_map/add | solution.py:292
  (29 shorter events, 0.1 us)
Async XLA Ops:
  0.6 43.5 %copy-start = (f32[128256]{0:T(1024)S(1)}, f32[128256]{0:T(1024)}, u32[]{:S(2)}) copy-start(f32[128256]{0:T(1024)} %param.16) | copy-start | bytes 1539076
  0.6 8.6 %collective-permute-start.4 = (bf16[4,8,4096]{2,1,0:T(8,128)(2,1)}, bf16[4,8,4096]{2,1,0:T(8,128)(2,1)S(1)}, u32[]{:S(2)}, u32[]{:S(2)}) collective-permute-start(bf16[4,8,4096]{2,1,0:T(8,128)(2,1)} %query_ref.1), channel_id=1, source_target_pairs={{0,2},{2,0},{4,6},{6,4},{8,10},{10,8},{12,14},{14,12},{1,3},{3,1},... | collective-permute-start | bytes 786440 | tf_op jit(solution)/shard_map/ppermute | solution.py:252
  1.9 24.8 %collective-permute-start.2 = (bf16[4,8,4096]{2,1,0:T(8,128)(2,1)}, bf16[4,8,4096]{2,1,0:T(8,128)(2,1)S(1)}, u32[]{:S(2)}, u32[]{:S(2)}) collective-permute-start(bf16[4,8,4096]{2,1,0:T(8,128)(2,1)} %query_ref.1), channel_id=1, source_target_pairs={{4,8},{8,4},{6,10},{10,6},{5,9},{9,5},{7,11},{11,7},{20,24},{24,20... | collective-permute-start | bytes 786440 | tf_op jit(solution)/shard_map/ppermute | solution.py:252
  5.1 18.7 %collective-permute-start = (bf16[4,8,4096]{2,1,0:T(8,128)(2,1)}, bf16[4,8,4096]{2,1,0:T(8,128)(2,1)S(1)}, u32[]{:S(2)}, u32[]{:S(2)}) collective-permute-start(bf16[4,8,4096]{2,1,0:T(8,128)(2,1)} %query_ref.1), channel_id=1, source_target_pairs={{0,4},{4,0},{2,6},{6,2},{8,12},{12,8},{10,14},{14,10},{1,5},{5,1},... | collective-permute-start | bytes 786440 | tf_op jit(solution)/shard_map/ppermute | solution.py:252
  5.2 12.4 %collective-permute-start.6 = (bf16[4,8,4096]{2,1,0:T(8,128)(2,1)}, bf16[4,8,4096]{2,1,0:T(8,128)(2,1)S(1)}, u32[]{:S(2)}, u32[]{:S(2)}) collective-permute-start(bf16[4,8,4096]{2,1,0:T(8,128)(2,1)} %query_ref.1), channel_id=1, source_target_pairs={{2,4},{4,2},{6,8},{8,6},{10,12},{12,10},{3,5},{5,3},{7,9},{9,7},{1... | collective-permute-start | bytes 786440 | tf_op jit(solution)/shard_map/ppermute | solution.py:252
  9.2 1.6 %copy-start.1 = (bf16[2,8,128,512]{3,2,1,0:T(8,128)(2,1)S(1)}, bf16[2,8,128,512]{3,2,1,0:T(8,128)(2,1)}, u32[]{:S(2)}) copy-start(bf16[2,8,128,512]{3,2,1,0:T(8,128)(2,1)} %tail_ref.9) | copy-start | bytes 6291460
  10.8 0.7 %copy-start.6 = (s32[64]{0:T(128)S(1)}, s32[64]{0:T(128)}, u32[]{:S(2)}) copy-start(s32[64]{0:T(128)} %ancestors_ref.11) | copy-start | bytes 772
  14.3 24.7 %collective-permute-start.5 = (s16[4,8,4224]{2,1,0:T(8,128)(2,1)S(1)}, s16[4,8,4224]{2,1,0:T(8,128)(2,1)S(1)}, u32[]{:S(2)}, u32[]{:S(2)}) collective-permute-start(s16[4,8,4224]{2,1,0:T(8,128)(2,1)S(1)} %serve.6), channel_id=1, source_target_pairs={{0,2},{2,0},{4,6},{6,4},{8,10},{10,8},{12,14},{14,12},{1,3},{3,1},... | collective-permute-start | bytes 811016 | tf_op jit(solution)/shard_map/ppermute | solution.py:275
  20.4 12.7 %copy-start.2 = (bf16[2,8,128,512]{3,2,1,0:T(8,128)(2,1)S(1)}, bf16[2,8,128,512]{3,2,1,0:T(8,128)(2,1)}, u32[]{:S(2)}) copy-start(bf16[2,8,128,512]{3,2,1,0:T(8,128)(2,1)} %tail_ref.9) | copy-start | bytes 6291460
  20.4 12.7 %copy-start.3 = (bf16[2,1024,512]{2,1,0:T(8,128)(2,1)S(1)}, bf16[2,1024,512]{2,1,0:T(8,128)(2,1)}, u32[]{:S(2)}) copy-start(bf16[2,1024,512]{2,1,0:T(8,128)(2,1)} %prefix_ref.1) | copy-start | bytes 6291460
  20.4 12.7 %copy-start.4 = (bf16[4,8,4096]{2,1,0:T(8,128)(2,1)S(1)}, bf16[4,8,4096]{2,1,0:T(8,128)(2,1)}, u32[]{:S(2)}) copy-start(bf16[4,8,4096]{2,1,0:T(8,128)(2,1)} %query_ref.1) | copy-start | bytes 786436
  20.4 12.7 %copy-start.5 = (bf16[2,4,8,512]{3,2,1,0:T(8,128)(2,1)S(1)}, bf16[2,4,8,512]{3,2,1,0:T(8,128)(2,1)}, u32[]{:S(2)}) copy-start(bf16[2,4,8,512]{3,2,1,0:T(8,128)(2,1)} %fresh_ref.1) | copy-start | bytes 196612
  20.5 18.5 %collective-permute-start.7 = (s16[4,8,4224]{2,1,0:T(8,128)(2,1)S(1)}, s16[4,8,4224]{2,1,0:T(8,128)(2,1)S(1)}, u32[]{:S(2)}, u32[]{:S(2)}) collective-permute-start(s16[4,8,4224]{2,1,0:T(8,128)(2,1)S(1)} %serve.7), channel_id=1, source_target_pairs={{2,4},{4,2},{6,8},{8,6},{10,12},{12,10},{3,5},{5,3},{7,9},{9,7},{1... | collective-permute-start | bytes 811016 | tf_op jit(solution)/shard_map/ppermute | solution.py:275
  26.7 12.3 %collective-permute-start.1 = (s16[4,8,4224]{2,1,0:T(8,128)(2,1)S(1)}, s16[4,8,4224]{2,1,0:T(8,128)(2,1)S(1)}, u32[]{:S(2)}, u32[]{:S(2)}) collective-permute-start(s16[4,8,4224]{2,1,0:T(8,128)(2,1)S(1)} %serve.4), channel_id=1, source_target_pairs={{0,4},{4,0},{2,6},{6,2},{8,12},{12,8},{10,14},{14,10},{1,5},{5,1},... | collective-permute-start | bytes 811016 | tf_op jit(solution)/shard_map/ppermute | solution.py:275
  29.5 9.2 %copy-start.9 = (s32[4,8]{1,0:T(4,128)S(1)}, s32[4,8]{1,0:T(4,128)}, u32[]{:S(2)}) copy-start(s32[4,8]{1,0:T(4,128)} %param.15) | copy-start | bytes 388
  29.6 9.1 %copy-start.10 = (s32[1024]{0:T(1024)S(1)}, s32[1024]{0:T(1024)}, u32[]{:S(2)}) copy-start(s32[1024]{0:T(1024)} %param.14) | copy-start | bytes 12292
  29.6 9.4 %copy-start.7 = (s32[64]{0:T(128)S(1)}, s32[64]{0:T(128)}, u32[]{:S(2)}) copy-start(s32[64]{0:T(128)} %ancestors_ref.11) | copy-start | bytes 772
  29.6 9.4 %copy-start.8 = (f32[4096]{0:T(1024)S(1)}, f32[4096]{0:T(1024)}, u32[]{:S(2)}) copy-start(f32[4096]{0:T(1024)} %param.17) | copy-start | bytes 49156
  29.6 9.4 %collective-permute-start.3 = (s16[4,8,4224]{2,1,0:T(8,128)(2,1)S(1)}, s16[4,8,4224]{2,1,0:T(8,128)(2,1)S(1)}, u32[]{:S(2)}, u32[]{:S(2)}) collective-permute-start(s16[4,8,4224]{2,1,0:T(8,128)(2,1)S(1)} %serve.5), channel_id=1, source_target_pairs={{4,8},{8,4},{6,10},{10,6},{5,9},{9,5},{7,11},{11,7},{20,24},{24,20... | collective-permute-start | bytes 811016 | tf_op jit(solution)/shard_map/ppermute | solution.py:275
  41.1 3.9 %collective-permute-start.8 = (f32[4,8]{1,0:T(4,128)S(1)}, f32[4,8]{1,0:T(4,128)S(1)}, u32[]{:S(2)}, u32[]{:S(2)}) collective-permute-start(f32[4,8]{1,0:T(4,128)S(1)} %get-tuple-element.9), channel_id=1, source_target_pairs={{0,1},{1,0},{2,3},{3,2},{4,5},{5,4},{6,7},{7,6},{8,9},{9,8},{10,11... | collective-permute-start | bytes 392 | tf_op jit(solution)/shard_map/ppermute | solution.py:288

commit v2 on v1

--- a/solution.py
+++ b/solution.py
@@ -27,14 +27,18 @@
 SMEM = pltpu.MemorySpace.SMEM
 
 
-def exchanges(length):
+def exchanges(length, cores):
     found = []
     for reach in range(REACH, 0, -1):
         for parity in (0, 1):
-            pairs = []
+            partner = list(range(length))
             for i in range(length - reach):
                 if (i // reach) % 2 == parity:
-                    pairs += [(i, i + reach), (i + reach, i)]
+                    partner[i], partner[i + reach] = i + reach, i
+            pairs = []
+            for i, other in enumerate(partner):
+                turn = 1 if other == i else 0
+                pairs += [(i * cores + c, other * cores + (c + turn) % cores) for c in range(cores)]
             found.append((reach, parity, pairs))
     return found
 
@@ -248,8 +252,9 @@
 ):
     steps, count, width = queries.shape
     lanes = width // HEAD
-    plans = exchanges(length)
-    asked = [lax.ppermute(queries, "particle", pairs) for _, _, pairs in plans]
+    cores = lax.axis_size("tensor")
+    plans = exchanges(length, cores)
+    asked = [lax.ppermute(queries, ("particle", "tensor"), pairs) for _, _, pairs in plans]
     work = 4 * steps * count * width * HEAD
     tail_work = 4 * steps * count * width * count * tail_cache.shape[2]
     local_work = 4 * steps * count * width * (prefix_cache.shape[1] + count * tail_cache.shape[2]) + work
@@ -272,7 +277,7 @@
             [ancestors, question, tail_cache],
             tail_work,
         )
-        answers.append(lax.ppermute(answer, "particle", pairs))
+        answers.append(lax.ppermute(answer, ("particle", "tensor"), pairs))
     attended, partial_value = call(
         functools.partial(combine_kernel, length, [plan[:2] for plan in plans]),
         [
@@ -283,13 +288,14 @@
         [ancestors, local, logs, readout.reshape(1, width)] + answers,
         16 * steps * count * width,
     )
-    other = lax.axis_size("tensor")
-    swap = [(i, (i + 1) % other) for i in range(other)]
-    twist_attn = partial_value + lax.ppermute(partial_value, "tensor", swap)
+    if cores == 2:
+        twist_attn = partial_value + lax.ppermute(partial_value, "tensor", [(0, 1), (1, 0)])
+    else:
+        twist_attn = lax.psum(partial_value, "tensor")
     repeats = jnp.sum(
         (sampled_ids[:, :, None] == prompt_ids[None, None, :]).astype(jnp.int32), axis=-1
     )
-    twists = jnp.take(twist_table, sampled_ids) - 2.0 * repeats.astype(F32) + twist_attn
+    twists = twist_table.at[sampled_ids].get(mode="promise_in_bounds") - 2.0 * repeats.astype(F32) + twist_attn
     return (attended, twists)
 
 

time: 45.8 us -> 40.2 us (0.88)
  starting transfers between devices: 18.1 us -> 11.7 us
  waiting for transfers between devices: 3.24 us -> 4.03 us
    ppermute x9, starting transfers between devices: 18.1 us -> 11.7 us  [the longest x4 5.26 us: on_device(): answers.append(lax.ppermute(answer, ('particle', 'tensor'), pairs))]
    ppermute x9, waiting for transfers between devices: 3.24 us -> 4.03 us  [the longest x4 3.99 us: on_device(): lax.ppermute(queries, ('particle', 'tensor'), pairs)]
  transfers between devices with their start and end apart: 9 -> 9, of which waited for: 1 -> 2; matrix products, arithmetic and copies ran while one was open for 4% -> 4% of each run, Pallas kernels for 36% -> 41%
where the time goes in v2:
time: 40.2 us; the launch traced here: 39.9 us
  Pallas kernels  18.7 us (47%)
  starting transfers between devices  11.7 us (29%)
  waiting for transfers between devices  4.03 us (10%)
  local copies, waits for them, and re-layouts  3.17 us (8%)
  other arithmetic  1.5 us (4%)
  between operations  0.82 us (2%)
    pallas_call x6, Pallas kernels, call(): pl.pallas_call(kernel, out_shape=tuple(outs), in_specs=specs, out_specs=t...  18.7 us
    ppermute x4, starting transfers between devices, on_device(): answers.append(lax.ppermute(answer, ('particle', 'tensor'), pairs))  5.26 us
    ppermute x4, starting transfers between devices, on_device(): lax.ppermute(queries, ('particle', 'tensor'), pairs)  4.01 us
    ppermute x4, waiting for transfers between devices, on_device(): lax.ppermute(queries, ('particle', 'tensor'), pairs)  3.99 us
    ppermute x1, starting transfers between devices, on_device(): lax.ppermute(partial_value, 'tensor', [(0, 1), (1, 0)])  2.42 us
    unnamed x22, local copies, waits for them, and re-layouts  2.31 us
  transfers between devices with their start and end apart: 9, of which 2 were waited for; matrix products, arithmetic and copies ran while one was open for 4% of the time, Pallas kernels for 41%

profile of v2, /device:TPU:9, one launch (start us, length us, event | category | flops | bytes accessed | tf_op | source)
XLA Modules:
  0.0 39.9 jit_solution(4068751552542502156)
XLA Ops:
  0.6 1.3 %collective-permute-start.4 = (bf16[4,8,4096]{2,1,0:T(8,128)(2,1)}, bf16[4,8,4096]{2,1,0:T(8,128)(2,1)S(1)}, u32[]{:S(2)}, u32[]{:S(2)}) collective-permute-start(bf16[4,8,4096]{2,1,0:T(8,128)(2,1)} %query_ref.1), channel_id=1, source_target_pairs={{0,2},{1,3},{2,0},{3,1},{4,6},{5,7},{6,4},{7,5},{8,10},{9,11},{10,... | collective-permute-start | bytes 786440 | tf_op jit(solution)/shard_map/ppermute | solution.py:257
  1.9 1.3 %collective-permute-start.2 = (bf16[4,8,4096]{2,1,0:T(8,128)(2,1)}, bf16[4,8,4096]{2,1,0:T(8,128)(2,1)S(1)}, u32[]{:S(2)}, u32[]{:S(2)}) collective-permute-start(bf16[4,8,4096]{2,1,0:T(8,128)(2,1)} %query_ref.1), channel_id=1, source_target_pairs={{0,1},{1,0},{2,3},{3,2},{4,8},{5,9},{6,10},{7,11},{8,4},{9,5},{10,... | collective-permute-start | bytes 786440 | tf_op jit(solution)/shard_map/ppermute | solution.py:257
  3.2 1.4 %collective-permute-start.6 = (bf16[4,8,4096]{2,1,0:T(8,128)(2,1)}, bf16[4,8,4096]{2,1,0:T(8,128)(2,1)S(1)}, u32[]{:S(2)}, u32[]{:S(2)}) collective-permute-start(bf16[4,8,4096]{2,1,0:T(8,128)(2,1)} %query_ref.1), channel_id=1, source_target_pairs={{0,1},{1,0},{2,4},{3,5},{4,2},{5,3},{6,8},{7,9},{8,6},{9,7},{10,12... | collective-permute-start | bytes 786440 | tf_op jit(solution)/shard_map/ppermute | solution.py:257
  4.7 0.7 %compare_select_fusion = s32[4,8]{1,0:T(4,128)S(1)} fusion(s32[4,8]{1,0:T(4,128)} %param.15), kind=kLoop, calls=%fused_computation.2 | loop fusion | flops 96 | bytes 256 | tf_op jit(solution)/shard_map/select_n | solution.py:298
  5.3 2.8 %collective-permute-done.4.query_ref = bf16[4,8,4096]{2,1,0:T(8,128)(2,1)S(1)} collective-permute-done((bf16[4,8,4096]{2,1,0:T(8,128)(2,1)}, bf16[4,8,4096]{2,1,0:T(8,128)(2,1)S(1)}, u32[]{:S(2)}, u32[]{:S(2)}) %collective-permute-start.4) | collective-permute-done | bytes 262176 | tf_op jit(solution)/shard_map/ppermute | solution.py:257
  8.1 1.6 %copy-done.1 = bf16[2,8,128,512]{3,2,1,0:T(8,128)(2,1)S(1)} copy-done((bf16[2,8,128,512]{3,2,1,0:T(8,128)(2,1)S(1)}, bf16[2,8,128,512]{3,2,1,0:T(8,128)(2,1)}, u32[]{:S(2)}) %copy-start.1) | copy-done | bytes 2097176
  9.7 0.7 %copy-done.6 = s32[64]{0:T(128)S(1)} copy-done((s32[64]{0:T(128)S(1)}, s32[64]{0:T(128)}, u32[]{:S(2)}) %copy-start.6) | copy-done | bytes 280
  10.4 2.8 %serve.6 = s16[4,8,4224]{2,1,0:T(8,128)(2,1)S(1)} custom-call(s32[64]{0:T(128)S(1)} %copy-done.6, bf16[4,8,4096]{2,1,0:T(8,128)(2,1)S(1)} %collective-permute-done.4.query_ref, bf16[2,8,128,512]{3,2,1,0:T(8,128)(2,1)S(1)} %copy-done.1), custom_call_target="tpu_custom_call" | custom-call | flops 536870912 | bytes 2629888 | tf_op jit(solution)/shard_map/serve/pallas_call | solution.py:230
  13.2 1.3 %collective-permute-start.5 = (s16[4,8,4224]{2,1,0:T(8,128)(2,1)S(1)}, s16[4,8,4224]{2,1,0:T(8,128)(2,1)S(1)}, u32[]{:S(2)}, u32[]{:S(2)}) collective-permute-start(s16[4,8,4224]{2,1,0:T(8,128)(2,1)S(1)} %serve.6), channel_id=1, source_target_pairs={{0,2},{1,3},{2,0},{3,1},{4,6},{5,7},{6,4},{7,5},{8,10},{9,11},{10,... | collective-permute-start | bytes 811016 | tf_op jit(solution)/shard_map/ppermute | solution.py:280
  14.4 1.2 %collective-permute-done.6.query_ref = bf16[4,8,4096]{2,1,0:T(8,128)(2,1)S(1)} collective-permute-done((bf16[4,8,4096]{2,1,0:T(8,128)(2,1)}, bf16[4,8,4096]{2,1,0:T(8,128)(2,1)S(1)}, u32[]{:S(2)}, u32[]{:S(2)}) %collective-permute-start.6) | collective-permute-done | bytes 262176 | tf_op jit(solution)/shard_map/ppermute | solution.py:257
  15.6 2.8 %serve.7 = s16[4,8,4224]{2,1,0:T(8,128)(2,1)S(1)} custom-call(s32[64]{0:T(128)S(1)} %copy-done.6, bf16[4,8,4096]{2,1,0:T(8,128)(2,1)S(1)} %collective-permute-done.6.query_ref, bf16[2,8,128,512]{3,2,1,0:T(8,128)(2,1)S(1)} %copy-done.1), custom_call_target="tpu_custom_call" | custom-call | flops 536870912 | bytes 2629888 | tf_op jit(solution)/shard_map/serve/pallas_call | solution.py:230
  18.5 1.3 %collective-permute-start.7 = (s16[4,8,4224]{2,1,0:T(8,128)(2,1)S(1)}, s16[4,8,4224]{2,1,0:T(8,128)(2,1)S(1)}, u32[]{:S(2)}, u32[]{:S(2)}) collective-permute-start(s16[4,8,4224]{2,1,0:T(8,128)(2,1)S(1)} %serve.7), channel_id=1, source_target_pairs={{0,1},{1,0},{2,4},{3,5},{4,2},{5,3},{6,8},{7,9},{8,6},{9,7},{10,12... | collective-permute-start | bytes 811016 | tf_op jit(solution)/shard_map/ppermute | solution.py:280
  19.8 2.8 %serve.4 = s16[4,8,4224]{2,1,0:T(8,128)(2,1)S(1)} custom-call(s32[64]{0:T(128)S(1)} %copy-done.6, bf16[4,8,4096]{2,1,0:T(8,128)(2,1)S(1)} %collective-permute-done.query_ref, bf16[2,8,128,512]{3,2,1,0:T(8,128)(2,1)S(1)} %copy-done.1), custom_call_target="tpu_custom_call" | custom-call | flops 536870912 | bytes 2629888 | tf_op jit(solution)/shard_map/serve/pallas_call | solution.py:230
  22.6 0.1 collective-permute-start.1
  22.7 2.8 %serve.5 = s16[4,8,4224]{2,1,0:T(8,128)(2,1)S(1)} custom-call(s32[64]{0:T(128)S(1)} %copy-done.6, bf16[4,8,4096]{2,1,0:T(8,128)(2,1)S(1)} %collective-permute-done.2.query_ref, bf16[2,8,128,512]{3,2,1,0:T(8,128)(2,1)S(1)} %copy-done.1), custom_call_target="tpu_custom_call" | custom-call | flops 536870912 | bytes 2629888 | tf_op jit(solution)/shard_map/serve/pallas_call | solution.py:230
  25.5 2.6 %collective-permute-start.3 = (s16[4,8,4224]{2,1,0:T(8,128)(2,1)S(1)}, s16[4,8,4224]{2,1,0:T(8,128)(2,1)S(1)}, u32[]{:S(2)}, u32[]{:S(2)}) collective-permute-start(s16[4,8,4224]{2,1,0:T(8,128)(2,1)S(1)} %serve.5), channel_id=1, source_target_pairs={{0,1},{1,0},{2,3},{3,2},{4,8},{5,9},{6,10},{7,11},{8,4},{9,5},{10,... | collective-permute-start | bytes 811016 | tf_op jit(solution)/shard_map/ppermute | solution.py:280
  28.1 5.4 %local.1 = (f32[4,8,4096]{2,1,0:T(8,128)S(1)}, f32[4,8,128]{2,1,0:T(8,128)S(1)}) custom-call(s32[64]{0:T(128)S(1)} %copy-done.6, bf16[4,8,4096]{2,1,0:T(8,128)(2,1)S(1)} %copy-done.4, bf16[2,1024,512]{2,1,0:T(8,128)(2,1)S(1)} %copy-done.3, bf16[2,8,128,512]{3,2,1,0:T(8,128)(2,1)S(1)} %copy-done.2, bf16[2,4,8,512]{3,2,1,0:T(8,128)(2,1)S(1)} %copy-done.5), custom_call_target="tpu_custom_call" | custom-call | flops 1140850688 | bytes 5062912 | tf_op jit(solution)/shard_map/local/pallas_call | solution.py:230
  33.6 0.1 reshape.12
  33.7 0.2 convert_reduce_fusion
  33.9 2.1 %combine.1 = (bf16[4,8,4096]{2,1,0:T(8,128)(2,1)}, f32[4,8]{1,0:T(4,128)S(1)}) custom-call(s32[64]{0:T(128)S(1)} %copy-done.7, f32[4,8,4096]{2,1,0:T(8,128)S(1)} %get-tuple-element.6.local_ref, f32[4,8,128]{2,1,0:T(8,128)S(1)} %get-tuple-element.7.log_ref, f32[1,4096]{1,0:T(1,128)S(1)} %bitcast.1, s16[4,8,4224]{2,1,0:T(8,128)(2,1)S(1)} %collective-permute-done.1.refs_0_, ...), custom_call_target="tpu_custom_call" | custom-call | flops 2097152 | bytes 1900928 | tf_op jit(solution)/shard_map/combine/pallas_call | solution.py:230
  36.1 2.4 %collective-permute-start.8 = (f32[4,8]{1,0:T(4,128)S(1)}, f32[4,8]{1,0:T(4,128)S(1)}, u32[]{:S(2)}, u32[]{:S(2)}) collective-permute-start(f32[4,8]{1,0:T(4,128)S(1)} %get-tuple-element.9), channel_id=1, source_target_pairs={{0,1},{1,0},{2,3},{3,2},{4,5},{5,4},{6,7},{7,6},{8,9},{9,8},{10,11... | collective-permute-start | bytes 392 | tf_op jit(solution)/shard_map/ppermute | solution.py:292
  38.5 0.7 %gather_fusion = f32[32]{0:T(128)S(1)} fusion(f32[128256]{0:T(1024)S(1)} %copy-done, s32[1024]{0:T(1024)S(1)} %pad_clamp_fusion), kind=kCustom, calls=%fused_computation | custom fusion | bytes 384 | tf_op jit(solution)/shard_map/gather | solution.py:298
  39.2 0.1 reshape.11
  39.3 0.6 %add_add_fusion = f32[4,8]{1,0:T(4,128)} fusion(f32[4,8]{1,0:T(4,128)S(1)} %get-tuple-element.9, f32[4,8]{1,0:T(4,128)S(1)} %collective-permute-done.8, f32[4,8]{1,0:T(4,128)S(1)} %reshape.11, s32[4,8]{1,0:T(4,128)S(1)} %convert_reduce_fusion), kind=kLoop, calls=%fused_computation.4 | loop fusion | flops 160 | bytes 640 | tf_op jit(solution)/shard_map/add | solution.py:298
  (29 shorter events, 0.1 us)
Async XLA Ops:
  0.6 37.8 %copy-start = (f32[128256]{0:T(1024)S(1)}, f32[128256]{0:T(1024)}, u32[]{:S(2)}) copy-start(f32[128256]{0:T(1024)} %param.16) | copy-start | bytes 1539076
  0.6 7.5 %collective-permute-start.4 = (bf16[4,8,4096]{2,1,0:T(8,128)(2,1)}, bf16[4,8,4096]{2,1,0:T(8,128)(2,1)S(1)}, u32[]{:S(2)}, u32[]{:S(2)}) collective-permute-start(bf16[4,8,4096]{2,1,0:T(8,128)(2,1)} %query_ref.1), channel_id=1, source_target_pairs={{0,2},{1,3},{2,0},{3,1},{4,6},{5,7},{6,4},{7,5},{8,10},{9,11},{10,... | collective-permute-start | bytes 786440 | tf_op jit(solution)/shard_map/ppermute | solution.py:257
  1.9 20.8 %collective-permute-start.2 = (bf16[4,8,4096]{2,1,0:T(8,128)(2,1)}, bf16[4,8,4096]{2,1,0:T(8,128)(2,1)S(1)}, u32[]{:S(2)}, u32[]{:S(2)}) collective-permute-start(bf16[4,8,4096]{2,1,0:T(8,128)(2,1)} %query_ref.1), channel_id=1, source_target_pairs={{0,1},{1,0},{2,3},{3,2},{4,8},{5,9},{6,10},{7,11},{8,4},{9,5},{10,... | collective-permute-start | bytes 786440 | tf_op jit(solution)/shard_map/ppermute | solution.py:257
  3.2 16.6 %collective-permute-start = (bf16[4,8,4096]{2,1,0:T(8,128)(2,1)}, bf16[4,8,4096]{2,1,0:T(8,128)(2,1)S(1)}, u32[]{:S(2)}, u32[]{:S(2)}) collective-permute-start(bf16[4,8,4096]{2,1,0:T(8,128)(2,1)} %query_ref.1), channel_id=1, source_target_pairs={{0,4},{1,5},{2,6},{3,7},{4,0},{5,1},{6,2},{7,3},{8,12},{9,13},{10,... | collective-permute-start | bytes 786440 | tf_op jit(solution)/shard_map/ppermute | solution.py:257
  3.2 12.4 %collective-permute-start.6 = (bf16[4,8,4096]{2,1,0:T(8,128)(2,1)}, bf16[4,8,4096]{2,1,0:T(8,128)(2,1)S(1)}, u32[]{:S(2)}, u32[]{:S(2)}) collective-permute-start(bf16[4,8,4096]{2,1,0:T(8,128)(2,1)} %query_ref.1), channel_id=1, source_target_pairs={{0,1},{1,0},{2,4},{3,5},{4,2},{5,3},{6,8},{7,9},{8,6},{9,7},{10,12... | collective-permute-start | bytes 786440 | tf_op jit(solution)/shard_map/ppermute | solution.py:257
  8.1 1.6 %copy-start.1 = (bf16[2,8,128,512]{3,2,1,0:T(8,128)(2,1)S(1)}, bf16[2,8,128,512]{3,2,1,0:T(8,128)(2,1)}, u32[]{:S(2)}) copy-start(bf16[2,8,128,512]{3,2,1,0:T(8,128)(2,1)} %tail_ref.9) | copy-start | bytes 6291460
  9.7 0.7 %copy-start.6 = (s32[64]{0:T(128)S(1)}, s32[64]{0:T(128)}, u32[]{:S(2)}) copy-start(s32[64]{0:T(128)} %ancestors_ref.11) | copy-start | bytes 772
  13.2 20.7 %collective-permute-start.5 = (s16[4,8,4224]{2,1,0:T(8,128)(2,1)S(1)}, s16[4,8,4224]{2,1,0:T(8,128)(2,1)S(1)}, u32[]{:S(2)}, u32[]{:S(2)}) collective-permute-start(s16[4,8,4224]{2,1,0:T(8,128)(2,1)S(1)} %serve.6), channel_id=1, source_target_pairs={{0,2},{1,3},{2,0},{3,1},{4,6},{5,7},{6,4},{7,5},{8,10},{9,11},{10,... | collective-permute-start | bytes 811016 | tf_op jit(solution)/shard_map/ppermute | solution.py:280
  18.4 9.7 %copy-start.2 = (bf16[2,8,128,512]{3,2,1,0:T(8,128)(2,1)S(1)}, bf16[2,8,128,512]{3,2,1,0:T(8,128)(2,1)}, u32[]{:S(2)}) copy-start(bf16[2,8,128,512]{3,2,1,0:T(8,128)(2,1)} %tail_ref.9) | copy-start | bytes 6291460
  18.4 9.7 %copy-start.3 = (bf16[2,1024,512]{2,1,0:T(8,128)(2,1)S(1)}, bf16[2,1024,512]{2,1,0:T(8,128)(2,1)}, u32[]{:S(2)}) copy-start(bf16[2,1024,512]{2,1,0:T(8,128)(2,1)} %prefix_ref.1) | copy-start | bytes 6291460
  18.5 9.7 %copy-start.4 = (bf16[4,8,4096]{2,1,0:T(8,128)(2,1)S(1)}, bf16[4,8,4096]{2,1,0:T(8,128)(2,1)}, u32[]{:S(2)}) copy-start(bf16[4,8,4096]{2,1,0:T(8,128)(2,1)} %query_ref.1) | copy-start | bytes 786436
  18.5 9.7 %copy-start.5 = (bf16[2,4,8,512]{3,2,1,0:T(8,128)(2,1)S(1)}, bf16[2,4,8,512]{3,2,1,0:T(8,128)(2,1)}, u32[]{:S(2)}) copy-start(bf16[2,4,8,512]{3,2,1,0:T(8,128)(2,1)} %fresh_ref.1) | copy-start | bytes 196612
  18.5 15.4 %collective-permute-start.7 = (s16[4,8,4224]{2,1,0:T(8,128)(2,1)S(1)}, s16[4,8,4224]{2,1,0:T(8,128)(2,1)S(1)}, u32[]{:S(2)}, u32[]{:S(2)}) collective-permute-start(s16[4,8,4224]{2,1,0:T(8,128)(2,1)S(1)} %serve.7), channel_id=1, source_target_pairs={{0,1},{1,0},{2,4},{3,5},{4,2},{5,3},{6,8},{7,9},{8,6},{9,7},{10,12... | collective-permute-start | bytes 811016 | tf_op jit(solution)/shard_map/ppermute | solution.py:280
  22.6 11.3 %collective-permute-start.1 = (s16[4,8,4224]{2,1,0:T(8,128)(2,1)S(1)}, s16[4,8,4224]{2,1,0:T(8,128)(2,1)S(1)}, u32[]{:S(2)}, u32[]{:S(2)}) collective-permute-start(s16[4,8,4224]{2,1,0:T(8,128)(2,1)S(1)} %serve.4), channel_id=1, source_target_pairs={{0,4},{1,5},{2,6},{3,7},{4,0},{5,1},{6,2},{7,3},{8,12},{9,13},{10,... | collective-permute-start | bytes 811016 | tf_op jit(solution)/shard_map/ppermute | solution.py:280
  25.5 8.2 %copy-start.9 = (s32[4,8]{1,0:T(4,128)S(1)}, s32[4,8]{1,0:T(4,128)}, u32[]{:S(2)}) copy-start(s32[4,8]{1,0:T(4,128)} %param.15) | copy-start | bytes 388
  25.5 8.2 %copy-start.10 = (s32[1024]{0:T(1024)S(1)}, s32[1024]{0:T(1024)}, u32[]{:S(2)}) copy-start(s32[1024]{0:T(1024)} %param.14) | copy-start | bytes 12292
  25.5 8.4 %copy-start.7 = (s32[64]{0:T(128)S(1)}, s32[64]{0:T(128)}, u32[]{:S(2)}) copy-start(s32[64]{0:T(128)} %ancestors_ref.11) | copy-start | bytes 772
  25.5 8.4 %copy-start.8 = (f32[4096]{0:T(1024)S(1)}, f32[4096]{0:T(1024)}, u32[]{:S(2)}) copy-start(f32[4096]{0:T(1024)} %param.17) | copy-start | bytes 49156
  25.5 8.4 %collective-permute-start.3 = (s16[4,8,4224]{2,1,0:T(8,128)(2,1)S(1)}, s16[4,8,4224]{2,1,0:T(8,128)(2,1)S(1)}, u32[]{:S(2)}, u32[]{:S(2)}) collective-permute-start(s16[4,8,4224]{2,1,0:T(8,128)(2,1)S(1)} %serve.5), channel_id=1, source_target_pairs={{0,1},{1,0},{2,3},{3,2},{4,8},{5,9},{6,10},{7,11},{8,4},{9,5},{10,... | collective-permute-start | bytes 811016 | tf_op jit(solution)/shard_map/ppermute | solution.py:280
  36.1 3.2 %collective-permute-start.8 = (f32[4,8]{1,0:T(4,128)S(1)}, f32[4,8]{1,0:T(4,128)S(1)}, u32[]{:S(2)}, u32[]{:S(2)}) collective-permute-start(f32[4,8]{1,0:T(4,128)S(1)} %get-tuple-element.9), channel_id=1, source_target_pairs={{0,1},{1,0},{2,3},{3,2},{4,5},{5,4},{6,7},{7,6},{8,9},{9,8},{10,11... | collective-permute-start | bytes 392 | tf_op jit(solution)/shard_map/ppermute | solution.py:292

commit v3 on v2

v3 whole, which is shorter than its diff:
```python
import functools
import math

import jax
import jax.numpy as jnp
from jax import lax
from jax.experimental import pallas as pl
from jax.experimental.pallas import tpu as pltpu
from jax.sharding import PartitionSpec as P

HEADS = 64
KV_HEADS = 8
HEAD = 128
REACH = 2
GROUP = HEADS // KV_HEADS
EXPONENT_SCALE = math.log2(math.e) / math.sqrt(HEAD)

NEG_FILL = -1e30
LOG_STEPS = 32.0
LOG_FRACTION = 65534.0
TOP_CODE = 32000.0
TINY = 1e-30
LANES = 128

F32 = jnp.float32
BF16 = jnp.bfloat16
VMEM = pltpu.MemorySpace.VMEM
SMEM = pltpu.MemorySpace.SMEM


def exchanges(length, cores):
    found = []
    for reach in range(REACH, 0, -1):
        for parity in (0, 1):
            partner = list(range(length))
            for i in range(length - reach):
                if (i // reach) % 2 == parity:
                    partner[i], partner[i + reach] = i + reach, i
            pairs = []
            for i, other in enumerate(partner):
                turn = 1 if other == i else 0
                pairs += [(i * cores + c, other * cores + (c + turn) % cores) for c in range(cores)]
            found.append((reach, parity, pairs))
    return found


def partner_of(index, reach, parity):
    return jnp.where((index // reach) % 2 == parity, index + reach, index - reach)


def held_by(ancestors_ref, owner, holder, length, count):
    safe = jnp.clip(owner, 0, length - 1)
    exists = safe == owner
    found = []
    for p in range(count):
        slot = ancestors_ref[safe * count + p] - holder * count
        found.append((exists & (slot >= 0) & (slot < count), jnp.clip(slot, 0, count - 1)))
    return found


def head_tiles(query_ref, base):
    return [
        query_ref[t, :, base + g * HEAD : base + (g + 1) * HEAD].astype(F32)
        for t in range(query_ref.shape[0])
        for g in range(GROUP)
    ]


def scores_of(rows, keys):
    return lax.dot_general(rows, keys, (((1,), (1,)), ((), ())), preferred_element_type=F32)


def softmax_terms(scores):
    top = jnp.max(scores, axis=-1, keepdims=True)
    expo = jnp.exp2((scores - top) * EXPONENT_SCALE)
    return top, expo, jnp.sum(expo, axis=-1, keepdims=True)


def two_codes(value):
    value = value * LOG_STEPS
    whole = jnp.round(value)
    return whole, jnp.round((value - whole) * LOG_FRACTION)


def from_codes(whole, part):
    return (whole + part * (1.0 / LOG_FRACTION)) * (1.0 / LOG_STEPS)


def serve(slots, query_ref, tail_ref, out_ref):
    steps, count = query_ref.shape[0], query_ref.shape[1]
    heads = tail_ref.shape[3] // HEAD
    many = steps * GROUP
    each = heads * many
    lane = lax.broadcasted_iota(jnp.int32, (GROUP, LANES), 1)
    row = lax.broadcasted_iota(jnp.int32, (GROUP, LANES), 0)
    notes = [[jnp.zeros((GROUP, LANES), F32) for _ in range(count)] for _ in range(3)]
    scores = []
    for k in range(heads):
        tiles = jnp.stack(head_tiles(query_ref, k * GROUP * HEAD), axis=0)
        rows = jnp.swapaxes(tiles, 0, 1).astype(BF16)
        cols = slice(k * HEAD, (k + 1) * HEAD)
        scores += [scores_of(rows[p], tail_ref[0, slots[p], :, cols]) for p in range(count)]
    terms = [softmax_terms(score) for score in scores]
    outs = [
        jnp.dot(
            terms[k * count + p][1].astype(BF16),
            tail_ref[1, slots[p], :, k * HEAD : (k + 1) * HEAD],
            preferred_element_type=F32,
        )
        for k in range(heads)
        for p in range(count)
    ]
    for k in range(heads):
        for p in range(count):
            top, _, total = terms[k * count + p]
            out = outs[k * count + p]
            largest = jnp.maximum(jnp.max(jnp.abs(out), axis=-1, keepdims=True), TINY)
            code = jnp.round(out * (TOP_CODE / largest)).astype(jnp.int32)
            at = p * each + k * many
            out_ref[at : at + many, :] = code.astype(jnp.int16)
            for t in range(steps):
                here = lane == row + (k * many + t * GROUP)
                part = slice(t * GROUP, (t + 1) * GROUP)
                for note, column in zip(notes, (top, total, largest)):
                    note[p] = jnp.where(here, column[part], note[p])
    top, total, largest = (
        jnp.concatenate([jnp.sum(n, axis=0, keepdims=True) for n in note], axis=0) for note in notes
    )
    if each < LANES:
        total, largest = jnp.maximum(total, TINY), jnp.maximum(largest, TINY)
    spread = jnp.log2(total)
    level = two_codes(top * EXPONENT_SCALE + spread)
    scale = two_codes(jnp.log2(largest) - spread - math.log2(TOP_CODE))
    coded = jnp.concatenate(level + scale, axis=0).astype(jnp.int32)
    out_ref[count * each :, :] = coded.astype(jnp.int16)


def serve_kernel(length, reach, parity, ancestors_ref, query_ref, tail_ref, out_ref):
    count = query_ref.shape[1]
    me = lax.axis_index("particle")
    found = held_by(ancestors_ref, partner_of(me, reach, parity), me, length, count)
    serve([slot for _, slot in found], query_ref, tail_ref, out_ref)


def serve_own_kernel(length, ancestors_ref, query_ref, tail_ref, out_ref, held_ref, sem):
    copy = pltpu.make_async_copy(tail_ref, held_ref, sem)
    copy.start()
    count = query_ref.shape[1]
    me = lax.axis_index("particle")
    found = held_by(ancestors_ref, me, me, length, count)
    copy.wait()
    serve([slot for _, slot in found], query_ref, held_ref, out_ref)


def local_kernel(query_ref, prefix_ref, fresh_ref, out_ref, log_ref):
    steps, count = query_ref.shape[0], query_ref.shape[1]
    heads = prefix_ref.shape[2] // HEAD
    many = steps * GROUP
    lane = lax.broadcasted_iota(jnp.int32, (count, LANES), 1)
    logs = []
    for k in range(heads):
        cols = slice(k * HEAD, (k + 1) * HEAD)
        rows = jnp.concatenate(head_tiles(query_ref, k * GROUP * HEAD), axis=0).astype(BF16)
        top1, expo1, total1 = softmax_terms(scores_of(rows, prefix_ref[0, :, cols]))
        out1 = jnp.dot(expo1.astype(BF16), prefix_ref[1, :, cols], preferred_element_type=F32)
        fresh_keys = jnp.concatenate([fresh_ref[0, s, :, cols].astype(F32) for s in range(steps)], axis=0)
        fresh_values = jnp.concatenate([fresh_ref[1, s, :, cols].astype(F32) for s in range(steps)], axis=0)
        scores2 = scores_of(rows, fresh_keys.astype(BF16))
        row = lax.broadcasted_iota(jnp.int32, scores2.shape, 0)
        col = lax.broadcasted_iota(jnp.int32, scores2.shape, 1)
        seen = (row % count == col % count) & (col // count <= row // (GROUP * count))
        top2, expo2, total2 = softmax_terms(jnp.where(seen, scores2, NEG_FILL))
        out2 = jnp.dot(expo2.astype(BF16), fresh_values.astype(BF16), preferred_element_type=F32)
        top = jnp.maximum(top1, top2)
        share1 = jnp.exp2((top1 - top) * EXPONENT_SCALE)
        share2 = jnp.exp2((top2 - top) * EXPONENT_SCALE)
        total = share1 * total1 + share2 * total2
        context = (share1 * out1 + share2 * out2) / total
        context = context.reshape(many, count, HEAD)
        top, total = top.reshape(many, count, 1), total.reshape(many, count, 1)
        held = [jnp.zeros((count, LANES), F32) for _ in range(2)]
        for t in range(steps):
            for g in range(GROUP):
                at = (k * GROUP + g) * HEAD
                r = t * GROUP + g
                out_ref[t, :, at : at + HEAD] = context[r]
                held[0] = jnp.where(lane == k * many + r, top[r], held[0])
                held[1] = jnp.where(lane == k * many + r, total[r], held[1])
        inside = (lane >= k * many) & (lane < (k + 1) * many)
        level = held[0] * EXPONENT_SCALE + jnp.log2(jnp.where(inside, held[1], 1.0))
        logs.append(level)
    log_ref[...] = functools.reduce(jnp.add, logs)


def combine_kernel(length, plans, ancestors_ref, local_ref, log_ref, readout_ref, *refs):
    sent_refs, (out_ref, twist_ref) = refs[: len(plans) + 1], refs[len(plans) + 1 :]
    steps, count = local_ref.shape[0], local_ref.shape[1]
    heads = local_ref.shape[2] // (HEAD * GROUP)
    many = steps * GROUP
    each = heads * many
    me = lax.axis_index("particle")
    source = [jnp.int32(0)] * count
    for m, (reach, parity) in enumerate(plans):
        found = held_by(ancestors_ref, me, partner_of(me, reach, parity), length, count)
        source = [jnp.where(here, m + 1, old) for (here, _), old in zip(found, source)]
    row = lax.broadcasted_iota(jnp.int32, (count, LANES), 0)
    lane = lax.broadcasted_iota(jnp.int32, (count, LANES), 1)

    def notes_of(ref):
        notes = ref[count * each :, :].astype(jnp.int32).astype(F32)
        return [notes[i * count : (i + 1) * count] for i in range(4)]

    sources = jnp.zeros((count, LANES), jnp.int32)
    for p in range(count):
        sources = jnp.where(row == p, source[p], sources)
    notes = notes_of(sent_refs[0])
    for m, ref in enumerate(sent_refs[1:], 1):
        notes = [jnp.where(sources == m, new, old) for new, old in zip(notes_of(ref), notes)]
    remote_level, scale = from_codes(*notes[:2]), from_codes(*notes[2:])
    local_level = log_ref[...]
    level = jnp.maximum(local_level, remote_level)
    local_share = jnp.exp2(local_level - level)
    remote_share = jnp.exp2(remote_level - level)
    total = local_share + remote_share
    local_share = local_share / total
    remote_share = remote_share / total * jnp.exp2(scale)
    gathered = [jnp.zeros((count, HEAD), F32) for _ in range(steps)]
    for k in range(heads):
        for pair in range(steps // 2):
            at = k * many + pair * 2 * GROUP
            picked = []
            for p in range(count):
                here = slice(p * each + at, p * each + at + 2 * GROUP)
                code = sent_refs[0][here, :]
                for m, ref in enumerate(sent_refs[1:], 1):
                    code = jnp.where(source[p] == m, ref[here, :], code)
                picked.append(code.astype(jnp.int32).astype(F32))
            tiles = jnp.swapaxes(jnp.stack(picked, axis=0), 0, 1)
            for r in range(2 * GROUP):
                t, h = pair * 2 + r // GROUP, k * GROUP + r % GROUP
                cols = slice(h * HEAD, (h + 1) * HEAD)
                context = local_share[:, at + r : at + r + 1] * local_ref[t, :, cols]
                context = context + remote_share[:, at + r : at + r + 1] * tiles[r]
                out_ref[t, :, cols] = context.astype(BF16)
                gathered[t] = gathered[t] + context * readout_ref[:, cols]
    for t in range(steps):
        column = jnp.sum(gathered[t], axis=-1, keepdims=True)
        line = jnp.sum(jnp.where(row == lane, column, 0.0), axis=0, keepdims=True)
        twist_ref[t : t + 1, :] = line[:, :count]


def call(kernel, outs, name, operands, flops, spaces=None, scratch=(), limit=24 << 20):
    moved = sum(math.prod(o.shape) * o.dtype.itemsize for o in operands)
    moved += sum(math.prod(o.shape) * o.dtype.itemsize for o in outs)
    spaces = spaces or [SMEM] + [VMEM] * (len(operands) - 1)
    return pl.pallas_call(
        kernel,
        out_shape=tuple(outs),
        in_specs=[pl.BlockSpec(memory_space=space) for space in spaces],
        out_specs=tuple(pl.BlockSpec(memory_space=VMEM) for _ in outs),
        scratch_shapes=scratch,
        compiler_params=pltpu.CompilerParams(vmem_limit_bytes=limit),
        cost_estimate=pl.CostEstimate(flops=flops, bytes_accessed=moved, transcendentals=0),
        name=name,
    )(*operands)


def on_device(
    length,
    prefix_cache,
    tail_cache,
    ancestors,
    queries,
    fresh_kv,
    prompt_ids,
    sampled_ids,
    twist_table,
    readout,
):
    steps, count, width = queries.shape
    rows = steps * width // HEAD
    assert rows <= LANES and steps % 2 == 0
    cores = lax.axis_size("tensor")
    both = ("particle", "tensor")
    plans = exchanges(length, cores)
    asked = [lax.ppermute(queries, both, pairs) for _, _, pairs in plans]
    reply = jax.ShapeDtypeStruct((count * rows + 4 * count, HEAD), jnp.int16)
    tail_work = 4 * steps * count * width * tail_cache.shape[2]
    local_work = 4 * steps * count * width * prefix_cache.shape[1]
    own, tails = call(
        functools.partial(serve_own_kernel, length),
        [reply, jax.ShapeDtypeStruct(tail_cache.shape, tail_cache.dtype)],
        "own",
        [ancestors, queries, tail_cache],
        tail_work,
        spaces=[SMEM, VMEM, pl.ANY],
        scratch=(pltpu.SemaphoreType.DMA,),
    )
    answers = [own]
    for (reach, parity, pairs), question in zip(plans, asked):
        (answer,) = call(
            functools.partial(serve_kernel, length, reach, parity),
            [reply],
            "serve",
            [ancestors, question, tails],
            tail_work,
        )
        answers.append(lax.ppermute(answer, both, pairs))
    local, logs = call(
        local_kernel,
        [jax.ShapeDtypeStruct(queries.shape, F32), jax.ShapeDtypeStruct((count, LANES), F32)],
        "local",
        [queries, prefix_cache, fresh_kv],
        local_work,
        spaces=[VMEM] * 3,
    )
    attended, partial_value = call(
        functools.partial(combine_kernel, length, [plan[:2] for plan in plans]),
        [jax.ShapeDtypeStruct(queries.shape, BF16), jax.ShapeDtypeStruct((steps, count), F32)],
        "combine",
        [ancestors, local, logs, readout.reshape(1, width)] + answers,
        16 * steps * count * width,
    )
    if cores == 2:
        twist_attn = partial_value + lax.ppermute(partial_value, "tensor", [(0, 1), (1, 0)])
    else:
        twist_attn = lax.psum(partial_value, "tensor")
    repeats = jnp.sum(
        (sampled_ids[:, :, None] == prompt_ids[None, None, :]).astype(jnp.int32), axis=-1
    )
    twists = twist_table.at[sampled_ids].get(mode="promise_in_bounds") - 2.0 * repeats.astype(F32) + twist_attn
    return (attended, twists)


def solution(mesh):
    return jax.shard_map(
        functools.partial(on_device, mesh.shape["particle"]),
        mesh=mesh,
        in_specs=(
            P(None, "groups", "tensor"),
            P(None, ("groups", "particle"), None, "tensor"),
            P("groups"),
            P(None, ("groups", "particle"), "tensor"),
            P(None, None, ("groups", "particle"), "tensor"),
            P("groups"),
            P(None, ("groups", "particle")),
            P(),
            P("tensor"),
        ),
        out_specs=(P(None, ("groups", "particle"), "tensor"), P(None, ("groups", "particle"))),
        check_vma=False,
    )
```

time: 40.2 us -> 37.1 us (0.923)
  the two profiles are of different devices: /device:TPU:9 before, /device:TPU:0 now
where the time goes in v3:
time: 37.1 us; the launch traced here: 36.9 us
  Pallas kernels  13.4 us (36%)
  starting transfers between devices  10.1 us (27%)
  waiting for transfers between devices  6.89 us (19%)
  local copies, waits for them, and re-layouts  4.12 us (11%)
  other arithmetic  1.5 us (4%)
  between operations  0.84 us (2%)
    pallas_call x7, Pallas kernels, call(): pl.pallas_call(kernel, out_shape=tuple(outs), in_specs=[pl.BlockSpec(memo...  13.4 us
    ppermute x4, waiting for transfers between devices, on_device(): answers.append(lax.ppermute(answer, both, pairs))  6.51 us
    ppermute x4, starting transfers between devices, on_device(): answers.append(lax.ppermute(answer, both, pairs))  5.27 us
    ppermute x4, starting transfers between devices, on_device(): asked = [lax.ppermute(queries, both, pairs) for _, _, pairs in plans]  4.84 us
    unnamed x22, local copies, waits for them, and re-layouts  3.25 us
    gather x2, local copies, waits for them, and re-layouts, on_device(): twist_table.at[sampled_ids].get(mode='promise_in_bounds')  0.78 us
  transfers between devices with their start and end apart: 9, of which 2 were waited for; matrix products, arithmetic and copies ran while one was open for 5% of the time, Pallas kernels for 31%

profile of v3, /device:TPU:0, one launch (start us, length us, event | category | flops | bytes accessed | tf_op | source)
XLA Modules:
  0.0 36.9 jit_solution(1189673162262001366)
XLA Ops:
  0.6 3.1 %collective-permute-start = (bf16[4,8,4096]{2,1,0:T(8,128)(2,1)}, bf16[4,8,4096]{2,1,0:T(8,128)(2,1)S(1)}, u32[]{:S(2)}, u32[]{:S(2)}) collective-permute-start(bf16[4,8,4096]{2,1,0:T(8,128)(2,1)} %query_ref.3), channel_id=1, source_target_pairs={{0,4},{1,5},{2,6},{3,7},{4,0},{5,1},{6,2},{7,3},{8,12},{9,13},{10,... | collective-permute-start | bytes 786440 | tf_op jit(solution)/shard_map/ppermute | solution.py:286
  3.8 1.5 %collective-permute-start.4 = (bf16[4,8,4096]{2,1,0:T(8,128)(2,1)}, bf16[4,8,4096]{2,1,0:T(8,128)(2,1)S(1)}, u32[]{:S(2)}, u32[]{:S(2)}) collective-permute-start(bf16[4,8,4096]{2,1,0:T(8,128)(2,1)} %query_ref.3), channel_id=1, source_target_pairs={{0,2},{1,3},{2,0},{3,1},{4,6},{5,7},{6,4},{7,5},{8,10},{9,11},{10,... | collective-permute-start | bytes 786440 | tf_op jit(solution)/shard_map/ppermute | solution.py:286
  5.3 0.2 collective-permute-start.6
  5.5 0.7 %compare_select_fusion = s32[4,8]{1,0:T(4,128)S(1)} fusion(s32[4,8]{1,0:T(4,128)} %param.15), kind=kLoop, calls=%fused_computation.2 | loop fusion | flops 96 | bytes 256 | tf_op jit(solution)/shard_map/select_n | solution.py:331
  6.2 0.1 reshape.12
  6.3 1.6 %copy-done.1 = bf16[2,8,128,512]{3,2,1,0:T(8,128)(2,1)S(1)} copy-done((bf16[2,8,128,512]{3,2,1,0:T(8,128)(2,1)S(1)}, bf16[2,8,128,512]{3,2,1,0:T(8,128)(2,1)}, u32[]{:S(2)}) %copy-start.1) | copy-done | bytes 2097176
  7.8 0.9 %copy-done.3 = bf16[4,8,4096]{2,1,0:T(8,128)(2,1)S(1)} copy-done((bf16[4,8,4096]{2,1,0:T(8,128)(2,1)S(1)}, bf16[4,8,4096]{2,1,0:T(8,128)(2,1)}, u32[]{:S(2)}) %copy-start.3) | copy-done | bytes 262168
  8.8 0.7 %copy-done.6 = s32[64]{0:T(128)S(1)} copy-done((s32[64]{0:T(128)S(1)}, s32[64]{0:T(128)}, u32[]{:S(2)}) %copy-start.6) | copy-done | bytes 280
  9.5 1.8 %own.1 = (s16[1056,128]{1,0:T(8,128)(2,1)S(1)}, bf16[2,8,128,512]{3,2,1,0:T(8,128)(2,1)S(1)}) custom-call(s32[64]{0:T(128)S(1)} %copy-done.6, bf16[4,8,4096]{2,1,0:T(8,128)(2,1)S(1)} %copy-done.3, bf16[2,8,128,512]{3,2,1,0:T(8,128)(2,1)S(1)} %copy-done.1), custom_call_target="tpu_custom_call" | custom-call | flops 67108864 | bytes 4727040 | tf_op jit(solution)/shard_map/own/pallas_call | solution.py:256
  11.3 1.7 %serve.4 = s16[1056,128]{1,0:T(8,128)(2,1)S(1)} custom-call(s32[64]{0:T(128)S(1)} %copy-done.6, bf16[4,8,4096]{2,1,0:T(8,128)(2,1)S(1)} %collective-permute-done.query_ref, bf16[2,8,128,512]{3,2,1,0:T(8,128)(2,1)S(1)} %get-tuple-element.11.tail_ref), custom_call_target="tpu_custom_call" | custom-call | flops 67108864 | bytes 2629888 | tf_op jit(solution)/shard_map/serve/pallas_call | solution.py:256
  12.9 3.0 %collective-permute-start.1 = (s16[1056,128]{1,0:T(8,128)(2,1)S(1)}, s16[1056,128]{1,0:T(8,128)(2,1)S(1)}, u32[]{:S(2)}, u32[]{:S(2)}) collective-permute-start(s16[1056,128]{1,0:T(8,128)(2,1)S(1)} %serve.4), channel_id=1, source_target_pairs={{0,4},{1,5},{2,6},{3,7},{4,0},{5,1},{6,2},{7,3},{8,12},{9,13},{10,... | collective-permute-start | bytes 811016 | tf_op jit(solution)/shard_map/ppermute | solution.py:308
  15.9 1.7 %serve.5 = s16[1056,128]{1,0:T(8,128)(2,1)S(1)} custom-call(s32[64]{0:T(128)S(1)} %copy-done.6, bf16[4,8,4096]{2,1,0:T(8,128)(2,1)S(1)} %collective-permute-done.2.query_ref, bf16[2,8,128,512]{3,2,1,0:T(8,128)(2,1)S(1)} %get-tuple-element.11.tail_ref), custom_call_target="tpu_custom_call" | custom-call | flops 67108864 | bytes 2629888 | tf_op jit(solution)/shard_map/serve/pallas_call | solution.py:256
  17.6 0.1 collective-permute-start.3
  17.7 1.6 %serve.6 = s16[1056,128]{1,0:T(8,128)(2,1)S(1)} custom-call(s32[64]{0:T(128)S(1)} %copy-done.7, bf16[4,8,4096]{2,1,0:T(8,128)(2,1)S(1)} %collective-permute-done.4.query_ref, bf16[2,8,128,512]{3,2,1,0:T(8,128)(2,1)S(1)} %get-tuple-element.11.tail_ref), custom_call_target="tpu_custom_call" | custom-call | flops 67108864 | bytes 2629888 | tf_op jit(solution)/shard_map/serve/pallas_call | solution.py:256
  19.4 2.1 %collective-permute-start.5 = (s16[1056,128]{1,0:T(8,128)(2,1)S(1)}, s16[1056,128]{1,0:T(8,128)(2,1)S(1)}, u32[]{:S(2)}, u32[]{:S(2)}) collective-permute-start(s16[1056,128]{1,0:T(8,128)(2,1)S(1)} %serve.6), channel_id=1, source_target_pairs={{0,2},{1,3},{2,0},{3,1},{4,6},{5,7},{6,4},{7,5},{8,10},{9,11},{10,... | collective-permute-start | bytes 811016 | tf_op jit(solution)/shard_map/ppermute | solution.py:308
  21.6 1.6 %serve.7 = s16[1056,128]{1,0:T(8,128)(2,1)S(1)} custom-call(s32[64]{0:T(128)S(1)} %copy-done.7, bf16[4,8,4096]{2,1,0:T(8,128)(2,1)S(1)} %collective-permute-done.6.query_ref, bf16[2,8,128,512]{3,2,1,0:T(8,128)(2,1)S(1)} %get-tuple-element.11.tail_ref), custom_call_target="tpu_custom_call" | custom-call | flops 67108864 | bytes 2629888 | tf_op jit(solution)/shard_map/serve/pallas_call | solution.py:256
  23.3 3.0 %local.1 = (f32[4,8,4096]{2,1,0:T(8,128)S(1)}, f32[8,128]{1,0:T(8,128)S(1)}) custom-call(bf16[4,8,4096]{2,1,0:T(8,128)(2,1)S(1)} %copy-done.4, bf16[2,1024,512]{2,1,0:T(8,128)(2,1)S(1)} %copy-done.2, bf16[2,4,8,512]{3,2,1,0:T(8,128)(2,1)S(1)} %copy-done.5), custom_call_target="tpu_custom_call" | custom-call | flops 536870912 | bytes 2953216 | tf_op jit(solution)/shard_map/local/pallas_call | solution.py:256
  26.4 0.2 convert_reduce_fusion
  26.6 6.5 %collective-permute-done.5.refs_3_ = s16[1056,128]{1,0:T(8,128)(2,1)S(1)} collective-permute-done((s16[1056,128]{1,0:T(8,128)(2,1)S(1)}, s16[1056,128]{1,0:T(8,128)(2,1)S(1)}, u32[]{:S(2)}, u32[]{:S(2)}) %collective-permute-start.5) | collective-permute-done | bytes 270368 | tf_op jit(solution)/shard_map/ppermute | solution.py:308
  33.2 2.0 %combine.1 = (bf16[4,8,4096]{2,1,0:T(8,128)(2,1)}, f32[4,8]{1,0:T(4,128)S(1)}) custom-call(s32[64]{0:T(128)S(1)} %copy-done.7, f32[4,8,4096]{2,1,0:T(8,128)S(1)} %get-tuple-element.8.local_ref, f32[8,128]{1,0:T(8,128)S(1)} %get-tuple-element.9.log_ref, f32[1,4096]{1,0:T(1,128)S(1)} %bitcast.1, s16[1056,128]{1,0:T(8,128)(2,1)S(1)} %get-tuple-element.10.refs_0_, ...), custom_call_target="tpu_custom_call" | custom-call | flops 2097152 | bytes 2158976 | tf_op jit(solution)/shard_map/combine/pallas_call | solution.py:256
  35.1 0.7 %gather_fusion = f32[32]{0:T(128)S(1)} fusion(f32[128256]{0:T(1024)S(1)} %copy-done, s32[1024]{0:T(1024)S(1)} %pad_clamp_fusion), kind=kCustom, calls=%fused_computation | custom fusion | bytes 384 | tf_op jit(solution)/shard_map/gather | solution.py:331
  35.8 0.1 reshape.11
  35.9 0.4 %collective-permute-done.8 = f32[4,8]{1,0:T(4,128)S(1)} collective-permute-done((f32[4,8]{1,0:T(4,128)S(1)}, f32[4,8]{1,0:T(4,128)S(1)}, u32[]{:S(2)}, u32[]{:S(2)}) %collective-permute-start.8) | collective-permute-done | bytes 160 | tf_op jit(solution)/shard_map/ppermute | solution.py:325
  36.3 0.6 %add_add_fusion = f32[4,8]{1,0:T(4,128)} fusion(f32[4,8]{1,0:T(4,128)S(1)} %get-tuple-element.13, f32[4,8]{1,0:T(4,128)S(1)} %collective-permute-done.8, f32[4,8]{1,0:T(4,128)S(1)} %reshape.11, s32[4,8]{1,0:T(4,128)S(1)} %convert_reduce_fusion), kind=kLoop, calls=%fused_computation.4 | loop fusion | flops 160 | bytes 640 | tf_op jit(solution)/shard_map/add | solution.py:331
  (30 shorter events, 0.2 us)
Async XLA Ops:
  0.6 34.5 %copy-start = (f32[128256]{0:T(1024)S(1)}, f32[128256]{0:T(1024)}, u32[]{:S(2)}) copy-start(f32[128256]{0:T(1024)} %param.16) | copy-start | bytes 1539076
  0.6 10.6 %collective-permute-start = (bf16[4,8,4096]{2,1,0:T(8,128)(2,1)}, bf16[4,8,4096]{2,1,0:T(8,128)(2,1)S(1)}, u32[]{:S(2)}, u32[]{:S(2)}) collective-permute-start(bf16[4,8,4096]{2,1,0:T(8,128)(2,1)} %query_ref.3), channel_id=1, source_target_pairs={{0,4},{1,5},{2,6},{3,7},{4,0},{5,1},{6,2},{7,3},{8,12},{9,13},{10,... | collective-permute-start | bytes 786440 | tf_op jit(solution)/shard_map/ppermute | solution.py:286
  3.8 12.2 %collective-permute-start.2 = (bf16[4,8,4096]{2,1,0:T(8,128)(2,1)}, bf16[4,8,4096]{2,1,0:T(8,128)(2,1)S(1)}, u32[]{:S(2)}, u32[]{:S(2)}) collective-permute-start(bf16[4,8,4096]{2,1,0:T(8,128)(2,1)} %query_ref.3), channel_id=1, source_target_pairs={{0,1},{1,0},{2,3},{3,2},{4,8},{5,9},{6,10},{7,11},{8,4},{9,5},{10,... | collective-permute-start | bytes 786440 | tf_op jit(solution)/shard_map/ppermute | solution.py:286
  3.8 14.0 %collective-permute-start.4 = (bf16[4,8,4096]{2,1,0:T(8,128)(2,1)}, bf16[4,8,4096]{2,1,0:T(8,128)(2,1)S(1)}, u32[]{:S(2)}, u32[]{:S(2)}) collective-permute-start(bf16[4,8,4096]{2,1,0:T(8,128)(2,1)} %query_ref.3), channel_id=1, source_target_pairs={{0,2},{1,3},{2,0},{3,1},{4,6},{5,7},{6,4},{7,5},{8,10},{9,11},{10,... | collective-permute-start | bytes 786440 | tf_op jit(solution)/shard_map/ppermute | solution.py:286
  5.3 16.3 %collective-permute-start.6 = (bf16[4,8,4096]{2,1,0:T(8,128)(2,1)}, bf16[4,8,4096]{2,1,0:T(8,128)(2,1)S(1)}, u32[]{:S(2)}, u32[]{:S(2)}) collective-permute-start(bf16[4,8,4096]{2,1,0:T(8,128)(2,1)} %query_ref.3), channel_id=1, source_target_pairs={{0,1},{1,0},{2,4},{3,5},{4,2},{5,3},{6,8},{7,9},{8,6},{9,7},{10,12... | collective-permute-start | bytes 786440 | tf_op jit(solution)/shard_map/ppermute | solution.py:286
  6.3 1.6 %copy-start.1 = (bf16[2,8,128,512]{3,2,1,0:T(8,128)(2,1)S(1)}, bf16[2,8,128,512]{3,2,1,0:T(8,128)(2,1)}, u32[]{:S(2)}) copy-start(bf16[2,8,128,512]{3,2,1,0:T(8,128)(2,1)} %tail_ref.1) | copy-start | bytes 6291460
  7.8 0.9 %copy-start.3 = (bf16[4,8,4096]{2,1,0:T(8,128)(2,1)S(1)}, bf16[4,8,4096]{2,1,0:T(8,128)(2,1)}, u32[]{:S(2)}) copy-start(bf16[4,8,4096]{2,1,0:T(8,128)(2,1)} %query_ref.3) | copy-start | bytes 786436
  8.8 0.7 %copy-start.6 = (s32[64]{0:T(128)S(1)}, s32[64]{0:T(128)}, u32[]{:S(2)}) copy-start(s32[64]{0:T(128)} %ancestors_ref.11) | copy-start | bytes 772
  11.3 6.4 %copy-start.7 = (s32[64]{0:T(128)S(1)}, s32[64]{0:T(128)}, u32[]{:S(2)}) copy-start(s32[64]{0:T(128)} %ancestors_ref.11) | copy-start | bytes 772
  12.9 13.7 %collective-permute-start.1 = (s16[1056,128]{1,0:T(8,128)(2,1)S(1)}, s16[1056,128]{1,0:T(8,128)(2,1)S(1)}, u32[]{:S(2)}, u32[]{:S(2)}) collective-permute-start(s16[1056,128]{1,0:T(8,128)(2,1)S(1)} %serve.4), channel_id=1, source_target_pairs={{0,4},{1,5},{2,6},{3,7},{4,0},{5,1},{6,2},{7,3},{8,12},{9,13},{10,... | collective-permute-start | bytes 811016 | tf_op jit(solution)/shard_map/ppermute | solution.py:308
  17.6 5.7 %copy-start.2 = (bf16[2,1024,512]{2,1,0:T(8,128)(2,1)S(1)}, bf16[2,1024,512]{2,1,0:T(8,128)(2,1)}, u32[]{:S(2)}) copy-start(bf16[2,1024,512]{2,1,0:T(8,128)(2,1)} %prefix_ref.1) | copy-start | bytes 6291460
  17.6 5.7 %copy-start.4 = (bf16[4,8,4096]{2,1,0:T(8,128)(2,1)S(1)}, bf16[4,8,4096]{2,1,0:T(8,128)(2,1)}, u32[]{:S(2)}) copy-start(bf16[4,8,4096]{2,1,0:T(8,128)(2,1)} %query_ref.3) | copy-start | bytes 786436
  17.6 5.7 %copy-start.5 = (bf16[2,4,8,512]{3,2,1,0:T(8,128)(2,1)S(1)}, bf16[2,4,8,512]{3,2,1,0:T(8,128)(2,1)}, u32[]{:S(2)}) copy-start(bf16[2,4,8,512]{3,2,1,0:T(8,128)(2,1)} %fresh_ref.1) | copy-start | bytes 196612
  17.6 9.0 %collective-permute-start.3 = (s16[1056,128]{1,0:T(8,128)(2,1)S(1)}, s16[1056,128]{1,0:T(8,128)(2,1)S(1)}, u32[]{:S(2)}, u32[]{:S(2)}) collective-permute-start(s16[1056,128]{1,0:T(8,128)(2,1)S(1)} %serve.5), channel_id=1, source_target_pairs={{0,1},{1,0},{2,3},{3,2},{4,8},{5,9},{6,10},{7,11},{8,4},{9,5},{10,... | collective-permute-start | bytes 811016 | tf_op jit(solution)/shard_map/ppermute | solution.py:308
  19.4 7.0 %copy-start.9 = (s32[4,8]{1,0:T(4,128)S(1)}, s32[4,8]{1,0:T(4,128)}, u32[]{:S(2)}) copy-start(s32[4,8]{1,0:T(4,128)} %param.15) | copy-start | bytes 388
  19.4 7.0 %copy-start.10 = (s32[1024]{0:T(1024)S(1)}, s32[1024]{0:T(1024)}, u32[]{:S(2)}) copy-start(s32[1024]{0:T(1024)} %param.14) | copy-start | bytes 12292
  19.4 13.7 %copy-start.8 = (f32[4096]{0:T(1024)S(1)}, f32[4096]{0:T(1024)}, u32[]{:S(2)}) copy-start(f32[4096]{0:T(1024)} %param.17) | copy-start | bytes 49156
  19.4 13.7 %collective-permute-start.5 = (s16[1056,128]{1,0:T(8,128)(2,1)S(1)}, s16[1056,128]{1,0:T(8,128)(2,1)S(1)}, u32[]{:S(2)}, u32[]{:S(2)}) collective-permute-start(s16[1056,128]{1,0:T(8,128)(2,1)S(1)} %serve.6), channel_id=1, source_target_pairs={{0,2},{1,3},{2,0},{3,1},{4,6},{5,7},{6,4},{7,5},{8,10},{9,11},{10,... | collective-permute-start | bytes 811016 | tf_op jit(solution)/shard_map/ppermute | solution.py:308
  23.2 9.9 %collective-permute-start.7 = (s16[1056,128]{1,0:T(8,128)(2,1)S(1)}, s16[1056,128]{1,0:T(8,128)(2,1)S(1)}, u32[]{:S(2)}, u32[]{:S(2)}) collective-permute-start(s16[1056,128]{1,0:T(8,128)(2,1)S(1)} %serve.7), channel_id=1, source_target_pairs={{0,1},{1,0},{2,4},{3,5},{4,2},{5,3},{6,8},{7,9},{8,6},{9,7},{10,12... | collective-permute-start | bytes 811016 | tf_op jit(solution)/shard_map/ppermute | solution.py:308
  35.1 1.2 %collective-permute-start.8 = (f32[4,8]{1,0:T(4,128)S(1)}, f32[4,8]{1,0:T(4,128)S(1)}, u32[]{:S(2)}, u32[]{:S(2)}) collective-permute-start(f32[4,8]{1,0:T(4,128)S(1)} %get-tuple-element.13), channel_id=1, source_target_pairs={{0,1},{1,0},{2,3},{3,2},{4,5},{5,4},{6,7},{7,6},{8,9},{9,8},{10,11... | collective-permute-start | bytes 392 | tf_op jit(solution)/shard_map/ppermute | solution.py:325

commit v4 on v3

--- a/solution.py
+++ b/solution.py
@@ -8,10 +8,11 @@
 from jax.experimental.pallas import tpu as pltpu
 from jax.sharding import PartitionSpec as P
 
+
 HEADS = 64
 KV_HEADS = 8
 HEAD = 128
-REACH = 2
+EXCHANGES = ((1, 0), (2, 0), (2, 1), (1, 1))
 GROUP = HEADS // KV_HEADS
 EXPONENT_SCALE = math.log2(math.e) / math.sqrt(HEAD)
 
@@ -30,17 +31,16 @@
 
 def exchanges(length, cores):
     found = []
-    for reach in range(REACH, 0, -1):
-        for parity in (0, 1):
-            partner = list(range(length))
-            for i in range(length - reach):
-                if (i // reach) % 2 == parity:
-                    partner[i], partner[i + reach] = i + reach, i
-            pairs = []
-            for i, other in enumerate(partner):
-                turn = 1 if other == i else 0
-                pairs += [(i * cores + c, other * cores + (c + turn) % cores) for c in range(cores)]
-            found.append((reach, parity, pairs))
+    for reach, parity in EXCHANGES:
+        partner = list(range(length))
+        for i in range(length - reach):
+            if (i // reach) % 2 == parity:
+                partner[i], partner[i + reach] = i + reach, i
+        pairs = []
+        for i, other in enumerate(partner):
+            turn = 1 if other == i else 0
+            pairs += [(i * cores + c, other * cores + (c + turn) % cores) for c in range(cores)]
+        found.append((reach, parity, pairs))
     return found
 
 
@@ -135,21 +135,36 @@
     out_ref[count * each :, :] = coded.astype(jnp.int16)
 
 
-def serve_kernel(length, reach, parity, ancestors_ref, query_ref, tail_ref, out_ref):
+def serve_kernel(length, reach, parity, ancestors_ref, query_ref, tail_ref, _, out_ref):
     count = query_ref.shape[1]
     me = lax.axis_index("particle")
     found = held_by(ancestors_ref, partner_of(me, reach, parity), me, length, count)
     serve([slot for _, slot in found], query_ref, tail_ref, out_ref)
 
 
-def serve_own_kernel(length, ancestors_ref, query_ref, tail_ref, out_ref, held_ref, sem):
-    copy = pltpu.make_async_copy(tail_ref, held_ref, sem)
-    copy.start()
+def serve_own_kernel(
+    length,
+    ancestors_ref,
+    query_ref,
+    tail_ref,
+    list_ref,
+    out_ref,
+    held_ref,
+    list_out,
+    sems,
+):
+    copies = [
+        pltpu.make_async_copy(tail_ref, held_ref, sems.at[0]),
+        pltpu.make_async_copy(list_ref, list_out, sems.at[1]),
+    ]
+    for copy in copies:
+        copy.start()
     count = query_ref.shape[1]
     me = lax.axis_index("particle")
     found = held_by(ancestors_ref, me, me, length, count)
-    copy.wait()
-    serve([slot for _, slot in found], query_ref, held_ref, out_ref)
+    serve([slot for _, slot in found], query_ref, tail_ref, out_ref)
+    for copy in copies:
+        copy.wait()
 
 
 def local_kernel(query_ref, prefix_ref, fresh_ref, out_ref, log_ref):
@@ -192,7 +207,7 @@
     log_ref[...] = functools.reduce(jnp.add, logs)
 
 
-def combine_kernel(length, plans, ancestors_ref, local_ref, log_ref, readout_ref, *refs):
+def combine_kernel(length, plans, ancestors_ref, local_ref, log_ref, readout_ref, base_ref, *refs):
     sent_refs, (out_ref, twist_ref) = refs[: len(plans) + 1], refs[len(plans) + 1 :]
     steps, count = local_ref.shape[0], local_ref.shape[1]
     heads = local_ref.shape[2] // (HEAD * GROUP)
@@ -246,10 +261,10 @@
     for t in range(steps):
         column = jnp.sum(gathered[t], axis=-1, keepdims=True)
         line = jnp.sum(jnp.where(row == lane, column, 0.0), axis=0, keepdims=True)
-        twist_ref[t : t + 1, :] = line[:, :count]
-
-
-def call(kernel, outs, name, operands, flops, spaces=None, scratch=(), limit=24 << 20):
+        twist_ref[t : t + 1, :] = line[:, :count] + base_ref[t : t + 1, :]
+
+
+def call(kernel, outs, operands, flops, spaces=None, scratch=(), limit=24 << 20):
     moved = sum(math.prod(o.shape) * o.dtype.itemsize for o in operands)
     moved += sum(math.prod(o.shape) * o.dtype.itemsize for o in outs)
     spaces = spaces or [SMEM] + [VMEM] * (len(operands) - 1)
@@ -261,7 +276,6 @@
         scratch_shapes=scratch,
         compiler_params=pltpu.CompilerParams(vmem_limit_bytes=limit),
         cost_estimate=pl.CostEstimate(flops=flops, bytes_accessed=moved, transcendentals=0),
-        name=name,
     )(*operands)
 
 
@@ -283,58 +297,68 @@
     cores = lax.axis_size("tensor")
     both = ("particle", "tensor")
     plans = exchanges(length, cores)
-    asked = [lax.ppermute(queries, both, pairs) for _, _, pairs in plans]
+    asked = []
+    for _, _, pairs in plans:
+        asked.append(lax.ppermute(queries, both, pairs))
     reply = jax.ShapeDtypeStruct((count * rows + 4 * count, HEAD), jnp.int16)
     tail_work = 4 * steps * count * width * tail_cache.shape[2]
     local_work = 4 * steps * count * width * prefix_cache.shape[1]
-    own, tails = call(
+    own, tails, ancestors = call(
         functools.partial(serve_own_kernel, length),
-        [reply, jax.ShapeDtypeStruct(tail_cache.shape, tail_cache.dtype)],
-        "own",
-        [ancestors, queries, tail_cache],
+        [
+            reply,
+            jax.ShapeDtypeStruct(tail_cache.shape, tail_cache.dtype),
+            jax.ShapeDtypeStruct(ancestors.shape, ancestors.dtype),
+        ],
+        [ancestors, queries, tail_cache, ancestors],
         tail_work,
-        spaces=[SMEM, VMEM, pl.ANY],
-        scratch=(pltpu.SemaphoreType.DMA,),
-    )
+        scratch=(pltpu.SemaphoreType.DMA((2,)),),
+    )
+    answer = own
     answers = [own]
     for (reach, parity, pairs), question in zip(plans, asked):
         (answer,) = call(
             functools.partial(serve_kernel, length, reach, parity),
             [reply],
-            "serve",
-            [ancestors, question, tails],
+            [ancestors, question, tails, answer],
             tail_work,
+            spaces=[SMEM, VMEM, VMEM, pl.ANY],
         )
         answers.append(lax.ppermute(answer, both, pairs))
     local, logs = call(
         local_kernel,
         [jax.ShapeDtypeStruct(queries.shape, F32), jax.ShapeDtypeStruct((count, LANES), F32)],
-        "local",
         [queries, prefix_cache, fresh_kv],
         local_work,
         spaces=[VMEM] * 3,
     )
+    repeats = jnp.sum(
+        (sampled_ids[:, :, None] == prompt_ids[None, None, :]).astype(jnp.int32), axis=-1
+    )
+    looked_up = twist_table.at[sampled_ids].get(
+        mode="promise_in_bounds", wrap_negative_indices=False
+    )
+    base = (looked_up - 2.0 * repeats.astype(F32)) * (1.0 / cores)
     attended, partial_value = call(
         functools.partial(combine_kernel, length, [plan[:2] for plan in plans]),
         [jax.ShapeDtypeStruct(queries.shape, BF16), jax.ShapeDtypeStruct((steps, count), F32)],
-        "combine",
-        [ancestors, local, logs, readout.reshape(1, width)] + answers,
+        [ancestors, local, logs, readout.reshape(1, width), base] + answers,
         16 * steps * count * width,
     )
     if cores == 2:
-        twist_attn = partial_value + lax.ppermute(partial_value, "tensor", [(0, 1), (1, 0)])
+        twists = partial_value + lax.ppermute(partial_value, "tensor", [(0, 1), (1, 0)])
     else:
-        twist_attn = lax.psum(partial_value, "tensor")
-    repeats = jnp.sum(
-        (sampled_ids[:, :, None] == prompt_ids[None, None, :]).astype(jnp.int32), axis=-1
-    )
-    twists = twist_table.at[sampled_ids].get(mode="promise_in_bounds") - 2.0 * repeats.astype(F32) + twist_attn
+        twists = lax.psum(partial_value, "tensor")
     return (attended, twists)
+
+
+def layer(length, *arguments):
+    return on_device(length, *arguments)
 
 
 def solution(mesh):
     return jax.shard_map(
-        functools.partial(on_device, mesh.shape["particle"]),
+        functools.partial(layer, mesh.shape["particle"]),
         mesh=mesh,
         in_specs=(
             P(None, "groups", "tensor"),

time: 37.1 us -> 35.6 us (0.960)
  the two profiles are of different devices: /device:TPU:0 before, /device:TPU:11 now
where the time goes in v4:
time: 35.6 us; the launch traced here: 35.4 us
  Pallas kernels  13.7 us (38%)
  starting transfers between devices  11.4 us (32%)
  waiting for transfers between devices  6.09 us (17%)
  local copies, waits for them, and re-layouts  2.56 us (7%)
  other arithmetic  0.82 us (2%)
  between operations  0.79 us (2%)
    pallas_call x7, Pallas kernels, call(): pl.pallas_call(kernel, out_shape=tuple(outs), in_specs=[pl.BlockSpec(memo...  13.7 us
    ppermute x4, waiting for transfers between devices, on_device(): answers.append(lax.ppermute(answer, both, pairs))  5.26 us
    ppermute x4, starting transfers between devices, on_device(): answers.append(lax.ppermute(answer, both, pairs))  4.37 us
    ppermute x4, starting transfers between devices, on_device(): asked.append(lax.ppermute(queries, both, pairs))  3.84 us
    ppermute x1, starting transfers between devices, on_device(): lax.ppermute(partial_value, 'tensor', [(0, 1), (1, 0)])  3.21 us
    unnamed x20, local copies, waits for them, and re-layouts  1.01 us
    ppermute x1, waiting for transfers between devices, on_device(): lax.ppermute(partial_value, 'tensor', [(0, 1), (1, 0)])  0.82 us
    gather x2, local copies, waits for them, and re-layouts, on_device(): twist_table.at[sampled_ids]  0.78 us
  transfers between devices with their start and end apart: 9, of which 2 were waited for; matrix products, arithmetic and copies ran while one was open for 5% of the time, Pallas kernels for 33%

profile of v4, /device:TPU:11, one launch (start us, length us, event | category | flops | bytes accessed | tf_op | source)
XLA Modules:
  0.0 35.4 jit_solution(13377411092078661961)
XLA Ops:
  0.6 0.0 copy-start
  0.7 0.3 collective-permute-start
  1.0 2.6 %collective-permute-start.4 = (bf16[4,8,4096]{2,1,0:T(8,128)(2,1)}, bf16[4,8,4096]{2,1,0:T(8,128)(2,1)S(1)}, u32[]{:S(2)}, u32[]{:S(2)}) collective-permute-start(bf16[4,8,4096]{2,1,0:T(8,128)(2,1)} %query_ref.3), channel_id=1, source_target_pairs={{0,1},{1,0},{2,3},{3,2},{4,8},{5,9},{6,10},{7,11},{8,4},{9,5},{10,... | collective-permute-start | bytes 786440 | tf_op jit(solution)/shard_map/ppermute | solution.py:302
  3.6 0.9 %collective-permute-start.6 = (bf16[4,8,4096]{2,1,0:T(8,128)(2,1)}, bf16[4,8,4096]{2,1,0:T(8,128)(2,1)S(1)}, u32[]{:S(2)}, u32[]{:S(2)}) collective-permute-start(bf16[4,8,4096]{2,1,0:T(8,128)(2,1)} %query_ref.3), channel_id=1, source_target_pairs={{0,1},{1,0},{2,4},{3,5},{4,2},{5,3},{6,8},{7,9},{8,6},{9,7},{10,12... | collective-permute-start | bytes 786440 | tf_op jit(solution)/shard_map/ppermute | solution.py:302
  4.5 0.8 %reshape.12 = s32[32]{0:T(128)S(1)} reshape(s32[4,8]{1,0:T(4,128)} %param.15) | data formatting | bytes 256 | tf_op jit(solution)/shard_map/broadcast_in_dim | solution.py:338
  5.3 0.7 %gather_fusion = f32[32]{0:T(128)S(1)} fusion(f32[128256]{0:T(1024)S(1)} %copy-done, s32[1024]{0:T(1024)S(1)} %pad_clamp_fusion), kind=kCustom, calls=%fused_computation | custom fusion | bytes 384 | tf_op jit(solution)/shard_map/gather | solution.py:338
  6.0 0.1 reshape.11
  6.1 1.0 %copy-done.3 = bf16[4,8,4096]{2,1,0:T(8,128)(2,1)S(1)} copy-done((bf16[4,8,4096]{2,1,0:T(8,128)(2,1)S(1)}, bf16[4,8,4096]{2,1,0:T(8,128)(2,1)}, u32[]{:S(2)}) %copy-start.3) | copy-done | bytes 262168
  7.1 1.8 %shard_map.104 = (s16[1056,128]{1,0:T(8,128)(2,1)S(1)}, bf16[2,8,128,512]{3,2,1,0:T(8,128)(2,1)S(1)}, s32[64]{0:T(128)S(1)}) custom-call(s32[64]{0:T(128)S(1)} %copy-done.7, bf16[4,8,4096]{2,1,0:T(8,128)(2,1)S(1)} %copy-done.3, bf16[2,8,128,512]{3,2,1,0:T(8,128)(2,1)S(1)} %copy-done.2, s32[64]{0:T(128)S(1)} %copy-done.7), custom_call_target="tpu_custom_call" | custom-call | flops 67108864 | bytes 4727552 | tf_op jit(solution)/shard_map/pallas_call | solution.py:271
  8.9 0.2 convert_reduce_fusion
  9.1 2.0 %shard_map.106._ = s16[1056,128]{1,0:T(8,128)(2,1)S(1)} custom-call(s32[64]{0:T(128)S(1)} %get-tuple-element.9.ancestors_ref, bf16[4,8,4096]{2,1,0:T(8,128)(2,1)} %collective-permute-done.query_ref, bf16[2,8,128,512]{3,2,1,0:T(8,128)(2,1)S(1)} %get-tuple-element.13.tail_ref, s16[1056,128]{1,0:T(8,128)(2,1)S(1)} %get-tuple-element.12._.refs_0_), custom_call_target="tpu_custom_call" | custom-call | flops 67108864 | bytes 2900224 | tf_op jit(solution)/shard_map/pallas_call | solution.py:271
  11.1 0.4 %collective-permute-start.1 = (s16[1056,128]{1,0:T(8,128)(2,1)S(1)}, s16[1056,128]{1,0:T(8,128)(2,1)S(1)}, u32[]{:S(2)}, u32[]{:S(2)}) collective-permute-start(s16[1056,128]{1,0:T(8,128)(2,1)S(1)} %shard_map.106._), channel_id=1, source_target_pairs={{0,2},{1,3},{2,0},{3,1},{4,6},{5,7},{6,4},{7,5},{8,10},{9,11},{10,... | collective-permute-start | bytes 811016 | tf_op jit(solution)/shard_map/ppermute | solution.py:327
  11.6 1.6 %shard_map.107._ = s16[1056,128]{1,0:T(8,128)(2,1)S(1)} custom-call(s32[64]{0:T(128)S(1)} %get-tuple-element.9.ancestors_ref, bf16[4,8,4096]{2,1,0:T(8,128)(2,1)S(1)} %collective-permute-done.2.query_ref, bf16[2,8,128,512]{3,2,1,0:T(8,128)(2,1)S(1)} %get-tuple-element.13.tail_ref, s16[1056,128]{1,0:T(8,128)(2,1)S(1)} %shard_map.106._), custom_call_target="tpu_custom_call" | custom-call | flops 67108864 | bytes 2900224 | tf_op jit(solution)/shard_map/pallas_call | solution.py:271
  13.2 1.2 %collective-permute-start.3 = (s16[1056,128]{1,0:T(8,128)(2,1)S(1)}, s16[1056,128]{1,0:T(8,128)(2,1)S(1)}, u32[]{:S(2)}, u32[]{:S(2)}) collective-permute-start(s16[1056,128]{1,0:T(8,128)(2,1)S(1)} %shard_map.107._), channel_id=1, source_target_pairs={{0,4},{1,5},{2,6},{3,7},{4,0},{5,1},{6,2},{7,3},{8,12},{9,13},{10,... | collective-permute-start | bytes 811016 | tf_op jit(solution)/shard_map/ppermute | solution.py:327
  14.4 1.6 %shard_map.108._ = s16[1056,128]{1,0:T(8,128)(2,1)S(1)} custom-call(s32[64]{0:T(128)S(1)} %get-tuple-element.9.ancestors_ref, bf16[4,8,4096]{2,1,0:T(8,128)(2,1)S(1)} %collective-permute-done.4.query_ref, bf16[2,8,128,512]{3,2,1,0:T(8,128)(2,1)S(1)} %get-tuple-element.13.tail_ref, s16[1056,128]{1,0:T(8,128)(2,1)S(1)} %shard_map.107._), custom_call_target="tpu_custom_call" | custom-call | flops 67108864 | bytes 2900224 | tf_op jit(solution)/shard_map/pallas_call | solution.py:271
  16.1 0.6 %collective-permute-start.5 = (s16[1056,128]{1,0:T(8,128)(2,1)S(1)}, s16[1056,128]{1,0:T(8,128)(2,1)S(1)}, u32[]{:S(2)}, u32[]{:S(2)}) collective-permute-start(s16[1056,128]{1,0:T(8,128)(2,1)S(1)} %shard_map.108._), channel_id=1, source_target_pairs={{0,1},{1,0},{2,3},{3,2},{4,8},{5,9},{6,10},{7,11},{8,4},{9,5},{10,... | collective-permute-start | bytes 811016 | tf_op jit(solution)/shard_map/ppermute | solution.py:327
  16.6 1.6 %shard_map.109 = s16[1056,128]{1,0:T(8,128)(2,1)S(1)} custom-call(s32[64]{0:T(128)S(1)} %get-tuple-element.9.ancestors_ref, bf16[4,8,4096]{2,1,0:T(8,128)(2,1)S(1)} %collective-permute-done.6.query_ref, bf16[2,8,128,512]{3,2,1,0:T(8,128)(2,1)S(1)} %get-tuple-element.13.tail_ref, s16[1056,128]{1,0:T(8,128)(2,1)S(1)} %shard_map.108._), custom_call_target="tpu_custom_call" | custom-call | flops 67108864 | bytes 2900224 | tf_op jit(solution)/shard_map/pallas_call | solution.py:271
  18.2 2.2 %collective-permute-start.7 = (s16[1056,128]{1,0:T(8,128)(2,1)S(1)}, s16[1056,128]{1,0:T(8,128)(2,1)S(1)}, u32[]{:S(2)}, u32[]{:S(2)}) collective-permute-start(s16[1056,128]{1,0:T(8,128)(2,1)S(1)} %shard_map.109), channel_id=1, source_target_pairs={{0,1},{1,0},{2,4},{3,5},{4,2},{5,3},{6,8},{7,9},{8,6},{9,7},{10,12... | collective-permute-start | bytes 811016 | tf_op jit(solution)/shard_map/ppermute | solution.py:327
  20.4 3.0 %shard_map.105 = (f32[4,8,4096]{2,1,0:T(8,128)S(1)}, f32[8,128]{1,0:T(8,128)S(1)}) custom-call(bf16[4,8,4096]{2,1,0:T(8,128)(2,1)S(1)} %copy-done.4, bf16[2,1024,512]{2,1,0:T(8,128)(2,1)S(1)} %copy-done.1, bf16[2,4,8,512]{3,2,1,0:T(8,128)(2,1)S(1)} %copy-done.5), custom_call_target="tpu_custom_call" | custom-call | flops 536870912 | bytes 2953216 | tf_op jit(solution)/shard_map/pallas_call | solution.py:271
  23.5 5.3 %collective-permute-done.7.refs_4_ = s16[1056,128]{1,0:T(8,128)(2,1)S(1)} collective-permute-done((s16[1056,128]{1,0:T(8,128)(2,1)S(1)}, s16[1056,128]{1,0:T(8,128)(2,1)S(1)}, u32[]{:S(2)}, u32[]{:S(2)}) %collective-permute-start.7) | collective-permute-done | bytes 270368 | tf_op jit(solution)/shard_map/ppermute | solution.py:327
  28.8 2.0 %shard_map.110 = (bf16[4,8,4096]{2,1,0:T(8,128)(2,1)}, f32[4,8]{1,0:T(4,128)S(1)}) custom-call(s32[64]{0:T(128)S(1)} %get-tuple-element.9.ancestors_ref, f32[4,8,4096]{2,1,0:T(8,128)S(1)} %get-tuple-element.10.local_ref, f32[8,128]{1,0:T(8,128)S(1)} %get-tuple-element.11.log_ref, f32[1,4096]{1,0:T(1,128)S(1)} %bitcast.1, ...), custom_call_target="tpu_custom_call" | custom-call | flops 2097152 | bytes 2159104 | tf_op jit(solution)/shard_map/pallas_call | solution.py:271
  30.8 3.2 %collective-permute-start.8 = (f32[4,8]{1,0:T(4,128)S(1)}, f32[4,8]{1,0:T(4,128)S(1)}, u32[]{:S(2)}, u32[]{:S(2)}) collective-permute-start(f32[4,8]{1,0:T(4,128)S(1)} %get-tuple-element.15), channel_id=1, source_target_pairs={{0,1},{1,0},{2,3},{3,2},{4,5},{5,4},{6,7},{7,6},{8,9},{9,8},{10,11... | collective-permute-start | bytes 392 | tf_op jit(solution)/shard_map/ppermute | solution.py:349
  34.0 0.8 %collective-permute-done.8 = f32[4,8]{1,0:T(4,128)S(1)} collective-permute-done((f32[4,8]{1,0:T(4,128)S(1)}, f32[4,8]{1,0:T(4,128)S(1)}, u32[]{:S(2)}, u32[]{:S(2)}) %collective-permute-start.8) | collective-permute-done | bytes 160 | tf_op jit(solution)/shard_map/ppermute | solution.py:349
  34.8 0.6 %add.3 = f32[4,8]{1,0:T(4,128)} add(f32[4,8]{1,0:T(4,128)S(1)} %get-tuple-element.15, f32[4,8]{1,0:T(4,128)S(1)} %collective-permute-done.8) | non-fusion elementwise | flops 32 | bytes 384 | tf_op jit(solution)/shard_map/add | solution.py:349
  (28 shorter events, 0.1 us)
Async XLA Ops:
  0.6 4.7 %copy-start = (f32[128256]{0:T(1024)S(1)}, f32[128256]{0:T(1024)}, u32[]{:S(2)}) copy-start(f32[128256]{0:T(1024)} %param.16) | copy-start | bytes 1539076
  0.6 5.5 %copy-start.2 = (bf16[2,8,128,512]{3,2,1,0:T(8,128)(2,1)S(1)}, bf16[2,8,128,512]{3,2,1,0:T(8,128)(2,1)}, u32[]{:S(2)}) copy-start(bf16[2,8,128,512]{3,2,1,0:T(8,128)(2,1)} %tail_ref.1) | copy-start | bytes 6291460
  0.7 5.4 %copy-start.7 = (s32[64]{0:T(128)S(1)}, s32[64]{0:T(128)}, u32[]{:S(2)}) copy-start(s32[64]{0:T(128)} %list_ref.1) | copy-start | bytes 772
  0.7 8.4 %collective-permute-start = (bf16[4,8,4096]{2,1,0:T(8,128)(2,1)}, bf16[4,8,4096]{2,1,0:T(8,128)(2,1)}, u32[]{:S(2)}, u32[]{:S(2)}) collective-permute-start(bf16[4,8,4096]{2,1,0:T(8,128)(2,1)} %query_ref.3), channel_id=1, source_target_pairs={{0,2},{1,3},{2,0},{3,1},{4,6},{5,7},{6,4},{7,5},{8,10},{9,11},{10,... | collective-permute-start | bytes 786440 | tf_op jit(solution)/shard_map/ppermute | solution.py:302
  1.0 10.6 %collective-permute-start.2 = (bf16[4,8,4096]{2,1,0:T(8,128)(2,1)}, bf16[4,8,4096]{2,1,0:T(8,128)(2,1)S(1)}, u32[]{:S(2)}, u32[]{:S(2)}) collective-permute-start(bf16[4,8,4096]{2,1,0:T(8,128)(2,1)} %query_ref.3), channel_id=1, source_target_pairs={{0,4},{1,5},{2,6},{3,7},{4,0},{5,1},{6,2},{7,3},{8,12},{9,13},{10,... | collective-permute-start | bytes 786440 | tf_op jit(solution)/shard_map/ppermute | solution.py:302
  1.0 13.4 %collective-permute-start.4 = (bf16[4,8,4096]{2,1,0:T(8,128)(2,1)}, bf16[4,8,4096]{2,1,0:T(8,128)(2,1)S(1)}, u32[]{:S(2)}, u32[]{:S(2)}) collective-permute-start(bf16[4,8,4096]{2,1,0:T(8,128)(2,1)} %query_ref.3), channel_id=1, source_target_pairs={{0,1},{1,0},{2,3},{3,2},{4,8},{5,9},{6,10},{7,11},{8,4},{9,5},{10,... | collective-permute-start | bytes 786440 | tf_op jit(solution)/shard_map/ppermute | solution.py:302
  3.6 13.0 %collective-permute-start.6 = (bf16[4,8,4096]{2,1,0:T(8,128)(2,1)}, bf16[4,8,4096]{2,1,0:T(8,128)(2,1)S(1)}, u32[]{:S(2)}, u32[]{:S(2)}) collective-permute-start(bf16[4,8,4096]{2,1,0:T(8,128)(2,1)} %query_ref.3), channel_id=1, source_target_pairs={{0,1},{1,0},{2,4},{3,5},{4,2},{5,3},{6,8},{7,9},{8,6},{9,7},{10,12... | collective-permute-start | bytes 786440 | tf_op jit(solution)/shard_map/ppermute | solution.py:302
  5.3 3.6 %copy-start.8 = (s32[4,8]{1,0:T(4,128)S(1)}, s32[4,8]{1,0:T(4,128)}, u32[]{:S(2)}) copy-start(s32[4,8]{1,0:T(4,128)} %param.15) | copy-start | bytes 388
  5.3 3.6 %copy-start.9 = (s32[1024]{0:T(1024)S(1)}, s32[1024]{0:T(1024)}, u32[]{:S(2)}) copy-start(s32[1024]{0:T(1024)} %param.14) | copy-start | bytes 12292
  6.1 1.0 %copy-start.3 = (bf16[4,8,4096]{2,1,0:T(8,128)(2,1)S(1)}, bf16[4,8,4096]{2,1,0:T(8,128)(2,1)}, u32[]{:S(2)}) copy-start(bf16[4,8,4096]{2,1,0:T(8,128)(2,1)} %query_ref.3) | copy-start | bytes 786436
  11.1 17.6 %collective-permute-start.1 = (s16[1056,128]{1,0:T(8,128)(2,1)S(1)}, s16[1056,128]{1,0:T(8,128)(2,1)S(1)}, u32[]{:S(2)}, u32[]{:S(2)}) collective-permute-start(s16[1056,128]{1,0:T(8,128)(2,1)S(1)} %shard_map.106._), channel_id=1, source_target_pairs={{0,2},{1,3},{2,0},{3,1},{4,6},{5,7},{6,4},{7,5},{8,10},{9,11},{10,... | collective-permute-start | bytes 811016 | tf_op jit(solution)/shard_map/ppermute | solution.py:327
  13.2 15.6 %collective-permute-start.3 = (s16[1056,128]{1,0:T(8,128)(2,1)S(1)}, s16[1056,128]{1,0:T(8,128)(2,1)S(1)}, u32[]{:S(2)}, u32[]{:S(2)}) collective-permute-start(s16[1056,128]{1,0:T(8,128)(2,1)S(1)} %shard_map.107._), channel_id=1, source_target_pairs={{0,4},{1,5},{2,6},{3,7},{4,0},{5,1},{6,2},{7,3},{8,12},{9,13},{10,... | collective-permute-start | bytes 811016 | tf_op jit(solution)/shard_map/ppermute | solution.py:327
  16.0 4.4 %copy-start.1 = (bf16[2,1024,512]{2,1,0:T(8,128)(2,1)S(1)}, bf16[2,1024,512]{2,1,0:T(8,128)(2,1)}, u32[]{:S(2)}) copy-start(bf16[2,1024,512]{2,1,0:T(8,128)(2,1)} %prefix_ref.1) | copy-start | bytes 6291460
  16.0 4.4 %copy-start.4 = (bf16[4,8,4096]{2,1,0:T(8,128)(2,1)S(1)}, bf16[4,8,4096]{2,1,0:T(8,128)(2,1)}, u32[]{:S(2)}) copy-start(bf16[4,8,4096]{2,1,0:T(8,128)(2,1)} %query_ref.3) | copy-start | bytes 786436
  16.0 4.4 %copy-start.5 = (bf16[2,4,8,512]{3,2,1,0:T(8,128)(2,1)S(1)}, bf16[2,4,8,512]{3,2,1,0:T(8,128)(2,1)}, u32[]{:S(2)}) copy-start(bf16[2,4,8,512]{3,2,1,0:T(8,128)(2,1)} %fresh_ref.1) | copy-start | bytes 196612
  16.0 12.7 %copy-start.6 = (f32[4096]{0:T(1024)S(1)}, f32[4096]{0:T(1024)}, u32[]{:S(2)}) copy-start(f32[4096]{0:T(1024)} %param.17) | copy-start | bytes 49156
  16.1 12.7 %collective-permute-start.5 = (s16[1056,128]{1,0:T(8,128)(2,1)S(1)}, s16[1056,128]{1,0:T(8,128)(2,1)S(1)}, u32[]{:S(2)}, u32[]{:S(2)}) collective-permute-start(s16[1056,128]{1,0:T(8,128)(2,1)S(1)} %shard_map.108._), channel_id=1, source_target_pairs={{0,1},{1,0},{2,3},{3,2},{4,8},{5,9},{6,10},{7,11},{8,4},{9,5},{10,... | collective-permute-start | bytes 811016 | tf_op jit(solution)/shard_map/ppermute | solution.py:327
  18.2 10.5 %collective-permute-start.7 = (s16[1056,128]{1,0:T(8,128)(2,1)S(1)}, s16[1056,128]{1,0:T(8,128)(2,1)S(1)}, u32[]{:S(2)}, u32[]{:S(2)}) collective-permute-start(s16[1056,128]{1,0:T(8,128)(2,1)S(1)} %shard_map.109), channel_id=1, source_target_pairs={{0,1},{1,0},{2,4},{3,5},{4,2},{5,3},{6,8},{7,9},{8,6},{9,7},{10,12... | collective-permute-start | bytes 811016 | tf_op jit(solution)/shard_map/ppermute | solution.py:327
  30.8 4.0 %collective-permute-start.8 = (f32[4,8]{1,0:T(4,128)S(1)}, f32[4,8]{1,0:T(4,128)S(1)}, u32[]{:S(2)}, u32[]{:S(2)}) collective-permute-start(f32[4,8]{1,0:T(4,128)S(1)} %get-tuple-element.15), channel_id=1, source_target_pairs={{0,1},{1,0},{2,3},{3,2},{4,5},{5,4},{6,7},{7,6},{8,9},{9,8},{10,11... | collective-permute-start | bytes 392 | tf_op jit(solution)/shard_map/ppermute | solution.py:349

commit v5 on v4

--- a/solution.py
+++ b/solution.py
@@ -86,9 +86,9 @@
     return (whole + part * (1.0 / LOG_FRACTION)) * (1.0 / LOG_STEPS)
 
 
-def serve(slots, query_ref, tail_ref, out_ref):
+def serve(slots, query_ref, key_ref, value_ref, out_ref):
     steps, count = query_ref.shape[0], query_ref.shape[1]
-    heads = tail_ref.shape[3] // HEAD
+    heads = value_ref.shape[2] // HEAD
     many = steps * GROUP
     each = heads * many
     lane = lax.broadcasted_iota(jnp.int32, (GROUP, LANES), 1)
@@ -99,12 +99,15 @@
         tiles = jnp.stack(head_tiles(query_ref, k * GROUP * HEAD), axis=0)
         rows = jnp.swapaxes(tiles, 0, 1).astype(BF16)
         cols = slice(k * HEAD, (k + 1) * HEAD)
-        scores += [scores_of(rows[p], tail_ref[0, slots[p], :, cols]) for p in range(count)]
+        scores += [
+            jnp.dot(rows[p], key_ref[slots[p], cols, :], preferred_element_type=F32)
+            for p in range(count)
+        ]
     terms = [softmax_terms(score) for score in scores]
     outs = [
         jnp.dot(
             terms[k * count + p][1].astype(BF16),
-            tail_ref[1, slots[p], :, k * HEAD : (k + 1) * HEAD],
+            value_ref[slots[p], :, k * HEAD : (k + 1) * HEAD],
             preferred_element_type=F32,
         )
         for k in range(heads)
@@ -135,11 +138,11 @@
     out_ref[count * each :, :] = coded.astype(jnp.int16)
 
 
-def serve_kernel(length, reach, parity, ancestors_ref, query_ref, tail_ref, _, out_ref):
+def serve_kernel(length, reach, parity, ancestors_ref, query_ref, key_ref, value_ref, _, out_ref):
     count = query_ref.shape[1]
     me = lax.axis_index("particle")
     found = held_by(ancestors_ref, partner_of(me, reach, parity), me, length, count)
-    serve([slot for _, slot in found], query_ref, tail_ref, out_ref)
+    serve([slot for _, slot in found], query_ref, key_ref, value_ref, out_ref)
 
 
 def serve_own_kernel(
@@ -149,12 +152,13 @@
     tail_ref,
     list_ref,
     out_ref,
-    held_ref,
+    key_ref,
+    value_ref,
     list_out,
     sems,
 ):
     copies = [
-        pltpu.make_async_copy(tail_ref, held_ref, sems.at[0]),
+        pltpu.make_async_copy(tail_ref.at[1], value_ref, sems.at[0]),
         pltpu.make_async_copy(list_ref, list_out, sems.at[1]),
     ]
     for copy in copies:
@@ -162,7 +166,10 @@
     count = query_ref.shape[1]
     me = lax.axis_index("particle")
     found = held_by(ancestors_ref, me, me, length, count)
-    serve([slot for _, slot in found], query_ref, tail_ref, out_ref)
+    for j in range(count):
+        for at in range(0, tail_ref.shape[3], HEAD):
+            key_ref[j, at : at + HEAD, :] = tail_ref[0, j, :, at : at + HEAD].T
+    serve([slot for _, slot in found], query_ref, key_ref, tail_ref.at[1], out_ref)
     for copy in copies:
         copy.wait()
 
@@ -293,6 +300,7 @@
 ):
     steps, count, width = queries.shape
     rows = steps * width // HEAD
+    tail_width = tail_cache.shape[3]
     assert rows <= LANES and steps % 2 == 0
     cores = lax.axis_size("tensor")
     both = ("particle", "tensor")
@@ -303,11 +311,12 @@
     reply = jax.ShapeDtypeStruct((count * rows + 4 * count, HEAD), jnp.int16)
     tail_work = 4 * steps * count * width * tail_cache.shape[2]
     local_work = 4 * steps * count * width * prefix_cache.shape[1]
-    own, tails, ancestors = call(
+    own, keys, values, ancestors = call(
         functools.partial(serve_own_kernel, length),
         [
             reply,
-            jax.ShapeDtypeStruct(tail_cache.shape, tail_cache.dtype),
+            jax.ShapeDtypeStruct((count, tail_width, tail_cache.shape[2]), BF16),
+            jax.ShapeDtypeStruct(tail_cache.shape[1:], BF16),
             jax.ShapeDtypeStruct(ancestors.shape, ancestors.dtype),
         ],
         [ancestors, queries, tail_cache, ancestors],
@@ -320,9 +329,9 @@
         (answer,) = call(
             functools.partial(serve_kernel, length, reach, parity),
             [reply],
-            [ancestors, question, tails, answer],
+            [ancestors, question, keys, values, answer],
             tail_work,
-            spaces=[SMEM, VMEM, VMEM, pl.ANY],
+            spaces=[SMEM, VMEM, VMEM, VMEM, pl.ANY],
         )
         answers.append(lax.ppermute(answer, both, pairs))
     local, logs = call(

time: 35.6 us -> 34.8 us (0.978)
  Pallas kernels: 13.7 us -> 12.6 us
    pallas_call x7, Pallas kernels: 13.7 us -> 12.6 us  [call(): pl.pallas_call(kernel, out_shape=tuple(outs), in_specs=[pl.BlockSpec(memo...]
  transfers between devices with their start and end apart: 9 -> 9, of which waited for: 2 -> 2; matrix products, arithmetic and copies ran while one was open for 5% -> 5% of each run, Pallas kernels for 33% -> 31%
where the time goes in v5:
time: 34.8 us; the launch traced here: 34.6 us
  Pallas kernels  12.6 us (36%)
  starting transfers between devices  11.4 us (33%)
  waiting for transfers between devices  6.36 us (18%)
  local copies, waits for them, and re-layouts  2.56 us (7%)
  other arithmetic  0.82 us (2%)
  between operations  0.79 us (2%)
    pallas_call x7, Pallas kernels, call(): pl.pallas_call(kernel, out_shape=tuple(outs), in_specs=[pl.BlockSpec(memo...  12.6 us
    ppermute x4, waiting for transfers between devices, on_device(): answers.append(lax.ppermute(answer, both, pairs))  5.53 us
    ppermute x4, starting transfers between devices, on_device(): answers.append(lax.ppermute(answer, both, pairs))  4.37 us
    ppermute x4, starting transfers between devices, on_device(): asked.append(lax.ppermute(queries, both, pairs))  3.84 us
    ppermute x1, starting transfers between devices, on_device(): lax.ppermute(partial_value, 'tensor', [(0, 1), (1, 0)])  3.21 us
    unnamed x20, local copies, waits for them, and re-layouts  1.01 us
    ppermute x1, waiting for transfers between devices, on_device(): lax.ppermute(partial_value, 'tensor', [(0, 1), (1, 0)])  0.82 us
    gather x2, local copies, waits for them, and re-layouts, on_device(): twist_table.at[sampled_ids]  0.78 us
  transfers between devices with their start and end apart: 9, of which 2 were waited for; matrix products, arithmetic and copies ran while one was open for 5% of the time, Pallas kernels for 31%

profile of v5, /device:TPU:11, one launch (start us, length us, event | category | flops | bytes accessed | tf_op | source)
XLA Modules:
  0.0 34.6 jit_solution(11875672835479837286)
XLA Ops:
  0.6 0.0 copy-start
  0.7 0.3 collective-permute-start
  1.0 2.6 %collective-permute-start.4 = (bf16[4,8,4096]{2,1,0:T(8,128)(2,1)}, bf16[4,8,4096]{2,1,0:T(8,128)(2,1)S(1)}, u32[]{:S(2)}, u32[]{:S(2)}) collective-permute-start(bf16[4,8,4096]{2,1,0:T(8,128)(2,1)} %query_ref.3), channel_id=1, source_target_pairs={{0,1},{1,0},{2,3},{3,2},{4,8},{5,9},{6,10},{7,11},{8,4},{9,5},{10,... | collective-permute-start | bytes 786440 | tf_op jit(solution)/shard_map/ppermute | solution.py:310
  3.6 0.9 %collective-permute-start.6 = (bf16[4,8,4096]{2,1,0:T(8,128)(2,1)}, bf16[4,8,4096]{2,1,0:T(8,128)(2,1)S(1)}, u32[]{:S(2)}, u32[]{:S(2)}) collective-permute-start(bf16[4,8,4096]{2,1,0:T(8,128)(2,1)} %query_ref.3), channel_id=1, source_target_pairs={{0,1},{1,0},{2,4},{3,5},{4,2},{5,3},{6,8},{7,9},{8,6},{9,7},{10,12... | collective-permute-start | bytes 786440 | tf_op jit(solution)/shard_map/ppermute | solution.py:310
  4.5 0.8 %reshape.12 = s32[32]{0:T(128)S(1)} reshape(s32[4,8]{1,0:T(4,128)} %param.15) | data formatting | bytes 256 | tf_op jit(solution)/shard_map/broadcast_in_dim | solution.py:347
  5.3 0.7 %gather_fusion = f32[32]{0:T(128)S(1)} fusion(f32[128256]{0:T(1024)S(1)} %copy-done, s32[1024]{0:T(1024)S(1)} %pad_clamp_fusion), kind=kCustom, calls=%fused_computation | custom fusion | bytes 384 | tf_op jit(solution)/shard_map/gather | solution.py:347
  6.0 0.1 reshape.11
  6.1 1.0 %copy-done.3 = bf16[4,8,4096]{2,1,0:T(8,128)(2,1)S(1)} copy-done((bf16[4,8,4096]{2,1,0:T(8,128)(2,1)S(1)}, bf16[4,8,4096]{2,1,0:T(8,128)(2,1)}, u32[]{:S(2)}) %copy-start.3) | copy-done | bytes 262168
  7.1 1.7 %shard_map.104 = (s16[1056,128]{1,0:T(8,128)(2,1)S(1)}, bf16[8,512,128]{2,1,0:T(8,128)(2,1)S(1)}, bf16[8,128,512]{2,1,0:T(8,128)(2,1)S(1)}, s32[64]{0:T(128)S(1)}) custom-call(s32[64]{0:T(128)S(1)} %copy-done.7, bf16[4,8,4096]{2,1,0:T(8,128)(2,1)S(1)} %copy-done.3, bf16[2,8,128,512]{3,2,1,0:T(8,128)(2,1)S(1)} %copy-done.2, s32[64]{0:T(128)S(1)} %copy-done.7), custom_call_target="tpu_custom_call" | custom-call | flops 67108864 | bytes 4727552 | tf_op jit(solution)/shard_map/pallas_call | solution.py:278
  8.8 0.2 convert_reduce_fusion
  9.1 1.8 %shard_map.106._ = s16[1056,128]{1,0:T(8,128)(2,1)S(1)} custom-call(s32[64]{0:T(128)S(1)} %get-tuple-element.10.ancestors_ref, bf16[4,8,4096]{2,1,0:T(8,128)(2,1)} %collective-permute-done.query_ref, bf16[8,512,128]{2,1,0:T(8,128)(2,1)S(1)} %get-tuple-element.14.key_ref, bf16[8,128,512]{2,1,0:T(8,128)(2,1)S(1)} %get-tuple-element.15.value_ref, ...), custom_call_target="tpu_custom_call" | custom-call | flops 67108864 | bytes 2900224 | tf_op jit(solution)/shard_map/pallas_call | solution.py:278
  10.8 0.4 %collective-permute-start.1 = (s16[1056,128]{1,0:T(8,128)(2,1)S(1)}, s16[1056,128]{1,0:T(8,128)(2,1)S(1)}, u32[]{:S(2)}, u32[]{:S(2)}) collective-permute-start(s16[1056,128]{1,0:T(8,128)(2,1)S(1)} %shard_map.106._), channel_id=1, source_target_pairs={{0,2},{1,3},{2,0},{3,1},{4,6},{5,7},{6,4},{7,5},{8,10},{9,11},{10,... | collective-permute-start | bytes 811016 | tf_op jit(solution)/shard_map/ppermute | solution.py:336
  11.3 1.4 %shard_map.107._ = s16[1056,128]{1,0:T(8,128)(2,1)S(1)} custom-call(s32[64]{0:T(128)S(1)} %get-tuple-element.10.ancestors_ref, bf16[4,8,4096]{2,1,0:T(8,128)(2,1)S(1)} %collective-permute-done.2.query_ref, bf16[8,512,128]{2,1,0:T(8,128)(2,1)S(1)} %get-tuple-element.14.key_ref, bf16[8,128,512]{2,1,0:T(8,128)(2,1)S(1)} %get-tuple-element.15.value_ref, ...), custom_call_target="tpu_custom_call" | custom-call | flops 67108864 | bytes 2900224 | tf_op jit(solution)/shard_map/pallas_call | solution.py:278
  12.6 1.2 %collective-permute-start.3 = (s16[1056,128]{1,0:T(8,128)(2,1)S(1)}, s16[1056,128]{1,0:T(8,128)(2,1)S(1)}, u32[]{:S(2)}, u32[]{:S(2)}) collective-permute-start(s16[1056,128]{1,0:T(8,128)(2,1)S(1)} %shard_map.107._), channel_id=1, source_target_pairs={{0,4},{1,5},{2,6},{3,7},{4,0},{5,1},{6,2},{7,3},{8,12},{9,13},{10,... | collective-permute-start | bytes 811016 | tf_op jit(solution)/shard_map/ppermute | solution.py:336
  13.8 1.4 %shard_map.108._ = s16[1056,128]{1,0:T(8,128)(2,1)S(1)} custom-call(s32[64]{0:T(128)S(1)} %get-tuple-element.10.ancestors_ref, bf16[4,8,4096]{2,1,0:T(8,128)(2,1)S(1)} %collective-permute-done.4.query_ref, bf16[8,512,128]{2,1,0:T(8,128)(2,1)S(1)} %get-tuple-element.14.key_ref, bf16[8,128,512]{2,1,0:T(8,128)(2,1)S(1)} %get-tuple-element.15.value_ref, ...), custom_call_target="tpu_custom_call" | custom-call | flops 67108864 | bytes 2900224 | tf_op jit(solution)/shard_map/pallas_call | solution.py:278
  15.3 0.6 %collective-permute-start.5 = (s16[1056,128]{1,0:T(8,128)(2,1)S(1)}, s16[1056,128]{1,0:T(8,128)(2,1)S(1)}, u32[]{:S(2)}, u32[]{:S(2)}) collective-permute-start(s16[1056,128]{1,0:T(8,128)(2,1)S(1)} %shard_map.108._), channel_id=1, source_target_pairs={{0,1},{1,0},{2,3},{3,2},{4,8},{5,9},{6,10},{7,11},{8,4},{9,5},{10,... | collective-permute-start | bytes 811016 | tf_op jit(solution)/shard_map/ppermute | solution.py:336
  15.9 1.4 %shard_map.109 = s16[1056,128]{1,0:T(8,128)(2,1)S(1)} custom-call(s32[64]{0:T(128)S(1)} %get-tuple-element.10.ancestors_ref, bf16[4,8,4096]{2,1,0:T(8,128)(2,1)S(1)} %collective-permute-done.6.query_ref, bf16[8,512,128]{2,1,0:T(8,128)(2,1)S(1)} %get-tuple-element.14.key_ref, bf16[8,128,512]{2,1,0:T(8,128)(2,1)S(1)} %get-tuple-element.15.value_ref, ...), custom_call_target="tpu_custom_call" | custom-call | flops 67108864 | bytes 2900224 | tf_op jit(solution)/shard_map/pallas_call | solution.py:278
  17.2 2.1 %collective-permute-start.7 = (s16[1056,128]{1,0:T(8,128)(2,1)S(1)}, s16[1056,128]{1,0:T(8,128)(2,1)S(1)}, u32[]{:S(2)}, u32[]{:S(2)}) collective-permute-start(s16[1056,128]{1,0:T(8,128)(2,1)S(1)} %shard_map.109), channel_id=1, source_target_pairs={{0,1},{1,0},{2,4},{3,5},{4,2},{5,3},{6,8},{7,9},{8,6},{9,7},{10,12... | collective-permute-start | bytes 811016 | tf_op jit(solution)/shard_map/ppermute | solution.py:336
  19.4 3.0 %shard_map.105 = (f32[4,8,4096]{2,1,0:T(8,128)S(1)}, f32[8,128]{1,0:T(8,128)S(1)}) custom-call(bf16[4,8,4096]{2,1,0:T(8,128)(2,1)S(1)} %copy-done.4, bf16[2,1024,512]{2,1,0:T(8,128)(2,1)S(1)} %copy-done.1, bf16[2,4,8,512]{3,2,1,0:T(8,128)(2,1)S(1)} %copy-done.5), custom_call_target="tpu_custom_call" | custom-call | flops 536870912 | bytes 2953216 | tf_op jit(solution)/shard_map/pallas_call | solution.py:278
  22.4 5.5 %collective-permute-done.7.refs_4_ = s16[1056,128]{1,0:T(8,128)(2,1)S(1)} collective-permute-done((s16[1056,128]{1,0:T(8,128)(2,1)S(1)}, s16[1056,128]{1,0:T(8,128)(2,1)S(1)}, u32[]{:S(2)}, u32[]{:S(2)}) %collective-permute-start.7) | collective-permute-done | bytes 270368 | tf_op jit(solution)/shard_map/ppermute | solution.py:336
  28.0 2.0 %shard_map.110 = (bf16[4,8,4096]{2,1,0:T(8,128)(2,1)}, f32[4,8]{1,0:T(4,128)S(1)}) custom-call(s32[64]{0:T(128)S(1)} %get-tuple-element.10.ancestors_ref, f32[4,8,4096]{2,1,0:T(8,128)S(1)} %get-tuple-element.11.local_ref, f32[8,128]{1,0:T(8,128)S(1)} %get-tuple-element.12.log_ref, f32[1,4096]{1,0:T(1,128)S(1)} %bitcast.1, ...), custom_call_target="tpu_custom_call" | custom-call | flops 2097152 | bytes 2159104 | tf_op jit(solution)/shard_map/pallas_call | solution.py:278
  30.0 3.2 %collective-permute-start.8 = (f32[4,8]{1,0:T(4,128)S(1)}, f32[4,8]{1,0:T(4,128)S(1)}, u32[]{:S(2)}, u32[]{:S(2)}) collective-permute-start(f32[4,8]{1,0:T(4,128)S(1)} %get-tuple-element.17), channel_id=1, source_target_pairs={{0,1},{1,0},{2,3},{3,2},{4,5},{5,4},{6,7},{7,6},{8,9},{9,8},{10,11... | collective-permute-start | bytes 392 | tf_op jit(solution)/shard_map/ppermute | solution.py:358
  33.2 0.8 %collective-permute-done.8 = f32[4,8]{1,0:T(4,128)S(1)} collective-permute-done((f32[4,8]{1,0:T(4,128)S(1)}, f32[4,8]{1,0:T(4,128)S(1)}, u32[]{:S(2)}, u32[]{:S(2)}) %collective-permute-start.8) | collective-permute-done | bytes 160 | tf_op jit(solution)/shard_map/ppermute | solution.py:358
  34.0 0.6 %add.3 = f32[4,8]{1,0:T(4,128)} add(f32[4,8]{1,0:T(4,128)S(1)} %get-tuple-element.17, f32[4,8]{1,0:T(4,128)S(1)} %collective-permute-done.8) | non-fusion elementwise | flops 32 | bytes 384 | tf_op jit(solution)/shard_map/add | solution.py:358
  (28 shorter events, 0.1 us)
Async XLA Ops:
  0.6 4.7 %copy-start = (f32[128256]{0:T(1024)S(1)}, f32[128256]{0:T(1024)}, u32[]{:S(2)}) copy-start(f32[128256]{0:T(1024)} %param.16) | copy-start | bytes 1539076
  0.6 5.5 %copy-start.2 = (bf16[2,8,128,512]{3,2,1,0:T(8,128)(2,1)S(1)}, bf16[2,8,128,512]{3,2,1,0:T(8,128)(2,1)}, u32[]{:S(2)}) copy-start(bf16[2,8,128,512]{3,2,1,0:T(8,128)(2,1)} %tail_ref.1) | copy-start | bytes 6291460
  0.7 5.4 %copy-start.7 = (s32[64]{0:T(128)S(1)}, s32[64]{0:T(128)}, u32[]{:S(2)}) copy-start(s32[64]{0:T(128)} %list_ref.1) | copy-start | bytes 772
  0.7 8.4 %collective-permute-start = (bf16[4,8,4096]{2,1,0:T(8,128)(2,1)}, bf16[4,8,4096]{2,1,0:T(8,128)(2,1)}, u32[]{:S(2)}, u32[]{:S(2)}) collective-permute-start(bf16[4,8,4096]{2,1,0:T(8,128)(2,1)} %query_ref.3), channel_id=1, source_target_pairs={{0,2},{1,3},{2,0},{3,1},{4,6},{5,7},{6,4},{7,5},{8,10},{9,11},{10,... | collective-permute-start | bytes 786440 | tf_op jit(solution)/shard_map/ppermute | solution.py:310
  1.0 10.3 %collective-permute-start.2 = (bf16[4,8,4096]{2,1,0:T(8,128)(2,1)}, bf16[4,8,4096]{2,1,0:T(8,128)(2,1)S(1)}, u32[]{:S(2)}, u32[]{:S(2)}) collective-permute-start(bf16[4,8,4096]{2,1,0:T(8,128)(2,1)} %query_ref.3), channel_id=1, source_target_pairs={{0,4},{1,5},{2,6},{3,7},{4,0},{5,1},{6,2},{7,3},{8,12},{9,13},{10,... | collective-permute-start | bytes 786440 | tf_op jit(solution)/shard_map/ppermute | solution.py:310
  1.0 12.8 %collective-permute-start.4 = (bf16[4,8,4096]{2,1,0:T(8,128)(2,1)}, bf16[4,8,4096]{2,1,0:T(8,128)(2,1)S(1)}, u32[]{:S(2)}, u32[]{:S(2)}) collective-permute-start(bf16[4,8,4096]{2,1,0:T(8,128)(2,1)} %query_ref.3), channel_id=1, source_target_pairs={{0,1},{1,0},{2,3},{3,2},{4,8},{5,9},{6,10},{7,11},{8,4},{9,5},{10,... | collective-permute-start | bytes 786440 | tf_op jit(solution)/shard_map/ppermute | solution.py:310
  3.6 12.3 %collective-permute-start.6 = (bf16[4,8,4096]{2,1,0:T(8,128)(2,1)}, bf16[4,8,4096]{2,1,0:T(8,128)(2,1)S(1)}, u32[]{:S(2)}, u32[]{:S(2)}) collective-permute-start(bf16[4,8,4096]{2,1,0:T(8,128)(2,1)} %query_ref.3), channel_id=1, source_target_pairs={{0,1},{1,0},{2,4},{3,5},{4,2},{5,3},{6,8},{7,9},{8,6},{9,7},{10,12... | collective-permute-start | bytes 786440 | tf_op jit(solution)/shard_map/ppermute | solution.py:310
  5.3 3.5 %copy-start.8 = (s32[4,8]{1,0:T(4,128)S(1)}, s32[4,8]{1,0:T(4,128)}, u32[]{:S(2)}) copy-start(s32[4,8]{1,0:T(4,128)} %param.15) | copy-start | bytes 388
  5.3 3.5 %copy-start.9 = (s32[1024]{0:T(1024)S(1)}, s32[1024]{0:T(1024)}, u32[]{:S(2)}) copy-start(s32[1024]{0:T(1024)} %param.14) | copy-start | bytes 12292
  6.1 1.0 %copy-start.3 = (bf16[4,8,4096]{2,1,0:T(8,128)(2,1)S(1)}, bf16[4,8,4096]{2,1,0:T(8,128)(2,1)}, u32[]{:S(2)}) copy-start(bf16[4,8,4096]{2,1,0:T(8,128)(2,1)} %query_ref.3) | copy-start | bytes 786436
  10.8 17.1 %collective-permute-start.1 = (s16[1056,128]{1,0:T(8,128)(2,1)S(1)}, s16[1056,128]{1,0:T(8,128)(2,1)S(1)}, u32[]{:S(2)}, u32[]{:S(2)}) collective-permute-start(s16[1056,128]{1,0:T(8,128)(2,1)S(1)} %shard_map.106._), channel_id=1, source_target_pairs={{0,2},{1,3},{2,0},{3,1},{4,6},{5,7},{6,4},{7,5},{8,10},{9,11},{10,... | collective-permute-start | bytes 811016 | tf_op jit(solution)/shard_map/ppermute | solution.py:336
  12.6 15.3 %collective-permute-start.3 = (s16[1056,128]{1,0:T(8,128)(2,1)S(1)}, s16[1056,128]{1,0:T(8,128)(2,1)S(1)}, u32[]{:S(2)}, u32[]{:S(2)}) collective-permute-start(s16[1056,128]{1,0:T(8,128)(2,1)S(1)} %shard_map.107._), channel_id=1, source_target_pairs={{0,4},{1,5},{2,6},{3,7},{4,0},{5,1},{6,2},{7,3},{8,12},{9,13},{10,... | collective-permute-start | bytes 811016 | tf_op jit(solution)/shard_map/ppermute | solution.py:336
  15.2 4.2 %copy-start.1 = (bf16[2,1024,512]{2,1,0:T(8,128)(2,1)S(1)}, bf16[2,1024,512]{2,1,0:T(8,128)(2,1)}, u32[]{:S(2)}) copy-start(bf16[2,1024,512]{2,1,0:T(8,128)(2,1)} %prefix_ref.1) | copy-start | bytes 6291460
  15.2 4.2 %copy-start.4 = (bf16[4,8,4096]{2,1,0:T(8,128)(2,1)S(1)}, bf16[4,8,4096]{2,1,0:T(8,128)(2,1)}, u32[]{:S(2)}) copy-start(bf16[4,8,4096]{2,1,0:T(8,128)(2,1)} %query_ref.3) | copy-start | bytes 786436
  15.2 4.2 %copy-start.5 = (bf16[2,4,8,512]{3,2,1,0:T(8,128)(2,1)S(1)}, bf16[2,4,8,512]{3,2,1,0:T(8,128)(2,1)}, u32[]{:S(2)}) copy-start(bf16[2,4,8,512]{3,2,1,0:T(8,128)(2,1)} %fresh_ref.1) | copy-start | bytes 196612
  15.2 12.7 %copy-start.6 = (f32[4096]{0:T(1024)S(1)}, f32[4096]{0:T(1024)}, u32[]{:S(2)}) copy-start(f32[4096]{0:T(1024)} %param.17) | copy-start | bytes 49156
  15.3 12.7 %collective-permute-start.5 = (s16[1056,128]{1,0:T(8,128)(2,1)S(1)}, s16[1056,128]{1,0:T(8,128)(2,1)S(1)}, u32[]{:S(2)}, u32[]{:S(2)}) collective-permute-start(s16[1056,128]{1,0:T(8,128)(2,1)S(1)} %shard_map.108._), channel_id=1, source_target_pairs={{0,1},{1,0},{2,3},{3,2},{4,8},{5,9},{6,10},{7,11},{8,4},{9,5},{10,... | collective-permute-start | bytes 811016 | tf_op jit(solution)/shard_map/ppermute | solution.py:336
  17.2 10.7 %collective-permute-start.7 = (s16[1056,128]{1,0:T(8,128)(2,1)S(1)}, s16[1056,128]{1,0:T(8,128)(2,1)S(1)}, u32[]{:S(2)}, u32[]{:S(2)}) collective-permute-start(s16[1056,128]{1,0:T(8,128)(2,1)S(1)} %shard_map.109), channel_id=1, source_target_pairs={{0,1},{1,0},{2,4},{3,5},{4,2},{5,3},{6,8},{7,9},{8,6},{9,7},{10,12... | collective-permute-start | bytes 811016 | tf_op jit(solution)/shard_map/ppermute | solution.py:336
  30.0 4.0 %collective-permute-start.8 = (f32[4,8]{1,0:T(4,128)S(1)}, f32[4,8]{1,0:T(4,128)S(1)}, u32[]{:S(2)}, u32[]{:S(2)}) collective-permute-start(f32[4,8]{1,0:T(4,128)S(1)} %get-tuple-element.17), channel_id=1, source_target_pairs={{0,1},{1,0},{2,3},{3,2},{4,5},{5,4},{6,7},{7,6},{8,9},{9,8},{10,11... | collective-permute-start | bytes 392 | tf_op jit(solution)/shard_map/ppermute | solution.py:358

commit v6 on v5

--- a/solution.py
+++ b/solution.py
@@ -141,35 +141,21 @@
 def serve_kernel(length, reach, parity, ancestors_ref, query_ref, key_ref, value_ref, _, out_ref):
     count = query_ref.shape[1]
     me = lax.axis_index("particle")
-    found = held_by(ancestors_ref, partner_of(me, reach, parity), me, length, count)
+    asker = partner_of(me, reach, parity) if reach else me
+    found = held_by(ancestors_ref, asker, me, length, count)
     serve([slot for _, slot in found], query_ref, key_ref, value_ref, out_ref)
 
 
-def serve_own_kernel(
-    length,
-    ancestors_ref,
-    query_ref,
-    tail_ref,
-    list_ref,
-    out_ref,
-    key_ref,
-    value_ref,
-    list_out,
-    sems,
-):
+def prepare_kernel(tail_ref, list_ref, key_ref, value_ref, list_out, sems):
     copies = [
         pltpu.make_async_copy(tail_ref.at[1], value_ref, sems.at[0]),
         pltpu.make_async_copy(list_ref, list_out, sems.at[1]),
     ]
     for copy in copies:
         copy.start()
-    count = query_ref.shape[1]
-    me = lax.axis_index("particle")
-    found = held_by(ancestors_ref, me, me, length, count)
-    for j in range(count):
+    for j in range(tail_ref.shape[1]):
         for at in range(0, tail_ref.shape[3], HEAD):
             key_ref[j, at : at + HEAD, :] = tail_ref[0, j, :, at : at + HEAD].T
-    serve([slot for _, slot in found], query_ref, key_ref, tail_ref.at[1], out_ref)
     for copy in copies:
         copy.wait()
 
@@ -311,29 +297,35 @@
     reply = jax.ShapeDtypeStruct((count * rows + 4 * count, HEAD), jnp.int16)
     tail_work = 4 * steps * count * width * tail_cache.shape[2]
     local_work = 4 * steps * count * width * prefix_cache.shape[1]
-    own, keys, values, ancestors = call(
-        functools.partial(serve_own_kernel, length),
+    keys, values, ancestors = call(
+        prepare_kernel,
         [
-            reply,
             jax.ShapeDtypeStruct((count, tail_width, tail_cache.shape[2]), BF16),
             jax.ShapeDtypeStruct(tail_cache.shape[1:], BF16),
             jax.ShapeDtypeStruct(ancestors.shape, ancestors.dtype),
         ],
-        [ancestors, queries, tail_cache, ancestors],
-        tail_work,
+        [tail_cache, ancestors],
+        0,
+        spaces=[VMEM] * 2,
         scratch=(pltpu.SemaphoreType.DMA((2,)),),
     )
-    answer = own
-    answers = [own]
-    for (reach, parity, pairs), question in zip(plans, asked):
+    answer = ancestors
+    answers = []
+
+    def reply_to(reach, parity, question, before):
         (answer,) = call(
             functools.partial(serve_kernel, length, reach, parity),
             [reply],
-            [ancestors, question, keys, values, answer],
+            [ancestors, question, keys, values, before],
             tail_work,
             spaces=[SMEM, VMEM, VMEM, VMEM, pl.ANY],
         )
+        return answer
+
+    for (reach, parity, pairs), question in zip(plans, asked):
+        answer = reply_to(reach, parity, question, answer)
         answers.append(lax.ppermute(answer, both, pairs))
+    answers.insert(0, reply_to(0, 0, queries, answer))
     local, logs = call(
         local_kernel,
         [jax.ShapeDtypeStruct(queries.shape, F32), jax.ShapeDtypeStruct((count, LANES), F32)],

time: 34.8 us -> 33.8 us (0.971)
  the two profiles are of different devices: /device:TPU:11 before, /device:TPU:17 now
where the time goes in v6:
time: 33.8 us; the launch traced here: 33.6 us
  Pallas kernels  12.7 us (38%)
  starting transfers between devices  11.2 us (33%)
  waiting for transfers between devices  6.49 us (19%)
  local copies, waits for them, and re-layouts  1.6 us (5%)
  other arithmetic  0.82 us (2%)
  between operations  0.79 us (2%)
    pallas_call x8, Pallas kernels, call(): pl.pallas_call(kernel, out_shape=tuple(outs), in_specs=[pl.BlockSpec(memo...  12.7 us
    ppermute x4, waiting for transfers between devices, on_device(): answers.append(lax.ppermute(answer, both, pairs))  4.19 us
    ppermute x4, starting transfers between devices, on_device(): answers.append(lax.ppermute(answer, both, pairs))  4.03 us
    ppermute x4, starting transfers between devices, on_device(): asked.append(lax.ppermute(queries, both, pairs))  4.01 us
    ppermute x1, starting transfers between devices, on_device(): lax.ppermute(partial_value, 'tensor', [(0, 1), (1, 0)])  3.17 us
    ppermute x4, waiting for transfers between devices, on_device(): asked.append(lax.ppermute(queries, both, pairs))  1.48 us
    ppermute x1, waiting for transfers between devices, on_device(): lax.ppermute(partial_value, 'tensor', [(0, 1), (1, 0)])  0.82 us
    gather x2, local copies, waits for them, and re-layouts, on_device(): twist_table.at[sampled_ids]  0.78 us
  transfers between devices with their start and end apart: 9, of which 4 were waited for; matrix products, arithmetic and copies ran while one was open for 5% of the time, Pallas kernels for 32%

profile of v6, /device:TPU:17, one launch (start us, length us, event | category | flops | bytes accessed | tf_op | source)
XLA Modules:
  0.0 33.6 jit_solution(12938057246928891870)
XLA Ops:
  0.7 1.3 %collective-permute-start.3 = (bf16[4,8,4096]{2,1,0:T(8,128)(2,1)}, bf16[4,8,4096]{2,1,0:T(8,128)(2,1)}, u32[]{:S(2)}, u32[]{:S(2)}) collective-permute-start(bf16[4,8,4096]{2,1,0:T(8,128)(2,1)} %query_ref.3), channel_id=1, source_target_pairs={{0,2},{1,3},{2,0},{3,1},{4,6},{5,7},{6,4},{7,5},{8,10},{9,11},{10,... | collective-permute-start | bytes 786440 | tf_op jit(solution)/shard_map/ppermute | solution.py:296
  1.9 1.3 %collective-permute-start.2 = (bf16[4,8,4096]{2,1,0:T(8,128)(2,1)}, bf16[4,8,4096]{2,1,0:T(8,128)(2,1)S(1)}, u32[]{:S(2)}, u32[]{:S(2)}) collective-permute-start(bf16[4,8,4096]{2,1,0:T(8,128)(2,1)} %query_ref.3), channel_id=1, source_target_pairs={{0,4},{1,5},{2,6},{3,7},{4,0},{5,1},{6,2},{7,3},{8,12},{9,13},{10,... | collective-permute-start | bytes 786440 | tf_op jit(solution)/shard_map/ppermute | solution.py:296
  3.2 1.4 %collective-permute-start = (bf16[4,8,4096]{2,1,0:T(8,128)(2,1)}, bf16[4,8,4096]{2,1,0:T(8,128)(2,1)S(1)}, u32[]{:S(2)}, u32[]{:S(2)}) collective-permute-start(bf16[4,8,4096]{2,1,0:T(8,128)(2,1)} %query_ref.3), channel_id=1, source_target_pairs={{0,1},{1,0},{2,4},{3,5},{4,2},{5,3},{6,8},{7,9},{8,6},{9,7},{10,12... | collective-permute-start | bytes 786440 | tf_op jit(solution)/shard_map/ppermute | solution.py:296
  4.7 0.8 %reshape.12 = s32[32]{0:T(128)S(1)} reshape(s32[4,8]{1,0:T(4,128)} %param.15) | data formatting | bytes 256 | tf_op jit(solution)/shard_map/broadcast_in_dim | solution.py:339
  5.5 0.7 %gather_fusion = f32[32]{0:T(128)S(1)} fusion(f32[128256]{0:T(1024)S(1)} %copy-done, s32[1024]{0:T(1024)S(1)} %pad_clamp_fusion), kind=kCustom, calls=%fused_computation | custom fusion | bytes 384 | tf_op jit(solution)/shard_map/gather | solution.py:339
  6.2 0.1 reshape.11
  6.3 0.4 %shard_map.104 = (bf16[8,512,128]{2,1,0:T(8,128)(2,1)S(1)}, bf16[8,128,512]{2,1,0:T(8,128)(2,1)S(1)}, s32[64]{0:T(128)S(1)}) custom-call(bf16[2,8,128,512]{3,2,1,0:T(8,128)(2,1)S(1)} %copy-done.1, s32[64]{0:T(128)S(1)} %copy-done.6), custom_call_target="tpu_custom_call" | custom-call | bytes 4194816 | tf_op jit(solution)/shard_map/pallas_call | solution.py:264
  6.7 0.2 convert_reduce_fusion
  6.9 1.3 %collective-permute-done.3.query_ref = bf16[4,8,4096]{2,1,0:T(8,128)(2,1)} collective-permute-done((bf16[4,8,4096]{2,1,0:T(8,128)(2,1)}, bf16[4,8,4096]{2,1,0:T(8,128)(2,1)}, u32[]{:S(2)}, u32[]{:S(2)}) %collective-permute-start.3) | collective-permute-done | bytes 262176 | tf_op jit(solution)/shard_map/ppermute | solution.py:296
  8.2 1.8 %shard_map.106._ = s16[1056,128]{1,0:T(8,128)(2,1)S(1)} custom-call(s32[64]{0:T(128)S(1)} %get-tuple-element.9.ancestors_ref._, bf16[4,8,4096]{2,1,0:T(8,128)(2,1)} %collective-permute-done.3.query_ref, bf16[8,512,128]{2,1,0:T(8,128)(2,1)S(1)} %get-tuple-element.12.key_ref, bf16[8,128,512]{2,1,0:T(8,128)(2,1)S(1)} %get-tuple-element.13.value_ref, ...), custom_call_target="tpu_custom_call" | custom-call | flops 67108864 | bytes 2630144 | tf_op jit(solution)/shard_map/pallas_call | solution.py:264
  10.0 1.3 %collective-permute-start.4 = (s16[1056,128]{1,0:T(8,128)(2,1)S(1)}, s16[1056,128]{1,0:T(8,128)(2,1)S(1)}, u32[]{:S(2)}, u32[]{:S(2)}) collective-permute-start(s16[1056,128]{1,0:T(8,128)(2,1)S(1)} %shard_map.106._), channel_id=1, source_target_pairs={{0,2},{1,3},{2,0},{3,1},{4,6},{5,7},{6,4},{7,5},{8,10},{9,11},{10,... | collective-permute-start | bytes 811016 | tf_op jit(solution)/shard_map/ppermute | solution.py:327
  11.3 1.4 %shard_map.107._ = s16[1056,128]{1,0:T(8,128)(2,1)S(1)} custom-call(s32[64]{0:T(128)S(1)} %get-tuple-element.9.ancestors_ref._, bf16[4,8,4096]{2,1,0:T(8,128)(2,1)S(1)} %collective-permute-done.2.query_ref, bf16[8,512,128]{2,1,0:T(8,128)(2,1)S(1)} %get-tuple-element.12.key_ref, bf16[8,128,512]{2,1,0:T(8,128)(2,1)S(1)} %get-tuple-element.13.value_ref, ...), custom_call_target="tpu_custom_call" | custom-call | flops 67108864 | bytes 2900224 | tf_op jit(solution)/shard_map/pallas_call | solution.py:264
  12.7 1.4 %collective-permute-start.5 = (s16[1056,128]{1,0:T(8,128)(2,1)S(1)}, s16[1056,128]{1,0:T(8,128)(2,1)S(1)}, u32[]{:S(2)}, u32[]{:S(2)}) collective-permute-start(s16[1056,128]{1,0:T(8,128)(2,1)S(1)} %shard_map.107._), channel_id=1, source_target_pairs={{0,4},{1,5},{2,6},{3,7},{4,0},{5,1},{6,2},{7,3},{8,12},{9,13},{10,... | collective-permute-start | bytes 811016 | tf_op jit(solution)/shard_map/ppermute | solution.py:327
  14.0 1.4 %shard_map.108._ = s16[1056,128]{1,0:T(8,128)(2,1)S(1)} custom-call(s32[64]{0:T(128)S(1)} %get-tuple-element.9.ancestors_ref._, bf16[4,8,4096]{2,1,0:T(8,128)(2,1)S(1)} %collective-permute-done.1.query_ref, bf16[8,512,128]{2,1,0:T(8,128)(2,1)S(1)} %get-tuple-element.12.key_ref, bf16[8,128,512]{2,1,0:T(8,128)(2,1)S(1)} %get-tuple-element.13.value_ref, ...), custom_call_target="tpu_custom_call" | custom-call | flops 67108864 | bytes 2900224 | tf_op jit(solution)/shard_map/pallas_call | solution.py:264
  15.5 0.2 collective-permute-done.query_ref
  15.7 1.4 %shard_map.109._ = s16[1056,128]{1,0:T(8,128)(2,1)S(1)} custom-call(s32[64]{0:T(128)S(1)} %get-tuple-element.9.ancestors_ref._, bf16[4,8,4096]{2,1,0:T(8,128)(2,1)S(1)} %collective-permute-done.query_ref, bf16[8,512,128]{2,1,0:T(8,128)(2,1)S(1)} %get-tuple-element.12.key_ref, bf16[8,128,512]{2,1,0:T(8,128)(2,1)S(1)} %get-tuple-element.13.value_ref, ...), custom_call_target="tpu_custom_call" | custom-call | flops 67108864 | bytes 2900224 | tf_op jit(solution)/shard_map/pallas_call | solution.py:264
  17.1 1.3 %collective-permute-start.7 = (s16[1056,128]{1,0:T(8,128)(2,1)S(1)}, s16[1056,128]{1,0:T(8,128)(2,1)S(1)}, u32[]{:S(2)}, u32[]{:S(2)}) collective-permute-start(s16[1056,128]{1,0:T(8,128)(2,1)S(1)} %shard_map.109._), channel_id=1, source_target_pairs={{0,1},{1,0},{2,4},{3,5},{4,2},{5,3},{6,8},{7,9},{8,6},{9,7},{10,12... | collective-permute-start | bytes 811016 | tf_op jit(solution)/shard_map/ppermute | solution.py:327
  18.4 3.0 %shard_map.105 = (f32[4,8,4096]{2,1,0:T(8,128)S(1)}, f32[8,128]{1,0:T(8,128)S(1)}) custom-call(bf16[4,8,4096]{2,1,0:T(8,128)(2,1)S(1)} %copy-done.3, bf16[2,1024,512]{2,1,0:T(8,128)(2,1)S(1)} %copy-done.2, bf16[2,4,8,512]{3,2,1,0:T(8,128)(2,1)S(1)} %copy-done.4), custom_call_target="tpu_custom_call" | custom-call | flops 536870912 | bytes 2953216 | tf_op jit(solution)/shard_map/pallas_call | solution.py:264
  21.5 1.4 %shard_map.110.refs_0_ = s16[1056,128]{1,0:T(8,128)(2,1)S(1)} custom-call(s32[64]{0:T(128)S(1)} %get-tuple-element.9.ancestors_ref._, bf16[4,8,4096]{2,1,0:T(8,128)(2,1)S(1)} %copy-done.3, bf16[8,512,128]{2,1,0:T(8,128)(2,1)S(1)} %get-tuple-element.12.key_ref, bf16[8,128,512]{2,1,0:T(8,128)(2,1)S(1)} %get-tuple-element.13.value_ref, ...), custom_call_target="tpu_custom_call" | custom-call | flops 67108864 | bytes 2900224 | tf_op jit(solution)/shard_map/pallas_call | solution.py:264
  22.8 4.2 %collective-permute-done.7.refs_4_ = s16[1056,128]{1,0:T(8,128)(2,1)S(1)} collective-permute-done((s16[1056,128]{1,0:T(8,128)(2,1)S(1)}, s16[1056,128]{1,0:T(8,128)(2,1)S(1)}, u32[]{:S(2)}, u32[]{:S(2)}) %collective-permute-start.7) | collective-permute-done | bytes 270368 | tf_op jit(solution)/shard_map/ppermute | solution.py:327
  27.0 2.0 %shard_map.111 = (bf16[4,8,4096]{2,1,0:T(8,128)(2,1)}, f32[4,8]{1,0:T(4,128)S(1)}) custom-call(s32[64]{0:T(128)S(1)} %get-tuple-element.9.ancestors_ref._, f32[4,8,4096]{2,1,0:T(8,128)S(1)} %get-tuple-element.10.local_ref, f32[8,128]{1,0:T(8,128)S(1)} %get-tuple-element.11.log_ref, f32[1,4096]{1,0:T(1,128)S(1)} %bitcast.1, ...), custom_call_target="tpu_custom_call" | custom-call | flops 2097152 | bytes 2159104 | tf_op jit(solution)/shard_map/pallas_call | solution.py:264
  29.0 3.2 %collective-permute-start.8 = (f32[4,8]{1,0:T(4,128)S(1)}, f32[4,8]{1,0:T(4,128)S(1)}, u32[]{:S(2)}, u32[]{:S(2)}) collective-permute-start(f32[4,8]{1,0:T(4,128)S(1)} %get-tuple-element.15), channel_id=1, source_target_pairs={{0,1},{1,0},{2,3},{3,2},{4,5},{5,4},{6,7},{7,6},{8,9},{9,8},{10,11... | collective-permute-start | bytes 392 | tf_op jit(solution)/shard_map/ppermute | solution.py:350
  32.2 0.8 %collective-permute-done.8 = f32[4,8]{1,0:T(4,128)S(1)} collective-permute-done((f32[4,8]{1,0:T(4,128)S(1)}, f32[4,8]{1,0:T(4,128)S(1)}, u32[]{:S(2)}, u32[]{:S(2)}) %collective-permute-start.8) | collective-permute-done | bytes 160 | tf_op jit(solution)/shard_map/ppermute | solution.py:350
  33.0 0.6 %add.3 = f32[4,8]{1,0:T(4,128)} add(f32[4,8]{1,0:T(4,128)S(1)} %get-tuple-element.15, f32[4,8]{1,0:T(4,128)S(1)} %collective-permute-done.8) | non-fusion elementwise | flops 32 | bytes 384 | tf_op jit(solution)/shard_map/add | solution.py:350
  (27 shorter events, 0.2 us)
Async XLA Ops:
  0.6 4.8 %copy-start = (f32[128256]{0:T(1024)S(1)}, f32[128256]{0:T(1024)}, u32[]{:S(2)}) copy-start(f32[128256]{0:T(1024)} %param.16) | copy-start | bytes 1539076
  0.6 5.6 %copy-start.1 = (bf16[2,8,128,512]{3,2,1,0:T(8,128)(2,1)S(1)}, bf16[2,8,128,512]{3,2,1,0:T(8,128)(2,1)}, u32[]{:S(2)}) copy-start(bf16[2,8,128,512]{3,2,1,0:T(8,128)(2,1)} %tail_ref.1) | copy-start | bytes 6291460
  0.7 5.6 %copy-start.6 = (s32[64]{0:T(128)S(1)}, s32[64]{0:T(128)}, u32[]{:S(2)}) copy-start(s32[64]{0:T(128)} %list_ref.1) | copy-start | bytes 772
  0.7 7.6 %collective-permute-start.3 = (bf16[4,8,4096]{2,1,0:T(8,128)(2,1)}, bf16[4,8,4096]{2,1,0:T(8,128)(2,1)}, u32[]{:S(2)}, u32[]{:S(2)}) collective-permute-start(bf16[4,8,4096]{2,1,0:T(8,128)(2,1)} %query_ref.3), channel_id=1, source_target_pairs={{0,2},{1,3},{2,0},{3,1},{4,6},{5,7},{6,4},{7,5},{8,10},{9,11},{10,... | collective-permute-start | bytes 786440 | tf_op jit(solution)/shard_map/ppermute | solution.py:296
  1.9 9.4 %collective-permute-start.2 = (bf16[4,8,4096]{2,1,0:T(8,128)(2,1)}, bf16[4,8,4096]{2,1,0:T(8,128)(2,1)S(1)}, u32[]{:S(2)}, u32[]{:S(2)}) collective-permute-start(bf16[4,8,4096]{2,1,0:T(8,128)(2,1)} %query_ref.3), channel_id=1, source_target_pairs={{0,4},{1,5},{2,6},{3,7},{4,0},{5,1},{6,2},{7,3},{8,12},{9,13},{10,... | collective-permute-start | bytes 786440 | tf_op jit(solution)/shard_map/ppermute | solution.py:296
  3.2 10.8 %collective-permute-start.1 = (bf16[4,8,4096]{2,1,0:T(8,128)(2,1)}, bf16[4,8,4096]{2,1,0:T(8,128)(2,1)S(1)}, u32[]{:S(2)}, u32[]{:S(2)}) collective-permute-start(bf16[4,8,4096]{2,1,0:T(8,128)(2,1)} %query_ref.3), channel_id=1, source_target_pairs={{0,1},{1,0},{2,3},{3,2},{4,8},{5,9},{6,10},{7,11},{8,4},{9,5},{10,... | collective-permute-start | bytes 786440 | tf_op jit(solution)/shard_map/ppermute | solution.py:296
  3.2 12.5 %collective-permute-start = (bf16[4,8,4096]{2,1,0:T(8,128)(2,1)}, bf16[4,8,4096]{2,1,0:T(8,128)(2,1)S(1)}, u32[]{:S(2)}, u32[]{:S(2)}) collective-permute-start(bf16[4,8,4096]{2,1,0:T(8,128)(2,1)} %query_ref.3), channel_id=1, source_target_pairs={{0,1},{1,0},{2,4},{3,5},{4,2},{5,3},{6,8},{7,9},{8,6},{9,7},{10,12... | collective-permute-start | bytes 786440 | tf_op jit(solution)/shard_map/ppermute | solution.py:296
  5.5 1.2 %copy-start.7 = (s32[4,8]{1,0:T(4,128)S(1)}, s32[4,8]{1,0:T(4,128)}, u32[]{:S(2)}) copy-start(s32[4,8]{1,0:T(4,128)} %param.15) | copy-start | bytes 388
  5.5 1.2 %copy-start.8 = (s32[1024]{0:T(1024)S(1)}, s32[1024]{0:T(1024)}, u32[]{:S(2)}) copy-start(s32[1024]{0:T(1024)} %param.14) | copy-start | bytes 12292
  10.0 17.0 %collective-permute-start.4 = (s16[1056,128]{1,0:T(8,128)(2,1)S(1)}, s16[1056,128]{1,0:T(8,128)(2,1)S(1)}, u32[]{:S(2)}, u32[]{:S(2)}) collective-permute-start(s16[1056,128]{1,0:T(8,128)(2,1)S(1)} %shard_map.106._), channel_id=1, source_target_pairs={{0,2},{1,3},{2,0},{3,1},{4,6},{5,7},{6,4},{7,5},{8,10},{9,11},{10,... | collective-permute-start | bytes 811016 | tf_op jit(solution)/shard_map/ppermute | solution.py:327
  12.7 14.3 %collective-permute-start.5 = (s16[1056,128]{1,0:T(8,128)(2,1)S(1)}, s16[1056,128]{1,0:T(8,128)(2,1)S(1)}, u32[]{:S(2)}, u32[]{:S(2)}) collective-permute-start(s16[1056,128]{1,0:T(8,128)(2,1)S(1)} %shard_map.107._), channel_id=1, source_target_pairs={{0,4},{1,5},{2,6},{3,7},{4,0},{5,1},{6,2},{7,3},{8,12},{9,13},{10,... | collective-permute-start | bytes 811016 | tf_op jit(solution)/shard_map/ppermute | solution.py:327
  15.4 3.0 %copy-start.2 = (bf16[2,1024,512]{2,1,0:T(8,128)(2,1)S(1)}, bf16[2,1024,512]{2,1,0:T(8,128)(2,1)}, u32[]{:S(2)}) copy-start(bf16[2,1024,512]{2,1,0:T(8,128)(2,1)} %prefix_ref.1) | copy-start | bytes 6291460
  15.4 3.0 %copy-start.3 = (bf16[4,8,4096]{2,1,0:T(8,128)(2,1)S(1)}, bf16[4,8,4096]{2,1,0:T(8,128)(2,1)}, u32[]{:S(2)}) copy-start(bf16[4,8,4096]{2,1,0:T(8,128)(2,1)} %query_ref.3) | copy-start | bytes 786436
  15.4 3.0 %copy-start.4 = (bf16[2,4,8,512]{3,2,1,0:T(8,128)(2,1)S(1)}, bf16[2,4,8,512]{3,2,1,0:T(8,128)(2,1)}, u32[]{:S(2)}) copy-start(bf16[2,4,8,512]{3,2,1,0:T(8,128)(2,1)} %fresh_ref.1) | copy-start | bytes 196612
  15.5 11.6 %collective-permute-start.6 = (s16[1056,128]{1,0:T(8,128)(2,1)S(1)}, s16[1056,128]{1,0:T(8,128)(2,1)S(1)}, u32[]{:S(2)}, u32[]{:S(2)}) collective-permute-start(s16[1056,128]{1,0:T(8,128)(2,1)S(1)} %shard_map.108._), channel_id=1, source_target_pairs={{0,1},{1,0},{2,3},{3,2},{4,8},{5,9},{6,10},{7,11},{8,4},{9,5},{10,... | collective-permute-start | bytes 811016 | tf_op jit(solution)/shard_map/ppermute | solution.py:327
  17.1 9.9 %copy-start.5 = (f32[4096]{0:T(1024)S(1)}, f32[4096]{0:T(1024)}, u32[]{:S(2)}) copy-start(f32[4096]{0:T(1024)} %param.17) | copy-start | bytes 49156
  17.1 9.9 %collective-permute-start.7 = (s16[1056,128]{1,0:T(8,128)(2,1)S(1)}, s16[1056,128]{1,0:T(8,128)(2,1)S(1)}, u32[]{:S(2)}, u32[]{:S(2)}) collective-permute-start(s16[1056,128]{1,0:T(8,128)(2,1)S(1)} %shard_map.109._), channel_id=1, source_target_pairs={{0,1},{1,0},{2,4},{3,5},{4,2},{5,3},{6,8},{7,9},{8,6},{9,7},{10,12... | collective-permute-start | bytes 811016 | tf_op jit(solution)/shard_map/ppermute | solution.py:327
  29.0 4.0 %collective-permute-start.8 = (f32[4,8]{1,0:T(4,128)S(1)}, f32[4,8]{1,0:T(4,128)S(1)}, u32[]{:S(2)}, u32[]{:S(2)}) collective-permute-start(f32[4,8]{1,0:T(4,128)S(1)} %get-tuple-element.15), channel_id=1, source_target_pairs={{0,1},{1,0},{2,3},{3,2},{4,5},{5,4},{6,7},{7,6},{8,9},{9,8},{10,11... | collective-permute-start | bytes 392 | tf_op jit(solution)/shard_map/ppermute | solution.py:350

commit v7 on v6

--- a/solution.py
+++ b/solution.py
@@ -104,6 +104,26 @@
             for p in range(count)
         ]
     terms = [softmax_terms(score) for score in scores]
+
+    def note(which, p, k, column):
+        for t in range(steps):
+            here = lane == row + (k * many + t * GROUP)
+            part = column[t * GROUP : (t + 1) * GROUP]
+            notes[which][p] = jnp.where(here, part, notes[which][p])
+
+    def gather_notes(which):
+        return jnp.concatenate([jnp.sum(n, axis=0, keepdims=True) for n in notes[which]], axis=0)
+
+    for k in range(heads):
+        for p in range(count):
+            top, _, total = terms[k * count + p]
+            note(0, p, k, top)
+            note(1, p, k, total)
+    top, total = gather_notes(0), gather_notes(1)
+    if each < LANES:
+        total = jnp.maximum(total, TINY)
+    spread = jnp.log2(total)
+    level = two_codes(top * EXPONENT_SCALE + spread)
     outs = [
         jnp.dot(
             terms[k * count + p][1].astype(BF16),
@@ -115,24 +135,15 @@
     ]
     for k in range(heads):
         for p in range(count):
-            top, _, total = terms[k * count + p]
             out = outs[k * count + p]
             largest = jnp.maximum(jnp.max(jnp.abs(out), axis=-1, keepdims=True), TINY)
             code = jnp.round(out * (TOP_CODE / largest)).astype(jnp.int32)
             at = p * each + k * many
             out_ref[at : at + many, :] = code.astype(jnp.int16)
-            for t in range(steps):
-                here = lane == row + (k * many + t * GROUP)
-                part = slice(t * GROUP, (t + 1) * GROUP)
-                for note, column in zip(notes, (top, total, largest)):
-                    note[p] = jnp.where(here, column[part], note[p])
-    top, total, largest = (
-        jnp.concatenate([jnp.sum(n, axis=0, keepdims=True) for n in note], axis=0) for note in notes
-    )
+            note(2, p, k, largest)
+    largest = gather_notes(2)
     if each < LANES:
-        total, largest = jnp.maximum(total, TINY), jnp.maximum(largest, TINY)
-    spread = jnp.log2(total)
-    level = two_codes(top * EXPONENT_SCALE + spread)
+        largest = jnp.maximum(largest, TINY)
     scale = two_codes(jnp.log2(largest) - spread - math.log2(TOP_CODE))
     coded = jnp.concatenate(level + scale, axis=0).astype(jnp.int32)
     out_ref[count * each :, :] = coded.astype(jnp.int16)
@@ -200,17 +211,20 @@
     log_ref[...] = functools.reduce(jnp.add, logs)
 
 
-def combine_kernel(length, plans, ancestors_ref, local_ref, log_ref, readout_ref, base_ref, *refs):
+def combine_kernel(plans, ancestors_ref, local_ref, log_ref, readout_ref, base_ref, *refs):
     sent_refs, (out_ref, twist_ref) = refs[: len(plans) + 1], refs[len(plans) + 1 :]
     steps, count = local_ref.shape[0], local_ref.shape[1]
     heads = local_ref.shape[2] // (HEAD * GROUP)
     many = steps * GROUP
     each = heads * many
     me = lax.axis_index("particle")
-    source = [jnp.int32(0)] * count
-    for m, (reach, parity) in enumerate(plans):
-        found = held_by(ancestors_ref, me, partner_of(me, reach, parity), length, count)
-        source = [jnp.where(here, m + 1, old) for (here, _), old in zip(found, source)]
+    source = []
+    for p in range(count):
+        parent = lax.div(ancestors_ref[me * count + p], count)
+        found = jnp.int32(0)
+        for m, (reach, parity) in enumerate(plans):
+            found = jnp.where(parent == partner_of(me, reach, parity), m + 1, found)
+        source.append(found)
     row = lax.broadcasted_iota(jnp.int32, (count, LANES), 0)
     lane = lax.broadcasted_iota(jnp.int32, (count, LANES), 1)
 
@@ -341,7 +355,7 @@
     )
     base = (looked_up - 2.0 * repeats.astype(F32)) * (1.0 / cores)
     attended, partial_value = call(
-        functools.partial(combine_kernel, length, [plan[:2] for plan in plans]),
+        functools.partial(combine_kernel, [plan[:2] for plan in plans]),
         [jax.ShapeDtypeStruct(queries.shape, BF16), jax.ShapeDtypeStruct((steps, count), F32)],
         [ancestors, local, logs, readout.reshape(1, width), base] + answers,
         16 * steps * count * width,

time: 33.8 us -> 33.7 us (level)
  no operation moved by 1% of the time
where the time goes in v7:
time: 33.7 us; the launch traced here: 33.5 us
  Pallas kernels  12.6 us (37%)
  starting transfers between devices  11.2 us (33%)
  waiting for transfers between devices  6.49 us (19%)
  local copies, waits for them, and re-layouts  1.6 us (5%)
  other arithmetic  0.82 us (2%)
  between operations  0.79 us (2%)
    pallas_call x8, Pallas kernels, call(): pl.pallas_call(kernel, out_shape=tuple(outs), in_specs=[pl.BlockSpec(memo...  12.6 us
    ppermute x4, waiting for transfers between devices, on_device(): answers.append(lax.ppermute(answer, both, pairs))  4.19 us
    ppermute x4, starting transfers between devices, on_device(): answers.append(lax.ppermute(answer, both, pairs))  4.03 us
    ppermute x4, starting transfers between devices, on_device(): asked.append(lax.ppermute(queries, both, pairs))  4.01 us
    ppermute x1, starting transfers between devices, on_device(): lax.ppermute(partial_value, 'tensor', [(0, 1), (1, 0)])  3.17 us
    ppermute x4, waiting for transfers between devices, on_device(): asked.append(lax.ppermute(queries, both, pairs))  1.48 us
    ppermute x1, waiting for transfers between devices, on_device(): lax.ppermute(partial_value, 'tensor', [(0, 1), (1, 0)])  0.82 us
    gather x2, local copies, waits for them, and re-layouts, on_device(): twist_table.at[sampled_ids]  0.78 us
  transfers between devices with their start and end apart: 9, of which 4 were waited for; matrix products, arithmetic and copies ran while one was open for 5% of the time, Pallas kernels for 32%

profile of v7, /device:TPU:17, one launch (start us, length us, event | category | flops | bytes accessed | tf_op | source)
XLA Modules:
  0.0 33.5 jit_solution(7862985247137416379)
XLA Ops:
  0.7 1.3 %collective-permute-start.3 = (bf16[4,8,4096]{2,1,0:T(8,128)(2,1)}, bf16[4,8,4096]{2,1,0:T(8,128)(2,1)}, u32[]{:S(2)}, u32[]{:S(2)}) collective-permute-start(bf16[4,8,4096]{2,1,0:T(8,128)(2,1)} %query_ref.3), channel_id=1, source_target_pairs={{0,2},{1,3},{2,0},{3,1},{4,6},{5,7},{6,4},{7,5},{8,10},{9,11},{10,... | collective-permute-start | bytes 786440 | tf_op jit(solution)/shard_map/ppermute | solution.py:310
  1.9 1.3 %collective-permute-start.2 = (bf16[4,8,4096]{2,1,0:T(8,128)(2,1)}, bf16[4,8,4096]{2,1,0:T(8,128)(2,1)S(1)}, u32[]{:S(2)}, u32[]{:S(2)}) collective-permute-start(bf16[4,8,4096]{2,1,0:T(8,128)(2,1)} %query_ref.3), channel_id=1, source_target_pairs={{0,4},{1,5},{2,6},{3,7},{4,0},{5,1},{6,2},{7,3},{8,12},{9,13},{10,... | collective-permute-start | bytes 786440 | tf_op jit(solution)/shard_map/ppermute | solution.py:310
  3.2 1.4 %collective-permute-start = (bf16[4,8,4096]{2,1,0:T(8,128)(2,1)}, bf16[4,8,4096]{2,1,0:T(8,128)(2,1)S(1)}, u32[]{:S(2)}, u32[]{:S(2)}) collective-permute-start(bf16[4,8,4096]{2,1,0:T(8,128)(2,1)} %query_ref.3), channel_id=1, source_target_pairs={{0,1},{1,0},{2,4},{3,5},{4,2},{5,3},{6,8},{7,9},{8,6},{9,7},{10,12... | collective-permute-start | bytes 786440 | tf_op jit(solution)/shard_map/ppermute | solution.py:310
  4.7 0.8 %reshape.12 = s32[32]{0:T(128)S(1)} reshape(s32[4,8]{1,0:T(4,128)} %param.15) | data formatting | bytes 256 | tf_op jit(solution)/shard_map/broadcast_in_dim | solution.py:353
  5.5 0.7 %gather_fusion = f32[32]{0:T(128)S(1)} fusion(f32[128256]{0:T(1024)S(1)} %copy-done, s32[1024]{0:T(1024)S(1)} %pad_clamp_fusion), kind=kCustom, calls=%fused_computation | custom fusion | bytes 384 | tf_op jit(solution)/shard_map/gather | solution.py:353
  6.2 0.1 reshape.11
  6.3 0.4 %shard_map.104 = (bf16[8,512,128]{2,1,0:T(8,128)(2,1)S(1)}, bf16[8,128,512]{2,1,0:T(8,128)(2,1)S(1)}, s32[64]{0:T(128)S(1)}) custom-call(bf16[2,8,128,512]{3,2,1,0:T(8,128)(2,1)S(1)} %copy-done.1, s32[64]{0:T(128)S(1)} %copy-done.6), custom_call_target="tpu_custom_call" | custom-call | bytes 4194816 | tf_op jit(solution)/shard_map/pallas_call | solution.py:278
  6.7 0.2 convert_reduce_fusion
  6.9 1.3 %collective-permute-done.3.query_ref = bf16[4,8,4096]{2,1,0:T(8,128)(2,1)} collective-permute-done((bf16[4,8,4096]{2,1,0:T(8,128)(2,1)}, bf16[4,8,4096]{2,1,0:T(8,128)(2,1)}, u32[]{:S(2)}, u32[]{:S(2)}) %collective-permute-start.3) | collective-permute-done | bytes 262176 | tf_op jit(solution)/shard_map/ppermute | solution.py:310
  8.2 1.8 %shard_map.106._ = s16[1056,128]{1,0:T(8,128)(2,1)S(1)} custom-call(s32[64]{0:T(128)S(1)} %get-tuple-element.9.ancestors_ref._, bf16[4,8,4096]{2,1,0:T(8,128)(2,1)} %collective-permute-done.3.query_ref, bf16[8,512,128]{2,1,0:T(8,128)(2,1)S(1)} %get-tuple-element.12.key_ref, bf16[8,128,512]{2,1,0:T(8,128)(2,1)S(1)} %get-tuple-element.13.value_ref, ...), custom_call_target="tpu_custom_call" | custom-call | flops 67108864 | bytes 2630144 | tf_op jit(solution)/shard_map/pallas_call | solution.py:278
  10.0 1.3 %collective-permute-start.4 = (s16[1056,128]{1,0:T(8,128)(2,1)S(1)}, s16[1056,128]{1,0:T(8,128)(2,1)S(1)}, u32[]{:S(2)}, u32[]{:S(2)}) collective-permute-start(s16[1056,128]{1,0:T(8,128)(2,1)S(1)} %shard_map.106._), channel_id=1, source_target_pairs={{0,2},{1,3},{2,0},{3,1},{4,6},{5,7},{6,4},{7,5},{8,10},{9,11},{10,... | collective-permute-start | bytes 811016 | tf_op jit(solution)/shard_map/ppermute | solution.py:341
  11.3 1.4 %shard_map.107._ = s16[1056,128]{1,0:T(8,128)(2,1)S(1)} custom-call(s32[64]{0:T(128)S(1)} %get-tuple-element.9.ancestors_ref._, bf16[4,8,4096]{2,1,0:T(8,128)(2,1)S(1)} %collective-permute-done.2.query_ref, bf16[8,512,128]{2,1,0:T(8,128)(2,1)S(1)} %get-tuple-element.12.key_ref, bf16[8,128,512]{2,1,0:T(8,128)(2,1)S(1)} %get-tuple-element.13.value_ref, ...), custom_call_target="tpu_custom_call" | custom-call | flops 67108864 | bytes 2900224 | tf_op jit(solution)/shard_map/pallas_call | solution.py:278
  12.7 1.4 %collective-permute-start.5 = (s16[1056,128]{1,0:T(8,128)(2,1)S(1)}, s16[1056,128]{1,0:T(8,128)(2,1)S(1)}, u32[]{:S(2)}, u32[]{:S(2)}) collective-permute-start(s16[1056,128]{1,0:T(8,128)(2,1)S(1)} %shard_map.107._), channel_id=1, source_target_pairs={{0,4},{1,5},{2,6},{3,7},{4,0},{5,1},{6,2},{7,3},{8,12},{9,13},{10,... | collective-permute-start | bytes 811016 | tf_op jit(solution)/shard_map/ppermute | solution.py:341
  14.0 1.4 %shard_map.108._ = s16[1056,128]{1,0:T(8,128)(2,1)S(1)} custom-call(s32[64]{0:T(128)S(1)} %get-tuple-element.9.ancestors_ref._, bf16[4,8,4096]{2,1,0:T(8,128)(2,1)S(1)} %collective-permute-done.1.query_ref, bf16[8,512,128]{2,1,0:T(8,128)(2,1)S(1)} %get-tuple-element.12.key_ref, bf16[8,128,512]{2,1,0:T(8,128)(2,1)S(1)} %get-tuple-element.13.value_ref, ...), custom_call_target="tpu_custom_call" | custom-call | flops 67108864 | bytes 2900224 | tf_op jit(solution)/shard_map/pallas_call | solution.py:278
  15.5 0.2 collective-permute-done.query_ref
  15.7 1.4 %shard_map.109._ = s16[1056,128]{1,0:T(8,128)(2,1)S(1)} custom-call(s32[64]{0:T(128)S(1)} %get-tuple-element.9.ancestors_ref._, bf16[4,8,4096]{2,1,0:T(8,128)(2,1)S(1)} %collective-permute-done.query_ref, bf16[8,512,128]{2,1,0:T(8,128)(2,1)S(1)} %get-tuple-element.12.key_ref, bf16[8,128,512]{2,1,0:T(8,128)(2,1)S(1)} %get-tuple-element.13.value_ref, ...), custom_call_target="tpu_custom_call" | custom-call | flops 67108864 | bytes 2900224 | tf_op jit(solution)/shard_map/pallas_call | solution.py:278
  17.1 1.3 %collective-permute-start.7 = (s16[1056,128]{1,0:T(8,128)(2,1)S(1)}, s16[1056,128]{1,0:T(8,128)(2,1)S(1)}, u32[]{:S(2)}, u32[]{:S(2)}) collective-permute-start(s16[1056,128]{1,0:T(8,128)(2,1)S(1)} %shard_map.109._), channel_id=1, source_target_pairs={{0,1},{1,0},{2,4},{3,5},{4,2},{5,3},{6,8},{7,9},{8,6},{9,7},{10,12... | collective-permute-start | bytes 811016 | tf_op jit(solution)/shard_map/ppermute | solution.py:341
  18.4 3.0 %shard_map.105 = (f32[4,8,4096]{2,1,0:T(8,128)S(1)}, f32[8,128]{1,0:T(8,128)S(1)}) custom-call(bf16[4,8,4096]{2,1,0:T(8,128)(2,1)S(1)} %copy-done.3, bf16[2,1024,512]{2,1,0:T(8,128)(2,1)S(1)} %copy-done.2, bf16[2,4,8,512]{3,2,1,0:T(8,128)(2,1)S(1)} %copy-done.4), custom_call_target="tpu_custom_call" | custom-call | flops 536870912 | bytes 2953216 | tf_op jit(solution)/shard_map/pallas_call | solution.py:278
  21.5 1.4 %shard_map.110.refs_0_ = s16[1056,128]{1,0:T(8,128)(2,1)S(1)} custom-call(s32[64]{0:T(128)S(1)} %get-tuple-element.9.ancestors_ref._, bf16[4,8,4096]{2,1,0:T(8,128)(2,1)S(1)} %copy-done.3, bf16[8,512,128]{2,1,0:T(8,128)(2,1)S(1)} %get-tuple-element.12.key_ref, bf16[8,128,512]{2,1,0:T(8,128)(2,1)S(1)} %get-tuple-element.13.value_ref, ...), custom_call_target="tpu_custom_call" | custom-call | flops 67108864 | bytes 2900224 | tf_op jit(solution)/shard_map/pallas_call | solution.py:278
  22.8 4.2 %collective-permute-done.7.refs_4_ = s16[1056,128]{1,0:T(8,128)(2,1)S(1)} collective-permute-done((s16[1056,128]{1,0:T(8,128)(2,1)S(1)}, s16[1056,128]{1,0:T(8,128)(2,1)S(1)}, u32[]{:S(2)}, u32[]{:S(2)}) %collective-permute-start.7) | collective-permute-done | bytes 270368 | tf_op jit(solution)/shard_map/ppermute | solution.py:341
  27.0 1.9 %shard_map.111 = (bf16[4,8,4096]{2,1,0:T(8,128)(2,1)}, f32[4,8]{1,0:T(4,128)S(1)}) custom-call(s32[64]{0:T(128)S(1)} %get-tuple-element.9.ancestors_ref._, f32[4,8,4096]{2,1,0:T(8,128)S(1)} %get-tuple-element.10.local_ref, f32[8,128]{1,0:T(8,128)S(1)} %get-tuple-element.11.log_ref, f32[1,4096]{1,0:T(1,128)S(1)} %bitcast.1, ...), custom_call_target="tpu_custom_call" | custom-call | flops 2097152 | bytes 2159104 | tf_op jit(solution)/shard_map/pallas_call | solution.py:278
  29.0 3.2 %collective-permute-start.8 = (f32[4,8]{1,0:T(4,128)S(1)}, f32[4,8]{1,0:T(4,128)S(1)}, u32[]{:S(2)}, u32[]{:S(2)}) collective-permute-start(f32[4,8]{1,0:T(4,128)S(1)} %get-tuple-element.15), channel_id=1, source_target_pairs={{0,1},{1,0},{2,3},{3,2},{4,5},{5,4},{6,7},{7,6},{8,9},{9,8},{10,11... | collective-permute-start | bytes 392 | tf_op jit(solution)/shard_map/ppermute | solution.py:364
  32.1 0.8 %collective-permute-done.8 = f32[4,8]{1,0:T(4,128)S(1)} collective-permute-done((f32[4,8]{1,0:T(4,128)S(1)}, f32[4,8]{1,0:T(4,128)S(1)}, u32[]{:S(2)}, u32[]{:S(2)}) %collective-permute-start.8) | collective-permute-done | bytes 160 | tf_op jit(solution)/shard_map/ppermute | solution.py:364
  33.0 0.6 %add.3 = f32[4,8]{1,0:T(4,128)} add(f32[4,8]{1,0:T(4,128)S(1)} %get-tuple-element.15, f32[4,8]{1,0:T(4,128)S(1)} %collective-permute-done.8) | non-fusion elementwise | flops 32 | bytes 384 | tf_op jit(solution)/shard_map/add | solution.py:364
  (27 shorter events, 0.2 us)
Async XLA Ops:
  0.6 4.8 %copy-start = (f32[128256]{0:T(1024)S(1)}, f32[128256]{0:T(1024)}, u32[]{:S(2)}) copy-start(f32[128256]{0:T(1024)} %param.16) | copy-start | bytes 1539076
  0.6 5.6 %copy-start.1 = (bf16[2,8,128,512]{3,2,1,0:T(8,128)(2,1)S(1)}, bf16[2,8,128,512]{3,2,1,0:T(8,128)(2,1)}, u32[]{:S(2)}) copy-start(bf16[2,8,128,512]{3,2,1,0:T(8,128)(2,1)} %tail_ref.1) | copy-start | bytes 6291460
  0.7 5.6 %copy-start.6 = (s32[64]{0:T(128)S(1)}, s32[64]{0:T(128)}, u32[]{:S(2)}) copy-start(s32[64]{0:T(128)} %list_ref.1) | copy-start | bytes 772
  0.7 7.6 %collective-permute-start.3 = (bf16[4,8,4096]{2,1,0:T(8,128)(2,1)}, bf16[4,8,4096]{2,1,0:T(8,128)(2,1)}, u32[]{:S(2)}, u32[]{:S(2)}) collective-permute-start(bf16[4,8,4096]{2,1,0:T(8,128)(2,1)} %query_ref.3), channel_id=1, source_target_pairs={{0,2},{1,3},{2,0},{3,1},{4,6},{5,7},{6,4},{7,5},{8,10},{9,11},{10,... | collective-permute-start | bytes 786440 | tf_op jit(solution)/shard_map/ppermute | solution.py:310
  1.9 9.4 %collective-permute-start.2 = (bf16[4,8,4096]{2,1,0:T(8,128)(2,1)}, bf16[4,8,4096]{2,1,0:T(8,128)(2,1)S(1)}, u32[]{:S(2)}, u32[]{:S(2)}) collective-permute-start(bf16[4,8,4096]{2,1,0:T(8,128)(2,1)} %query_ref.3), channel_id=1, source_target_pairs={{0,4},{1,5},{2,6},{3,7},{4,0},{5,1},{6,2},{7,3},{8,12},{9,13},{10,... | collective-permute-start | bytes 786440 | tf_op jit(solution)/shard_map/ppermute | solution.py:310
  3.2 10.8 %collective-permute-start.1 = (bf16[4,8,4096]{2,1,0:T(8,128)(2,1)}, bf16[4,8,4096]{2,1,0:T(8,128)(2,1)S(1)}, u32[]{:S(2)}, u32[]{:S(2)}) collective-permute-start(bf16[4,8,4096]{2,1,0:T(8,128)(2,1)} %query_ref.3), channel_id=1, source_target_pairs={{0,1},{1,0},{2,3},{3,2},{4,8},{5,9},{6,10},{7,11},{8,4},{9,5},{10,... | collective-permute-start | bytes 786440 | tf_op jit(solution)/shard_map/ppermute | solution.py:310
  3.2 12.5 %collective-permute-start = (bf16[4,8,4096]{2,1,0:T(8,128)(2,1)}, bf16[4,8,4096]{2,1,0:T(8,128)(2,1)S(1)}, u32[]{:S(2)}, u32[]{:S(2)}) collective-permute-start(bf16[4,8,4096]{2,1,0:T(8,128)(2,1)} %query_ref.3), channel_id=1, source_target_pairs={{0,1},{1,0},{2,4},{3,5},{4,2},{5,3},{6,8},{7,9},{8,6},{9,7},{10,12... | collective-permute-start | bytes 786440 | tf_op jit(solution)/shard_map/ppermute | solution.py:310
  5.5 1.2 %copy-start.7 = (s32[4,8]{1,0:T(4,128)S(1)}, s32[4,8]{1,0:T(4,128)}, u32[]{:S(2)}) copy-start(s32[4,8]{1,0:T(4,128)} %param.15) | copy-start | bytes 388
  5.5 1.2 %copy-start.8 = (s32[1024]{0:T(1024)S(1)}, s32[1024]{0:T(1024)}, u32[]{:S(2)}) copy-start(s32[1024]{0:T(1024)} %param.14) | copy-start | bytes 12292
  10.0 17.0 %collective-permute-start.4 = (s16[1056,128]{1,0:T(8,128)(2,1)S(1)}, s16[1056,128]{1,0:T(8,128)(2,1)S(1)}, u32[]{:S(2)}, u32[]{:S(2)}) collective-permute-start(s16[1056,128]{1,0:T(8,128)(2,1)S(1)} %shard_map.106._), channel_id=1, source_target_pairs={{0,2},{1,3},{2,0},{3,1},{4,6},{5,7},{6,4},{7,5},{8,10},{9,11},{10,... | collective-permute-start | bytes 811016 | tf_op jit(solution)/shard_map/ppermute | solution.py:341
  12.7 14.3 %collective-permute-start.5 = (s16[1056,128]{1,0:T(8,128)(2,1)S(1)}, s16[1056,128]{1,0:T(8,128)(2,1)S(1)}, u32[]{:S(2)}, u32[]{:S(2)}) collective-permute-start(s16[1056,128]{1,0:T(8,128)(2,1)S(1)} %shard_map.107._), channel_id=1, source_target_pairs={{0,4},{1,5},{2,6},{3,7},{4,0},{5,1},{6,2},{7,3},{8,12},{9,13},{10,... | collective-permute-start | bytes 811016 | tf_op jit(solution)/shard_map/ppermute | solution.py:341
  15.4 3.0 %copy-start.2 = (bf16[2,1024,512]{2,1,0:T(8,128)(2,1)S(1)}, bf16[2,1024,512]{2,1,0:T(8,128)(2,1)}, u32[]{:S(2)}) copy-start(bf16[2,1024,512]{2,1,0:T(8,128)(2,1)} %prefix_ref.1) | copy-start | bytes 6291460
  15.4 3.0 %copy-start.3 = (bf16[4,8,4096]{2,1,0:T(8,128)(2,1)S(1)}, bf16[4,8,4096]{2,1,0:T(8,128)(2,1)}, u32[]{:S(2)}) copy-start(bf16[4,8,4096]{2,1,0:T(8,128)(2,1)} %query_ref.3) | copy-start | bytes 786436
  15.4 3.0 %copy-start.4 = (bf16[2,4,8,512]{3,2,1,0:T(8,128)(2,1)S(1)}, bf16[2,4,8,512]{3,2,1,0:T(8,128)(2,1)}, u32[]{:S(2)}) copy-start(bf16[2,4,8,512]{3,2,1,0:T(8,128)(2,1)} %fresh_ref.1) | copy-start | bytes 196612
  15.5 11.6 %collective-permute-start.6 = (s16[1056,128]{1,0:T(8,128)(2,1)S(1)}, s16[1056,128]{1,0:T(8,128)(2,1)S(1)}, u32[]{:S(2)}, u32[]{:S(2)}) collective-permute-start(s16[1056,128]{1,0:T(8,128)(2,1)S(1)} %shard_map.108._), channel_id=1, source_target_pairs={{0,1},{1,0},{2,3},{3,2},{4,8},{5,9},{6,10},{7,11},{8,4},{9,5},{10,... | collective-permute-start | bytes 811016 | tf_op jit(solution)/shard_map/ppermute | solution.py:341
  17.1 9.9 %copy-start.5 = (f32[4096]{0:T(1024)S(1)}, f32[4096]{0:T(1024)}, u32[]{:S(2)}) copy-start(f32[4096]{0:T(1024)} %param.17) | copy-start | bytes 49156
  17.1 9.9 %collective-permute-start.7 = (s16[1056,128]{1,0:T(8,128)(2,1)S(1)}, s16[1056,128]{1,0:T(8,128)(2,1)S(1)}, u32[]{:S(2)}, u32[]{:S(2)}) collective-permute-start(s16[1056,128]{1,0:T(8,128)(2,1)S(1)} %shard_map.109._), channel_id=1, source_target_pairs={{0,1},{1,0},{2,4},{3,5},{4,2},{5,3},{6,8},{7,9},{8,6},{9,7},{10,12... | collective-permute-start | bytes 811016 | tf_op jit(solution)/shard_map/ppermute | solution.py:341
  29.0 4.0 %collective-permute-start.8 = (f32[4,8]{1,0:T(4,128)S(1)}, f32[4,8]{1,0:T(4,128)S(1)}, u32[]{:S(2)}, u32[]{:S(2)}) collective-permute-start(f32[4,8]{1,0:T(4,128)S(1)} %get-tuple-element.15), channel_id=1, source_target_pairs={{0,1},{1,0},{2,3},{3,2},{4,5},{5,4},{6,7},{7,6},{8,9},{9,8},{10,11... | collective-permute-start | bytes 392 | tf_op jit(solution)/shard_map/ppermute | solution.py:364

commit v8 on v7

--- a/solution.py
+++ b/solution.py
@@ -12,7 +12,8 @@
 HEADS = 64
 KV_HEADS = 8
 HEAD = 128
-EXCHANGES = ((1, 0), (2, 0), (2, 1), (1, 1))
+EXCHANGES = ((1, 0), (2, 1), (2, 0), (1, 1))
+SERVED = (0, 2, 1, 3)
 GROUP = HEADS // KV_HEADS
 EXPONENT_SCALE = math.log2(math.e) / math.sqrt(HEAD)
 
@@ -336,10 +337,12 @@
         )
         return answer
 
-    for (reach, parity, pairs), question in zip(plans, asked):
-        answer = reply_to(reach, parity, question, answer)
-        answers.append(lax.ppermute(answer, both, pairs))
-    answers.insert(0, reply_to(0, 0, queries, answer))
+    answers = [None] * (len(plans) + 1)
+    for i in SERVED:
+        reach, parity, pairs = plans[i]
+        answer = reply_to(reach, parity, asked[i], answer)
+        answers[i + 1] = lax.ppermute(answer, both, pairs)
+    answers[0] = reply_to(0, 0, queries, answer)
     local, logs = call(
         local_kernel,
         [jax.ShapeDtypeStruct(queries.shape, F32), jax.ShapeDtypeStruct((count, LANES), F32)],

time: 33.7 us -> 33.7 us (level)
  no operation moved by 1% of the time
where the time goes in v8:
time: 33.7 us; the launch traced here: 33.5 us
  Pallas kernels  12.6 us (37%)
  starting transfers between devices  11.2 us (33%)
  waiting for transfers between devices  6.49 us (19%)
  local copies, waits for them, and re-layouts  1.6 us (5%)
  other arithmetic  0.82 us (2%)
  between operations  0.79 us (2%)
    pallas_call x8, Pallas kernels, call(): pl.pallas_call(kernel, out_shape=tuple(outs), in_specs=[pl.BlockSpec(memo...  12.6 us
    ppermute x4, waiting for transfers between devices, on_device(): answers[i + 1] = lax.ppermute(answer, both, pairs)  4.19 us
    ppermute x4, starting transfers between devices, on_device(): answers[i + 1] = lax.ppermute(answer, both, pairs)  4.03 us
    ppermute x4, starting transfers between devices, on_device(): asked.append(lax.ppermute(queries, both, pairs))  4.01 us
    ppermute x1, starting transfers between devices, on_device(): lax.ppermute(partial_value, 'tensor', [(0, 1), (1, 0)])  3.17 us
    ppermute x4, waiting for transfers between devices, on_device(): asked.append(lax.ppermute(queries, both, pairs))  1.48 us
    ppermute x1, waiting for transfers between devices, on_device(): lax.ppermute(partial_value, 'tensor', [(0, 1), (1, 0)])  0.82 us
    gather x2, local copies, waits for them, and re-layouts, on_device(): twist_table.at[sampled_ids]  0.78 us
  transfers between devices with their start and end apart: 9, of which 4 were waited for; matrix products, arithmetic and copies ran while one was open for 5% of the time, Pallas kernels for 32%

profile of v8, /device:TPU:17, one launch (start us, length us, event | category | flops | bytes accessed | tf_op | source)
XLA Modules:
  0.0 33.5 jit_solution(3516696308956632721)
XLA Ops:
  0.7 1.3 %collective-permute-start.3 = (bf16[4,8,4096]{2,1,0:T(8,128)(2,1)}, bf16[4,8,4096]{2,1,0:T(8,128)(2,1)}, u32[]{:S(2)}, u32[]{:S(2)}) collective-permute-start(bf16[4,8,4096]{2,1,0:T(8,128)(2,1)} %query_ref.3), channel_id=1, source_target_pairs={{0,2},{1,3},{2,0},{3,1},{4,6},{5,7},{6,4},{7,5},{8,10},{9,11},{10,... | collective-permute-start | bytes 786440 | tf_op jit(solution)/shard_map/ppermute | solution.py:311
  1.9 1.3 %collective-permute-start.2 = (bf16[4,8,4096]{2,1,0:T(8,128)(2,1)}, bf16[4,8,4096]{2,1,0:T(8,128)(2,1)S(1)}, u32[]{:S(2)}, u32[]{:S(2)}) collective-permute-start(bf16[4,8,4096]{2,1,0:T(8,128)(2,1)} %query_ref.3), channel_id=1, source_target_pairs={{0,4},{1,5},{2,6},{3,7},{4,0},{5,1},{6,2},{7,3},{8,12},{9,13},{10,... | collective-permute-start | bytes 786440 | tf_op jit(solution)/shard_map/ppermute | solution.py:311
  3.2 1.4 %collective-permute-start = (bf16[4,8,4096]{2,1,0:T(8,128)(2,1)}, bf16[4,8,4096]{2,1,0:T(8,128)(2,1)S(1)}, u32[]{:S(2)}, u32[]{:S(2)}) collective-permute-start(bf16[4,8,4096]{2,1,0:T(8,128)(2,1)} %query_ref.3), channel_id=1, source_target_pairs={{0,1},{1,0},{2,4},{3,5},{4,2},{5,3},{6,8},{7,9},{8,6},{9,7},{10,12... | collective-permute-start | bytes 786440 | tf_op jit(solution)/shard_map/ppermute | solution.py:311
  4.7 0.8 %reshape.12 = s32[32]{0:T(128)S(1)} reshape(s32[4,8]{1,0:T(4,128)} %param.15) | data formatting | bytes 256 | tf_op jit(solution)/shard_map/broadcast_in_dim | solution.py:356
  5.5 0.7 %gather_fusion = f32[32]{0:T(128)S(1)} fusion(f32[128256]{0:T(1024)S(1)} %copy-done, s32[1024]{0:T(1024)S(1)} %pad_clamp_fusion), kind=kCustom, calls=%fused_computation | custom fusion | bytes 384 | tf_op jit(solution)/shard_map/gather | solution.py:356
  6.2 0.1 reshape.11
  6.3 0.4 %shard_map.104 = (bf16[8,512,128]{2,1,0:T(8,128)(2,1)S(1)}, bf16[8,128,512]{2,1,0:T(8,128)(2,1)S(1)}, s32[64]{0:T(128)S(1)}) custom-call(bf16[2,8,128,512]{3,2,1,0:T(8,128)(2,1)S(1)} %copy-done.1, s32[64]{0:T(128)S(1)} %copy-done.6), custom_call_target="tpu_custom_call" | custom-call | bytes 4194816 | tf_op jit(solution)/shard_map/pallas_call | solution.py:279
  6.7 0.2 convert_reduce_fusion
  6.9 1.3 %collective-permute-done.3.query_ref = bf16[4,8,4096]{2,1,0:T(8,128)(2,1)} collective-permute-done((bf16[4,8,4096]{2,1,0:T(8,128)(2,1)}, bf16[4,8,4096]{2,1,0:T(8,128)(2,1)}, u32[]{:S(2)}, u32[]{:S(2)}) %collective-permute-start.3) | collective-permute-done | bytes 262176 | tf_op jit(solution)/shard_map/ppermute | solution.py:311
  8.2 1.8 %shard_map.106._ = s16[1056,128]{1,0:T(8,128)(2,1)S(1)} custom-call(s32[64]{0:T(128)S(1)} %get-tuple-element.9.ancestors_ref._, bf16[4,8,4096]{2,1,0:T(8,128)(2,1)} %collective-permute-done.3.query_ref, bf16[8,512,128]{2,1,0:T(8,128)(2,1)S(1)} %get-tuple-element.12.key_ref, bf16[8,128,512]{2,1,0:T(8,128)(2,1)S(1)} %get-tuple-element.13.value_ref, ...), custom_call_target="tpu_custom_call" | custom-call | flops 67108864 | bytes 2630144 | tf_op jit(solution)/shard_map/pallas_call | solution.py:279
  10.0 1.3 %collective-permute-start.4 = (s16[1056,128]{1,0:T(8,128)(2,1)S(1)}, s16[1056,128]{1,0:T(8,128)(2,1)S(1)}, u32[]{:S(2)}, u32[]{:S(2)}) collective-permute-start(s16[1056,128]{1,0:T(8,128)(2,1)S(1)} %shard_map.106._), channel_id=1, source_target_pairs={{0,2},{1,3},{2,0},{3,1},{4,6},{5,7},{6,4},{7,5},{8,10},{9,11},{10,... | collective-permute-start | bytes 811016 | tf_op jit(solution)/shard_map/ppermute | solution.py:344
  11.3 1.4 %shard_map.107._ = s16[1056,128]{1,0:T(8,128)(2,1)S(1)} custom-call(s32[64]{0:T(128)S(1)} %get-tuple-element.9.ancestors_ref._, bf16[4,8,4096]{2,1,0:T(8,128)(2,1)S(1)} %collective-permute-done.2.query_ref, bf16[8,512,128]{2,1,0:T(8,128)(2,1)S(1)} %get-tuple-element.12.key_ref, bf16[8,128,512]{2,1,0:T(8,128)(2,1)S(1)} %get-tuple-element.13.value_ref, ...), custom_call_target="tpu_custom_call" | custom-call | flops 67108864 | bytes 2900224 | tf_op jit(solution)/shard_map/pallas_call | solution.py:279
  12.7 1.4 %collective-permute-start.6 = (s16[1056,128]{1,0:T(8,128)(2,1)S(1)}, s16[1056,128]{1,0:T(8,128)(2,1)S(1)}, u32[]{:S(2)}, u32[]{:S(2)}) collective-permute-start(s16[1056,128]{1,0:T(8,128)(2,1)S(1)} %shard_map.107._), channel_id=1, source_target_pairs={{0,4},{1,5},{2,6},{3,7},{4,0},{5,1},{6,2},{7,3},{8,12},{9,13},{10,... | collective-permute-start | bytes 811016 | tf_op jit(solution)/shard_map/ppermute | solution.py:344
  14.0 1.4 %shard_map.108._ = s16[1056,128]{1,0:T(8,128)(2,1)S(1)} custom-call(s32[64]{0:T(128)S(1)} %get-tuple-element.9.ancestors_ref._, bf16[4,8,4096]{2,1,0:T(8,128)(2,1)S(1)} %collective-permute-done.1.query_ref, bf16[8,512,128]{2,1,0:T(8,128)(2,1)S(1)} %get-tuple-element.12.key_ref, bf16[8,128,512]{2,1,0:T(8,128)(2,1)S(1)} %get-tuple-element.13.value_ref, ...), custom_call_target="tpu_custom_call" | custom-call | flops 67108864 | bytes 2900224 | tf_op jit(solution)/shard_map/pallas_call | solution.py:279
  15.5 0.2 collective-permute-done.query_ref
  15.7 1.4 %shard_map.109._ = s16[1056,128]{1,0:T(8,128)(2,1)S(1)} custom-call(s32[64]{0:T(128)S(1)} %get-tuple-element.9.ancestors_ref._, bf16[4,8,4096]{2,1,0:T(8,128)(2,1)S(1)} %collective-permute-done.query_ref, bf16[8,512,128]{2,1,0:T(8,128)(2,1)S(1)} %get-tuple-element.12.key_ref, bf16[8,128,512]{2,1,0:T(8,128)(2,1)S(1)} %get-tuple-element.13.value_ref, ...), custom_call_target="tpu_custom_call" | custom-call | flops 67108864 | bytes 2900224 | tf_op jit(solution)/shard_map/pallas_call | solution.py:279
  17.1 1.3 %collective-permute-start.7 = (s16[1056,128]{1,0:T(8,128)(2,1)S(1)}, s16[1056,128]{1,0:T(8,128)(2,1)S(1)}, u32[]{:S(2)}, u32[]{:S(2)}) collective-permute-start(s16[1056,128]{1,0:T(8,128)(2,1)S(1)} %shard_map.109._), channel_id=1, source_target_pairs={{0,1},{1,0},{2,4},{3,5},{4,2},{5,3},{6,8},{7,9},{8,6},{9,7},{10,12... | collective-permute-start | bytes 811016 | tf_op jit(solution)/shard_map/ppermute | solution.py:344
  18.4 3.0 %shard_map.105 = (f32[4,8,4096]{2,1,0:T(8,128)S(1)}, f32[8,128]{1,0:T(8,128)S(1)}) custom-call(bf16[4,8,4096]{2,1,0:T(8,128)(2,1)S(1)} %copy-done.3, bf16[2,1024,512]{2,1,0:T(8,128)(2,1)S(1)} %copy-done.2, bf16[2,4,8,512]{3,2,1,0:T(8,128)(2,1)S(1)} %copy-done.4), custom_call_target="tpu_custom_call" | custom-call | flops 536870912 | bytes 2953216 | tf_op jit(solution)/shard_map/pallas_call | solution.py:279
  21.5 1.4 %shard_map.110.refs_0_ = s16[1056,128]{1,0:T(8,128)(2,1)S(1)} custom-call(s32[64]{0:T(128)S(1)} %get-tuple-element.9.ancestors_ref._, bf16[4,8,4096]{2,1,0:T(8,128)(2,1)S(1)} %copy-done.3, bf16[8,512,128]{2,1,0:T(8,128)(2,1)S(1)} %get-tuple-element.12.key_ref, bf16[8,128,512]{2,1,0:T(8,128)(2,1)S(1)} %get-tuple-element.13.value_ref, ...), custom_call_target="tpu_custom_call" | custom-call | flops 67108864 | bytes 2900224 | tf_op jit(solution)/shard_map/pallas_call | solution.py:279
  22.8 4.2 %collective-permute-done.7.refs_4_ = s16[1056,128]{1,0:T(8,128)(2,1)S(1)} collective-permute-done((s16[1056,128]{1,0:T(8,128)(2,1)S(1)}, s16[1056,128]{1,0:T(8,128)(2,1)S(1)}, u32[]{:S(2)}, u32[]{:S(2)}) %collective-permute-start.7) | collective-permute-done | bytes 270368 | tf_op jit(solution)/shard_map/ppermute | solution.py:344
  27.0 1.9 %shard_map.111 = (bf16[4,8,4096]{2,1,0:T(8,128)(2,1)}, f32[4,8]{1,0:T(4,128)S(1)}) custom-call(s32[64]{0:T(128)S(1)} %get-tuple-element.9.ancestors_ref._, f32[4,8,4096]{2,1,0:T(8,128)S(1)} %get-tuple-element.10.local_ref, f32[8,128]{1,0:T(8,128)S(1)} %get-tuple-element.11.log_ref, f32[1,4096]{1,0:T(1,128)S(1)} %bitcast.1, ...), custom_call_target="tpu_custom_call" | custom-call | flops 2097152 | bytes 2159104 | tf_op jit(solution)/shard_map/pallas_call | solution.py:279
  29.0 3.2 %collective-permute-start.8 = (f32[4,8]{1,0:T(4,128)S(1)}, f32[4,8]{1,0:T(4,128)S(1)}, u32[]{:S(2)}, u32[]{:S(2)}) collective-permute-start(f32[4,8]{1,0:T(4,128)S(1)} %get-tuple-element.15), channel_id=1, source_target_pairs={{0,1},{1,0},{2,3},{3,2},{4,5},{5,4},{6,7},{7,6},{8,9},{9,8},{10,11... | collective-permute-start | bytes 392 | tf_op jit(solution)/shard_map/ppermute | solution.py:367
  32.1 0.8 %collective-permute-done.8 = f32[4,8]{1,0:T(4,128)S(1)} collective-permute-done((f32[4,8]{1,0:T(4,128)S(1)}, f32[4,8]{1,0:T(4,128)S(1)}, u32[]{:S(2)}, u32[]{:S(2)}) %collective-permute-start.8) | collective-permute-done | bytes 160 | tf_op jit(solution)/shard_map/ppermute | solution.py:367
  33.0 0.6 %add.3 = f32[4,8]{1,0:T(4,128)} add(f32[4,8]{1,0:T(4,128)S(1)} %get-tuple-element.15, f32[4,8]{1,0:T(4,128)S(1)} %collective-permute-done.8) | non-fusion elementwise | flops 32 | bytes 384 | tf_op jit(solution)/shard_map/add | solution.py:367
  (27 shorter events, 0.2 us)
Async XLA Ops:
  0.6 4.8 %copy-start = (f32[128256]{0:T(1024)S(1)}, f32[128256]{0:T(1024)}, u32[]{:S(2)}) copy-start(f32[128256]{0:T(1024)} %param.16) | copy-start | bytes 1539076
  0.6 5.6 %copy-start.1 = (bf16[2,8,128,512]{3,2,1,0:T(8,128)(2,1)S(1)}, bf16[2,8,128,512]{3,2,1,0:T(8,128)(2,1)}, u32[]{:S(2)}) copy-start(bf16[2,8,128,512]{3,2,1,0:T(8,128)(2,1)} %tail_ref.1) | copy-start | bytes 6291460
  0.7 5.6 %copy-start.6 = (s32[64]{0:T(128)S(1)}, s32[64]{0:T(128)}, u32[]{:S(2)}) copy-start(s32[64]{0:T(128)} %list_ref.1) | copy-start | bytes 772
  0.7 7.6 %collective-permute-start.3 = (bf16[4,8,4096]{2,1,0:T(8,128)(2,1)}, bf16[4,8,4096]{2,1,0:T(8,128)(2,1)}, u32[]{:S(2)}, u32[]{:S(2)}) collective-permute-start(bf16[4,8,4096]{2,1,0:T(8,128)(2,1)} %query_ref.3), channel_id=1, source_target_pairs={{0,2},{1,3},{2,0},{3,1},{4,6},{5,7},{6,4},{7,5},{8,10},{9,11},{10,... | collective-permute-start | bytes 786440 | tf_op jit(solution)/shard_map/ppermute | solution.py:311
  1.9 9.4 %collective-permute-start.2 = (bf16[4,8,4096]{2,1,0:T(8,128)(2,1)}, bf16[4,8,4096]{2,1,0:T(8,128)(2,1)S(1)}, u32[]{:S(2)}, u32[]{:S(2)}) collective-permute-start(bf16[4,8,4096]{2,1,0:T(8,128)(2,1)} %query_ref.3), channel_id=1, source_target_pairs={{0,4},{1,5},{2,6},{3,7},{4,0},{5,1},{6,2},{7,3},{8,12},{9,13},{10,... | collective-permute-start | bytes 786440 | tf_op jit(solution)/shard_map/ppermute | solution.py:311
  3.2 10.8 %collective-permute-start.1 = (bf16[4,8,4096]{2,1,0:T(8,128)(2,1)}, bf16[4,8,4096]{2,1,0:T(8,128)(2,1)S(1)}, u32[]{:S(2)}, u32[]{:S(2)}) collective-permute-start(bf16[4,8,4096]{2,1,0:T(8,128)(2,1)} %query_ref.3), channel_id=1, source_target_pairs={{0,1},{1,0},{2,3},{3,2},{4,8},{5,9},{6,10},{7,11},{8,4},{9,5},{10,... | collective-permute-start | bytes 786440 | tf_op jit(solution)/shard_map/ppermute | solution.py:311
  3.2 12.5 %collective-permute-start = (bf16[4,8,4096]{2,1,0:T(8,128)(2,1)}, bf16[4,8,4096]{2,1,0:T(8,128)(2,1)S(1)}, u32[]{:S(2)}, u32[]{:S(2)}) collective-permute-start(bf16[4,8,4096]{2,1,0:T(8,128)(2,1)} %query_ref.3), channel_id=1, source_target_pairs={{0,1},{1,0},{2,4},{3,5},{4,2},{5,3},{6,8},{7,9},{8,6},{9,7},{10,12... | collective-permute-start | bytes 786440 | tf_op jit(solution)/shard_map/ppermute | solution.py:311
  5.5 1.2 %copy-start.7 = (s32[4,8]{1,0:T(4,128)S(1)}, s32[4,8]{1,0:T(4,128)}, u32[]{:S(2)}) copy-start(s32[4,8]{1,0:T(4,128)} %param.15) | copy-start | bytes 388
  5.5 1.2 %copy-start.8 = (s32[1024]{0:T(1024)S(1)}, s32[1024]{0:T(1024)}, u32[]{:S(2)}) copy-start(s32[1024]{0:T(1024)} %param.14) | copy-start | bytes 12292
  10.0 17.0 %collective-permute-start.4 = (s16[1056,128]{1,0:T(8,128)(2,1)S(1)}, s16[1056,128]{1,0:T(8,128)(2,1)S(1)}, u32[]{:S(2)}, u32[]{:S(2)}) collective-permute-start(s16[1056,128]{1,0:T(8,128)(2,1)S(1)} %shard_map.106._), channel_id=1, source_target_pairs={{0,2},{1,3},{2,0},{3,1},{4,6},{5,7},{6,4},{7,5},{8,10},{9,11},{10,... | collective-permute-start | bytes 811016 | tf_op jit(solution)/shard_map/ppermute | solution.py:344
  12.7 14.3 %collective-permute-start.6 = (s16[1056,128]{1,0:T(8,128)(2,1)S(1)}, s16[1056,128]{1,0:T(8,128)(2,1)S(1)}, u32[]{:S(2)}, u32[]{:S(2)}) collective-permute-start(s16[1056,128]{1,0:T(8,128)(2,1)S(1)} %shard_map.107._), channel_id=1, source_target_pairs={{0,4},{1,5},{2,6},{3,7},{4,0},{5,1},{6,2},{7,3},{8,12},{9,13},{10,... | collective-permute-start | bytes 811016 | tf_op jit(solution)/shard_map/ppermute | solution.py:344
  15.4 3.0 %copy-start.2 = (bf16[2,1024,512]{2,1,0:T(8,128)(2,1)S(1)}, bf16[2,1024,512]{2,1,0:T(8,128)(2,1)}, u32[]{:S(2)}) copy-start(bf16[2,1024,512]{2,1,0:T(8,128)(2,1)} %prefix_ref.1) | copy-start | bytes 6291460
  15.4 3.0 %copy-start.3 = (bf16[4,8,4096]{2,1,0:T(8,128)(2,1)S(1)}, bf16[4,8,4096]{2,1,0:T(8,128)(2,1)}, u32[]{:S(2)}) copy-start(bf16[4,8,4096]{2,1,0:T(8,128)(2,1)} %query_ref.3) | copy-start | bytes 786436
  15.4 3.0 %copy-start.4 = (bf16[2,4,8,512]{3,2,1,0:T(8,128)(2,1)S(1)}, bf16[2,4,8,512]{3,2,1,0:T(8,128)(2,1)}, u32[]{:S(2)}) copy-start(bf16[2,4,8,512]{3,2,1,0:T(8,128)(2,1)} %fresh_ref.1) | copy-start | bytes 196612
  15.5 11.6 %collective-permute-start.5 = (s16[1056,128]{1,0:T(8,128)(2,1)S(1)}, s16[1056,128]{1,0:T(8,128)(2,1)S(1)}, u32[]{:S(2)}, u32[]{:S(2)}) collective-permute-start(s16[1056,128]{1,0:T(8,128)(2,1)S(1)} %shard_map.108._), channel_id=1, source_target_pairs={{0,1},{1,0},{2,3},{3,2},{4,8},{5,9},{6,10},{7,11},{8,4},{9,5},{10,... | collective-permute-start | bytes 811016 | tf_op jit(solution)/shard_map/ppermute | solution.py:344
  17.1 9.9 %copy-start.5 = (f32[4096]{0:T(1024)S(1)}, f32[4096]{0:T(1024)}, u32[]{:S(2)}) copy-start(f32[4096]{0:T(1024)} %param.17) | copy-start | bytes 49156
  17.1 9.9 %collective-permute-start.7 = (s16[1056,128]{1,0:T(8,128)(2,1)S(1)}, s16[1056,128]{1,0:T(8,128)(2,1)S(1)}, u32[]{:S(2)}, u32[]{:S(2)}) collective-permute-start(s16[1056,128]{1,0:T(8,128)(2,1)S(1)} %shard_map.109._), channel_id=1, source_target_pairs={{0,1},{1,0},{2,4},{3,5},{4,2},{5,3},{6,8},{7,9},{8,6},{9,7},{10,12... | collective-permute-start | bytes 811016 | tf_op jit(solution)/shard_map/ppermute | solution.py:344
  29.0 4.0 %collective-permute-start.8 = (f32[4,8]{1,0:T(4,128)S(1)}, f32[4,8]{1,0:T(4,128)S(1)}, u32[]{:S(2)}, u32[]{:S(2)}) collective-permute-start(f32[4,8]{1,0:T(4,128)S(1)} %get-tuple-element.15), channel_id=1, source_target_pairs={{0,1},{1,0},{2,3},{3,2},{4,5},{5,4},{6,7},{7,6},{8,9},{9,8},{10,11... | collective-permute-start | bytes 392 | tf_op jit(solution)/shard_map/ppermute | solution.py:367
